TPU v7x, 32 devices: a whole 2x2x4 slice. The times are simulated.
32 devices in a mesh: section: 4 (over y, core), batch: 8 (over z, x).
Axes of the slice: x: 2, y: 2, z: 4, core: 2. Of those that a mesh axis runs over, the one named last changes fastest.
Arguments:
- masters: float32 [32, 512, 1024], P('section', 'batch'), may hold values from -0.1875 to 0.1875
- first_moment: float32 [32, 512, 1024], P('section', 'batch')
- second_moment: float32 [32, 512, 1024], P('section', 'batch')
- section_table: float32 [8, 6144], P('section'), may hold values from -1.2 to 1.2
- table_first: float32 [8, 6144], P('section')
- table_second: float32 [8, 6144], P('section')
- owners: int32 [29], replicated, may hold values from 0 to 31, as said below
- step_count: int32 [1], replicated, may hold values from 2 to 20
- phones: int32 [64, 512], P(('section', 'batch')), may hold values from 0 to 511
- codes: int32 [64, 512, 8], P(('section', 'batch')), may hold values from 0 to 1023
- segments: int32 [64, 512], P(('section', 'batch')), may hold values from 0 to 2, never falling along the last dimension, each value on 1 to 384 neighbouring positions
- sections: int32 [64, 1], P(('section', 'batch')), may hold values from 0 to 7
- targets: int32 [64, 512], P(('section', 'batch')), may hold values from 0 to 1023
Outputs:
- new_masters: float32 [32, 512, 1024], P('section', 'batch')
- new_first: float32 [32, 512, 1024], P('section', 'batch')
- new_second: float32 [32, 512, 1024], P('section', 'batch')
- new_table: float32 [8, 6144], P('section')
- new_table_first: float32 [8, 6144], P('section')
- new_table_second: float32 [8, 6144], P('section')
- grad_norm: float32 [], replicated
- loss: float32 [], replicated
Inputs may be any that keep to these rules, and one draw needn't show every extreme that they name: `owners`: distinct slot numbers; slot 0 and slot 31 are always among them; a section index of the slots owns a varying number of blocks. `sections`: every section is the section of some row; rows of one section may stand on any device.
All inputs are finite; a program needn't handle non-finite values.
Results may differ from a plain program's by a relative error of at most 0.0067.
Values may be sent and summed in bfloat16 or wider, within the bound.
A program may use at most 320 MiB of HBM per device.

v0:
```python
import math

import jax
import jax.numpy as jnp
from jax import lax
from jax.sharding import PartitionSpec as P

D = 1024
HEADS = 16
HD = 64
FF = 4096
CODES = 1024
LEVELS = 8
PHONES = 512
SECTIONS = 8


clip_limit = 0.002
learn_rate = 0.02
table_rate = 0.1
beta_one = 0.9
beta_two = 0.95
adam_eps = 1e-08
decay_rate = 0.1
norm_eps = 1e-05
pos_scale = 0.1
exact = lax.Precision.HIGHEST
float_out = jnp.float32


def positions(segs):
    index = jnp.broadcast_to(jnp.arange(segs.shape[-1], dtype=jnp.int32), segs.shape)
    first = jnp.ones(segs.shape[:-1] + (1,), dtype=bool)
    change = jnp.concatenate([first, segs[..., 1:] != segs[..., :-1]], axis=-1)
    starts = lax.cummax(jnp.where(change, index, jnp.zeros_like(index)), axis=segs.ndim - 1)
    return (index - starts).astype(jnp.float32)


def sinusoid(place, width):
    column = jnp.arange(width)
    rate = jnp.exp(-(2 * (column // 2)).astype(jnp.float32) * (math.log(10000.0) / width))
    angle = place[..., None] * rate
    return pos_scale * jnp.where(column % 2 == 0, jnp.sin(angle), jnp.cos(angle))


def normalize(stream):
    centred = stream - jnp.mean(stream, axis=-1, keepdims=True)
    scale = lax.rsqrt(jnp.mean(centred * centred, axis=-1, keepdims=True) + norm_eps)
    return (centred * scale, scale)


def norm_back(grad, normed, scale, gain):
    inner = grad * (1.0 + gain)
    result = scale * (
        inner
        - jnp.mean(inner, axis=-1, keepdims=True)
        - normed * jnp.mean(inner * normed, axis=-1, keepdims=True)
    )
    return (result, jnp.sum(grad * normed, axis=1), jnp.sum(grad, axis=1))


def unpack(blocks):
    half = blocks.shape[1]
    width = blocks.shape[2]
    code_w = blocks[0:2].reshape(2 * half, width)
    phone_w = blocks[2]
    head_w = blocks[3:5].reshape(width, 2 * half)
    qkv_w = blocks[5:11].reshape(3, width, width)
    out_w = blocks[11:13].reshape(width, width)
    up_w = blocks[13:21].reshape(4, width, width)
    down_w = blocks[21:29].reshape(4 * width, width)
    return (code_w, phone_w, head_w, qkv_w, out_w, up_w, down_w)


def pack(pieces, half, width):
    return jnp.concatenate([piece.reshape(-1, half, width) for piece in pieces], axis=0)


def attend_scores(queries, key_vecs, same):
    scores = jnp.einsum(
        "rlhe,rmhe->rhlm", queries, key_vecs, preferred_element_type=float_out
    ) * HD ** (-0.5)
    return jnp.where(same[:, None], scores, -1000000000.0)


def forward(matrices, params, phones, codes, segments, section_ids, targets, section_hot):
    code_w, phone_w, head_w, qkv_w, out_w, up_w, down_w = matrices
    rows, length = segments.shape
    levels = (jnp.arange(LEVELS)[None, :] <= section_ids[:, None]).astype(jnp.bfloat16)
    vocab = jnp.arange(CODES)
    multi = jnp.zeros((rows, length, CODES), jnp.bfloat16)
    for level in range(LEVELS):
        multi = (
            multi
            + (codes[:, :, level, None] == vocab).astype(jnp.bfloat16)
            * levels[:, level, None, None]
        )
    phone_hot = (phones[:, :, None] == jnp.arange(PHONES)).astype(jnp.bfloat16)
    stream = jnp.einsum("rlc,cd->rld", multi, code_w, preferred_element_type=float_out)
    stream = stream + jnp.einsum(
        "rlp,pd->rld", phone_hot, phone_w, preferred_element_type=float_out
    )
    stream = stream + sinusoid(positions(segments), D)
    normed_one, scale_one = normalize(stream)
    input_one = (normed_one * (1.0 + params[:, 0]) + params[:, 1]).astype(jnp.bfloat16)
    qkv = jnp.einsum("rld,kde->krle", input_one, qkv_w, preferred_element_type=float_out).astype(
        jnp.bfloat16
    )
    heads = qkv.reshape(3, rows, length, HEADS, HD)
    same = segments[:, :, None] == segments[:, None, :]
    scores = attend_scores(heads[0], heads[1], same)
    log_total = jax.nn.logsumexp(scores, axis=-1)
    probs = jnp.exp(scores - log_total[..., None]).astype(jnp.bfloat16)
    mixed = jnp.einsum("rhlm,rmhe->rlhe", probs, heads[2], preferred_element_type=float_out)
    mixed = mixed.astype(jnp.bfloat16).reshape(rows, length, D)
    stream = stream + jnp.einsum("rld,de->rle", mixed, out_w, preferred_element_type=float_out)
    normed_two, scale_two = normalize(stream)
    input_two = (normed_two * (1.0 + params[:, 2]) + params[:, 3]).astype(jnp.bfloat16)
    hidden = jnp.einsum("rld,gde->rlge", input_two, up_w, preferred_element_type=float_out)
    active = jax.nn.gelu(hidden, approximate=False).astype(jnp.bfloat16).reshape(rows, length, FF)
    stream = stream + jnp.einsum("rlf,fd->rld", active, down_w, preferred_element_type=float_out)
    normed_three, scale_three = normalize(stream)
    input_three = (normed_three * (1.0 + params[:, 4]) + params[:, 5]).astype(jnp.bfloat16)
    logits = jnp.einsum("rld,dc->rlc", input_three, head_w, preferred_element_type=float_out)
    log_norm = jax.nn.logsumexp(logits, axis=-1)
    target_hot = (targets[:, :, None] == vocab).astype(jnp.float32)
    losses = log_norm - jnp.sum(logits * target_hot, axis=-1)
    section_loss = jnp.sum(section_hot * jnp.sum(losses, axis=1)[:, None], axis=0)
    kept = (
        multi,
        phone_hot,
        normed_one,
        scale_one,
        input_one,
        heads,
        same,
        log_total,
        mixed,
        normed_two,
        scale_two,
        input_two,
        hidden,
        active,
        normed_three,
        scale_three,
        input_three,
        logits,
        log_norm,
        target_hot,
    )
    return (kept, section_loss)


def backward(matrices, params, kept, row_weight):
    code_w, phone_w, head_w, qkv_w, out_w, up_w, down_w = matrices
    (
        multi,
        phone_hot,
        normed_one,
        scale_one,
        input_one,
        heads,
        same,
        log_total,
        mixed,
        normed_two,
        scale_two,
        input_two,
        hidden,
        active,
        normed_three,
        scale_three,
        input_three,
        logits,
        log_norm,
        target_hot,
    ) = kept
    rows, length = (same.shape[0], same.shape[1])
    predicted = jnp.exp(logits - log_norm[..., None])
    grad_logits = ((predicted - target_hot) * row_weight[:, None, None]).astype(jnp.bfloat16)
    grad_head = jnp.einsum(
        "rld,rlc->dc", input_three, grad_logits, preferred_element_type=float_out
    )
    grad_three = jnp.einsum("rlc,dc->rld", grad_logits, head_w, preferred_element_type=float_out)
    grad_stream, gain_three, shift_three = norm_back(
        grad_three, normed_three, scale_three, params[:, 4]
    )
    grad_ffn = grad_stream.astype(jnp.bfloat16)
    grad_down = jnp.einsum("rlf,rld->fd", active, grad_ffn, preferred_element_type=float_out)
    grad_active = jnp.einsum("rld,fd->rlf", grad_ffn, down_w, preferred_element_type=float_out)
    _, gelu_pull = jax.vjp(lambda value: jax.nn.gelu(value, approximate=False), hidden)
    grad_hidden = gelu_pull(grad_active.reshape(hidden.shape))[0].astype(jnp.bfloat16)
    grad_up = jnp.einsum("rld,rlge->gde", input_two, grad_hidden, preferred_element_type=float_out)
    grad_two = jnp.einsum("rlge,gde->rld", grad_hidden, up_w, preferred_element_type=float_out)
    grad_norm_two, gain_two, shift_two = norm_back(grad_two, normed_two, scale_two, params[:, 2])
    grad_stream = grad_stream + grad_norm_two
    grad_attn = grad_stream.astype(jnp.bfloat16)
    grad_out = jnp.einsum("rld,rle->de", mixed, grad_attn, preferred_element_type=float_out)
    grad_mixed = jnp.einsum("rle,de->rld", grad_attn, out_w, preferred_element_type=float_out)
    grad_mixed = grad_mixed.astype(jnp.bfloat16).reshape(rows, length, HEADS, HD)
    scores = attend_scores(heads[0], heads[1], same)
    probs = jnp.exp(scores - log_total[..., None])
    probs_low = probs.astype(jnp.bfloat16)
    grad_values = jnp.einsum(
        "rhlm,rlhe->rmhe", probs_low, grad_mixed, preferred_element_type=float_out
    )
    grad_probs = jnp.einsum(
        "rlhe,rmhe->rhlm", grad_mixed, heads[2], preferred_element_type=float_out
    )
    grad_scores = (
        probs * (grad_probs - jnp.sum(probs * grad_probs, axis=-1, keepdims=True))
    ).astype(jnp.bfloat16)
    grad_queries = jnp.einsum(
        "rhlm,rmhe->rlhe", grad_scores, heads[1], preferred_element_type=float_out
    ) * HD ** (-0.5)
    grad_key_vecs = jnp.einsum(
        "rhlm,rlhe->rmhe", grad_scores, heads[0], preferred_element_type=float_out
    ) * HD ** (-0.5)
    grad_qkv = (
        jnp.stack([grad_queries, grad_key_vecs, grad_values])
        .reshape(3, rows, length, D)
        .astype(jnp.bfloat16)
    )
    grad_proj = jnp.einsum("rld,krle->kde", input_one, grad_qkv, preferred_element_type=float_out)
    grad_one = jnp.einsum("krle,kde->rld", grad_qkv, qkv_w, preferred_element_type=float_out)
    grad_norm_one, gain_one, shift_one = norm_back(grad_one, normed_one, scale_one, params[:, 0])
    grad_embed = (grad_stream + grad_norm_one).astype(jnp.bfloat16)
    grad_code = jnp.einsum("rlc,rld->cd", multi, grad_embed, preferred_element_type=float_out)
    grad_phone = jnp.einsum("rlp,rld->pd", phone_hot, grad_embed, preferred_element_type=float_out)
    half = phone_w.shape[0]
    block_grads = pack(
        (grad_code, grad_phone, grad_head, grad_proj, grad_out, grad_up, grad_down), half, D
    )
    row_grads = jnp.stack(
        [gain_one, shift_one, gain_two, shift_two, gain_three, shift_three], axis=1
    )
    return (block_grads, row_grads)


def adam(weight, first, second, grad, rate, step):
    new_first = beta_one * first + (1.0 - beta_one) * grad
    new_second = beta_two * second + (1.0 - beta_two) * grad * grad
    fix_one = 1.0 - jnp.power(beta_one, step)
    fix_two = 1.0 - jnp.power(beta_two, step)
    update = new_first / fix_one / (jnp.sqrt(new_second / fix_two) + adam_eps)
    return (weight - rate * (update + decay_rate * weight), new_first, new_second)


def per_device(
    masters,
    first_moment,
    second_moment,
    section_table,
    table_first,
    table_second,
    owners,
    step_count,
    phones,
    codes,
    segments,
    sections,
    targets,
):
    section_width = lax.axis_size("section")
    batch_width = lax.axis_size("batch")
    section_ids = sections[:, 0]
    row_count = section_ids.shape[0]
    section_hot = (section_ids[:, None] == jnp.arange(SECTIONS)[None, :]).astype(jnp.float32)
    local_counts = jnp.sum(section_hot, axis=0) * segments.shape[1]
    shard_rows = lax.all_gather(masters.astype(jnp.bfloat16), "batch", axis=1, tiled=True)
    all_slots = lax.all_gather(shard_rows, "section", axis=0, tiled=True)
    blocks = jnp.take(all_slots, owners, axis=0)
    table = lax.all_gather(section_table, "section", axis=0, tiled=True)
    matrices = unpack(blocks)
    params = jnp.einsum("rs,sk->rk", section_hot, table, precision=exact).reshape(
        row_count, 6, 1, D
    )
    kept, section_loss = forward(
        matrices, params, phones, codes, segments, section_ids, targets, section_hot
    )
    counts, loss_sums = lax.psum((local_counts, section_loss), ("section", "batch"))
    row_weight = jnp.sum(section_hot / (SECTIONS * counts)[None, :], axis=1)
    block_grads, row_grads = backward(matrices, params, kept, row_weight)
    table_local = jnp.einsum(
        "rs,rk->sk", section_hot, row_grads.reshape(row_count, 6 * D), precision=exact
    )
    table_sum = lax.psum(table_local, ("section", "batch"))
    own_count = section_table.shape[0]
    table_grad = lax.dynamic_slice_in_dim(
        table_sum, lax.axis_index("section") * own_count, own_count, 0
    )
    per_group = masters.shape[0]
    piece_rows = masters.shape[1]
    split_grads = block_grads.reshape(block_grads.shape[0], batch_width, piece_rows, D)
    group_of = owners // per_group
    within = owners % per_group
    target_slot = (
        (group_of * batch_width)[:, None] * per_group
        + jnp.arange(batch_width)[None, :] * per_group
        + within[:, None]
    )
    arranged = jnp.zeros((section_width * batch_width * per_group, piece_rows, D), jnp.float32)
    arranged = arranged.at[target_slot.reshape(-1)].set(split_grads.reshape(-1, piece_rows, D))
    own_grad = lax.psum_scatter(arranged, ("section", "batch"), scatter_dimension=0, tiled=True)
    square_sum = jnp.sum(own_grad * own_grad) + jnp.sum(table_grad * table_grad) / batch_width
    grad_norm = jnp.sqrt(lax.psum(square_sum, ("section", "batch")))
    clip_factor = jnp.minimum(1.0, clip_limit / grad_norm)
    step = step_count[0].astype(jnp.float32)
    new_masters, new_first, new_second = adam(
        masters, first_moment, second_moment, own_grad * clip_factor, learn_rate, step
    )
    new_table, new_table_first, new_table_second = adam(
        section_table, table_first, table_second, table_grad * clip_factor, table_rate, step
    )
    loss = jnp.sum(loss_sums / (SECTIONS * counts))
    return (
        new_masters,
        new_first,
        new_second,
        new_table,
        new_table_first,
        new_table_second,
        grad_norm,
        loss,
    )


def solution(mesh):
    return jax.shard_map(
        per_device,
        mesh=mesh,
        in_specs=(
            P("section", "batch", None),
            P("section", "batch", None),
            P("section", "batch", None),
            P("section", None),
            P("section", None),
            P("section", None),
            P(),
            P(),
            P(("section", "batch"), None),
            P(("section", "batch"), None, None),
            P(("section", "batch"), None),
            P(("section", "batch"), None),
            P(("section", "batch"), None),
        ),
        out_specs=(
            P("section", "batch", None),
            P("section", "batch", None),
            P("section", "batch", None),
            P("section", None),
            P("section", None),
            P("section", None),
            P(),
            P(),
        ),
        check_vma=False,
    )
```

profile of v0, /device:TPU:0, one launch (start us, length us, event | category | flops | bytes accessed | tf_op | source)
XLA Modules:
  0.0 2446.8 jit_solution(5869725408270620591)
XLA Ops:
  7.2 2.7 convert_element_type.90
  10.0 128.4 %all-gather.4.cloned.1.call-done = bf16[8,512,1024]{2,1,0:T(8,128)(2,1)} async-done(((bf16[8,64,1024]{2,1,0:T(8,128)(2,1)}), bf16[8,512,1024]{2,1,0:T(8,128)(2,1)}) %all-gather.4.cloned.1.call-update) | async-done | bytes 8388624 | tf_op jit(solution)/shard_map/all_gather | solution.py:270
  139.2 38.7 %psum.28 = f32[8]{0:T(128)S(1)} all-reduce(f32[8]{0:T(128)S(1)} %broadcast_multiply_fusion.10), channel_id=1, replica_groups=mesh['section'=4,'batch'=8] {'section','batch'}, use_global_device_ids=true, to_apply=%region_13.14 | all-reduce | flops 8 | bytes 64 | tf_op jit(solution)/shard_map/psum | solution.py:281
  179.1 7.4 all-gather
  189.8 151.7 %all-gather.6.cloned.1.call-done = bf16[32,512,1024]{2,1,0:T(8,128)(2,1)} async-done(((bf16[8,512,1024]{2,1,0:T(8,128)(2,1)}), bf16[32,512,1024]{2,1,0:T(8,128)(2,1)}) %all-gather.6.cloned.1.call-update) | async-done | bytes 33554448 | tf_op jit(solution)/shard_map/all_gather | solution.py:271
  341.5 22.0 gather_fusion
  363.5 20.5 broadcast_select_fusion
  384.0 5.7 fusion.89
  389.7 3.5 slice.160
  393.2 14.4 fusion.88
  407.8 6.3 fusion.82
  414.1 17.7 fusion.92
  432.4 1.4 copy-done.47
  433.8 9.9 convert_bitcast_fusion
  443.7 3.3 fusion.90
  447.0 13.8 fusion
  460.8 14.1 exponential_reduce_fusion
  475.0 15.8 convolution_convert_fusion.2
  490.8 6.3 fusion.93
  497.7 49.3 %multiply_convert_fusion.1 = (bf16[2,512,4,1024]{3,1,2,0:T(8,128)(2,1)}, f32[2,512,4,1024]{3,1,2,0:T(8,128)}, f32[2,512,4,1024]{3,1,2,0:T(8,128)}) fusion(bf16[4,1024,1024,1]{2,1,0,3:T(8,128)(2,1)S(1)} %bitcast.258, f32[2,512,1024]{2,1,0:T(8,128)S(1)} %get-tuple-element.74, f32[2,1024]{1,0:T(2,128)S(1)} %get-tuple-element.95, ...), kind=kOutput, calls=%fused_computation.14 | convolution fusion | flops 8867807232 | bytes 54550528 | tf_op jit(solution)/shard_map/rld,gde->rlge/dot_general | solution.py:119
  547.0 11.4 copy.71
  558.4 14.6 fusion.94
  573.7 2.5 copy-done.28
  576.2 2.5 fusion.95
  578.8 1.6 select_reduce_fusion
  580.5 0.6 select_reduce_fusion.1
  581.2 4.0 multiply_reduce_fusion.1
  585.2 1.2 subtract_multiply_fusion
  586.4 24.3 add_convert_fusion
  610.7 15.8 fusion.12
  626.5 1.4 multiply_add_fusion
  627.9 2.0 copy-done.12
  629.9 3.7 convolution_convert_fusion.1
  633.6 2.9 copy.73
  636.6 25.7 %multiply_reduce_fusion = (f32[2,16,512]{2,1,0:T(8,128)S(1)}, f32[2,16,512,512]{2,3,1,0:T(8,128)}) fusion(f32[2,16,512,512]{2,3,1,0:T(8,128)} %get-tuple-element.72, f32[2,16,512]{2,1,0:T(8,128)S(1)} %copy-done.30, pred[2,512,512]{1,2,0:T(8,128)(4,1)S(1)} %copy-done.3, bf16[2,512,16,64]{1,3,2,0:T(8,128)(2,1)S(1)} %bitcast.243, ...), kind=kOutput, calls=%fused_computation.3 | convolution fusion | flops 1115668480 | bytes 71958528 | tf_op jit(solution)/shard_map/rlhe,rmhe->rhlm/dot_general | solution.py:207
  662.3 28.6 %multiply_convert_fusion = bf16[2,16,512,512]{2,3,1,0:T(8,128)(2,1)} fusion(f32[2,16,512,512]{2,3,1,0:T(8,128)} %get-tuple-element.83, f32[2,16,512,512]{2,3,1,0:T(8,128)} %get-tuple-element.72, f32[2,16,512]{2,1,0:T(8,128)S(1)} %get-tuple-element.82, f32[2,16,512]{2,1,0:T(8,128)S(1)} %copy-done.30, pred[2,512,512]{1,2,0:T(8,128)(4,1)S(1)} %copy-done.3), kind=kLoop, calls=%fused_computation.2 | loop fusion | flops 50331648 | bytes 84541440 | tf_op jit(solution)/shard_map/convert_element_type | solution.py:212
  690.9 9.9 multiply_convert_fusion.3
  700.8 13.0 multiply_convert_fusion.2
  713.8 16.2 convolution_convert_fusion
  730.1 23.2 fusion.76
  753.4 5.4 fusion.49
  758.7 2.4 copy.77
  761.2 4.1 copy.78
  765.3 3.9 copy.79
  769.3 14.6 fusion.23
  784.0 9.2 fusion.11
  793.3 0.9 fusion.60
  794.4 5.6 add_convert_fusion.1
  800.2 5.5 fusion.80
  805.8 2.3 constant_dynamic-update-slice_fusion.3
  808.1 2.6 bitcast_dynamic-update-slice_fusion.2
  810.7 2.3 constant_dynamic-update-slice_fusion.2
  813.0 12.1 constant_dynamic-update-slice_fusion.1
  825.1 4.3 bitcast_dynamic-update-slice_fusion.1
  829.4 13.1 constant_dynamic-update-slice_fusion
  842.5 12.4 bitcast_dynamic-update-slice_fusion
  854.9 21.3 broadcast_in_dim.44
  876.2 106.9 %scatter_fusion = f32[256,64,1024]{2,1,0:T(8,128)} fusion(f32[256,64,1024]{2,1,0:T(8,128)} %broadcast_in_dim.44, s32[232]{0:T(256)S(1)} %bitcast.280, f32[232,64,1024]{2,1,0:T(8,128)} %bitcast.238), kind=kCustom, calls=%fused_computation.1 | custom fusion | bytes 182453152 | tf_op jit(solution)/shard_map/scatter | solution.py:303
  984.1 1.6 multiply_reduce_fusion.10
  986.3 1399.5 %reduce-scatter.2.cloned.1.call-done = f32[8,64,1024]{2,1,0:T(8,128)} async-done(((f32[256,64,1024]{2,1,0:T(8,128)}), f32[8,64,1024]{2,1,0:T(8,128)}) %reduce-scatter.2.cloned.1.call-update) | async-done | bytes 2097168 | tf_op jit(solution)/shard_map/reduce_scatter | solution.py:304
  2385.8 2.7 multiply_reduce_fusion.9
  2389.2 39.4 %all-reduce.1 = (f32[]{:T(128)}, f32[8]{0:T(128)S(1)}) all-reduce(f32[]{:T(128)S(6)} %add.310, f32[8]{0:T(128)S(1)} %copy-done.99), channel_id=1, replica_groups=mesh['section'=4,'batch'=8] {'section','batch'}, use_global_device_ids=true, to_apply=%region_33.34 | all-reduce | flops 9 | bytes 72 | tf_op jit(solution)/shard_map/psum | solution.py:306
  2430.0 1.7 multiply_subtract_fusion.1
  2431.7 6.9 multiply_subtract_fusion
  (300 shorter events, 8.1 us)
Async XLA Ops:
  7.2 131.2 %all-gather.4.cloned.1.call-start = ((), (), s32[]{:S(2)}) async-start(), calls=%async_computation.1 | async-start | bytes 9437184 | tf_op jit(solution)/shard_map/all_gather | solution.py:270
  10.0 331.5 %all-gather.6.cloned.1.call-start = ((), (), s32[]{:S(2)}) async-start(), calls=%async_computation.2 | async-start | bytes 41943040 | tf_op jit(solution)/shard_map/all_gather | solution.py:271
  138.4 39.5 %copy-start.33 = (s32[2,512]{1,0:T(2,128)S(1)}, s32[2,512]{1,0:T(2,128)}, u32[]{:S(2)}) copy-start(s32[2,512]{1,0:T(2,128)} %param.23) | copy-start | bytes 12292
  138.4 40.7 %copy-start.31 = (f32[2,6144]{1,0:T(2,128)S(1)}, f32[2,6144]{1,0:T(2,128)}, u32[]{:S(2)}) copy-start(f32[2,6144]{1,0:T(2,128)} %param.16) | copy-start | bytes 147460
  138.4 48.6 %copy-start.103 = (s32[29]{0:T(128)S(1)}, s32[29]{0:T(128)}, u32[]{:S(2)}) copy-start(s32[29]{0:T(128)} %param.19) | copy-start | bytes 352
  138.4 50.1 %copy-start.42 = (s32[2,512,8]{1,2,0:T(8,128)S(1)}, s32[2,512,8]{1,2,0:T(8,128)}, u32[]{:S(2)}) copy-start(s32[2,512,8]{1,2,0:T(8,128)} %param.22) | copy-start | bytes 98308
  138.4 845.6 %all-reduce.4.cloned.1.call-start = ((), (), s32[]{:S(2)}) async-start(), calls=%async_computation.4 | async-start | bytes 393216 | tf_op jit(solution)/shard_map/psum | solution.py:287
  188.4 219.3 %copy-start.83 = (bf16[2]{0:T(256)(128)(2,1)}, bf16[2]{0:T(256)(128)(2,1)S(1)}, u32[]{:S(2)}) copy-start(bf16[2]{0:T(256)(128)(2,1)S(1)} %get-tuple-element.58) | copy-start | bytes 16
  188.4 219.3 %copy-start.85 = (bf16[2]{0:T(256)(128)(2,1)}, bf16[2]{0:T(256)(128)(2,1)S(1)}, u32[]{:S(2)}) copy-start(bf16[2]{0:T(256)(128)(2,1)S(1)} %get-tuple-element.59) | copy-start | bytes 16
  188.4 219.3 %copy-start.87 = (bf16[2]{0:T(256)(128)(2,1)}, bf16[2]{0:T(256)(128)(2,1)S(1)}, u32[]{:S(2)}) copy-start(bf16[2]{0:T(256)(128)(2,1)S(1)} %get-tuple-element.60) | copy-start | bytes 16
  188.4 219.3 %copy-start.89 = (bf16[2]{0:T(256)(128)(2,1)}, bf16[2]{0:T(256)(128)(2,1)S(1)}, u32[]{:S(2)}) copy-start(bf16[2]{0:T(256)(128)(2,1)S(1)} %get-tuple-element.61) | copy-start | bytes 16
  188.4 219.3 %copy-start.91 = (bf16[2]{0:T(256)(128)(2,1)}, bf16[2]{0:T(256)(128)(2,1)S(1)}, u32[]{:S(2)}) copy-start(bf16[2]{0:T(256)(128)(2,1)S(1)} %get-tuple-element.62) | copy-start | bytes 16
  188.4 219.3 %copy-start.93 = (bf16[2]{0:T(256)(128)(2,1)}, bf16[2]{0:T(256)(128)(2,1)S(1)}, u32[]{:S(2)}) copy-start(bf16[2]{0:T(256)(128)(2,1)S(1)} %get-tuple-element.63) | copy-start | bytes 16
  188.4 219.3 %copy-start.95 = (bf16[2]{0:T(256)(128)(2,1)}, bf16[2]{0:T(256)(128)(2,1)S(1)}, u32[]{:S(2)}) copy-start(bf16[2]{0:T(256)(128)(2,1)S(1)} %get-tuple-element.64) | copy-start | bytes 16
  188.4 219.3 %copy-start.97 = (bf16[2]{0:T(256)(128)(2,1)}, bf16[2]{0:T(256)(128)(2,1)S(1)}, u32[]{:S(2)}) copy-start(bf16[2]{0:T(256)(128)(2,1)S(1)} %get-tuple-element.65) | copy-start | bytes 16
  188.6 219.1 %copy-start.63 = (s32[2,512]{1,0:T(2,128)}, s32[2,512]{1,0:T(2,128)S(1)}, u32[]{:S(2)}) copy-start(s32[2,512]{1,0:T(2,128)S(1)} %get-tuple-element.85) | copy-start | bytes 12292
  188.6 219.1 %copy-start.65 = (s32[2,512]{1,0:T(2,128)}, s32[2,512]{1,0:T(2,128)S(1)}, u32[]{:S(2)}) copy-start(s32[2,512]{1,0:T(2,128)S(1)} %get-tuple-element.86) | copy-start | bytes 12292
  188.6 219.1 %copy-start.67 = (s32[2,512]{1,0:T(2,128)}, s32[2,512]{1,0:T(2,128)S(1)}, u32[]{:S(2)}) copy-start(s32[2,512]{1,0:T(2,128)S(1)} %get-tuple-element.87) | copy-start | bytes 12292
  188.6 219.1 %copy-start.69 = (s32[2,512]{1,0:T(2,128)}, s32[2,512]{1,0:T(2,128)S(1)}, u32[]{:S(2)}) copy-start(s32[2,512]{1,0:T(2,128)S(1)} %get-tuple-element.88) | copy-start | bytes 12292
  188.7 219.1 %copy-start.71 = (s32[2,512]{1,0:T(2,128)}, s32[2,512]{1,0:T(2,128)S(1)}, u32[]{:S(2)}) copy-start(s32[2,512]{1,0:T(2,128)S(1)} %get-tuple-element.89) | copy-start | bytes 12292
  188.7 219.1 %copy-start.73 = (s32[2,512]{1,0:T(2,128)}, s32[2,512]{1,0:T(2,128)S(1)}, u32[]{:S(2)}) copy-start(s32[2,512]{1,0:T(2,128)S(1)} %get-tuple-element.90) | copy-start | bytes 12292
  188.7 219.1 %copy-start.75 = (s32[2,512]{1,0:T(2,128)}, s32[2,512]{1,0:T(2,128)S(1)}, u32[]{:S(2)}) copy-start(s32[2,512]{1,0:T(2,128)S(1)} %get-tuple-element.91) | copy-start | bytes 12292
  188.7 219.1 %copy-start.77 = (s32[2,512]{1,0:T(2,128)}, s32[2,512]{1,0:T(2,128)S(1)}, u32[]{:S(2)}) copy-start(s32[2,512]{1,0:T(2,128)S(1)} %get-tuple-element.92) | copy-start | bytes 12292
  188.8 243.6 %copy-start.40 = (f32[2,1024]{1,0:T(2,128)}, f32[2,1024]{1,0:T(2,128)S(1)}, u32[]{:S(2)}) copy-start(f32[2,1024]{1,0:T(2,128)S(1)} %get-tuple-element.98) | copy-start | bytes 24580
  188.8 243.6 %copy-start.56 = (f32[2,1024]{1,0:T(2,128)}, f32[2,1024]{1,0:T(2,128)S(1)}, u32[]{:S(2)}) copy-start(f32[2,1024]{1,0:T(2,128)S(1)} %get-tuple-element.97) | copy-start | bytes 24580
  188.8 308.9 %copy-start.60 = (f32[2,1024]{1,0:T(2,128)}, f32[2,1024]{1,0:T(2,128)S(1)}, u32[]{:S(2)}) copy-start(f32[2,1024]{1,0:T(2,128)S(1)} %get-tuple-element.95) | copy-start | bytes 24580
  189.8 285.2 %copy-start.2 = (pred[2,512,512]{1,2,0:T(8,128)(4,1)}, pred[2,512,512]{1,2,0:T(8,128)(4,1)S(1)}, u32[]{:S(2)}) copy-start(pred[2,512,512]{1,2,0:T(8,128)(4,1)S(1)} %broadcast_compare_fusion) | copy-start | bytes 1572868
  393.2 39.2 %copy-start.20 = (bf16[6,512,1024]{2,1,0:T(8,128)(2,1)}, bf16[6,512,1024]{2,1,0:T(8,128)(2,1)S(1)}, u32[]{:S(2)}) copy-start(bf16[6,512,1024]{2,1,0:T(8,128)(2,1)S(1)} %slice.160) | copy-start | bytes 18874372
  447.0 13.8 copy-start
  447.0 13.8 copy-start.4
  447.0 28.0 %copy-start.7 = (bf16[1,2,512,1024]{2,3,1,0:T(8,128)(2,1)}, bf16[1,2,512,1024]{2,3,1,0:T(8,128)(2,1)S(1)}, u32[]{:S(2)}) copy-start(bf16[1,2,512,1024]{2,3,1,0:T(8,128)(2,1)S(1)} %get-tuple-element.43) | copy-start | bytes 6291460
  474.9 15.8 copy-start.29
  497.1 50.0 %copy-start.10 = (f32[2,512,1024]{2,1,0:T(8,128)}, f32[2,512,1024]{2,1,0:T(8,128)S(1)}, u32[]{:S(2)}) copy-start(f32[2,512,1024]{2,1,0:T(8,128)S(1)} %get-tuple-element.74) | copy-start | bytes 12582916
  586.4 40.1 %copy-start.8 = (f32[2,512,1024]{2,1,0:T(8,128)}, f32[2,512,1024]{2,1,0:T(8,128)S(1)}, u32[]{:S(2)}) copy-start(f32[2,512,1024]{2,1,0:T(8,128)S(1)} %subtract_multiply_fusion) | copy-start | bytes 12582916
  586.4 24.3 copy-start.11
  636.5 25.8 %copy-start.5 = (bf16[2,512,1024]{1,2,0:T(8,128)(2,1)}, bf16[2,512,1024]{1,2,0:T(8,128)(2,1)S(1)}, u32[]{:S(2)}) copy-start(bf16[2,512,1024]{1,2,0:T(8,128)(2,1)S(1)} %copy.73) | copy-start | bytes 6291460
  662.3 28.6 %copy-start.1 = (bf16[1,2,512,1024]{2,3,1,0:T(8,128)(2,1)S(1)}, bf16[1,2,512,1024]{2,3,1,0:T(8,128)(2,1)}, u32[]{:S(2)}) copy-start(bf16[1,2,512,1024]{2,3,1,0:T(8,128)(2,1)} %copy-done) | copy-start | bytes 6291460
  713.8 16.2 copy-start.61
  730.0 23.3 copy-start.15
  730.0 23.3 copy-start.23
  730.0 23.3 copy-start.37
  730.0 23.3 copy-start.44
  730.0 23.3 copy-start.46
  730.0 23.3 copy-start.59
  730.0 23.3 copy-start.80
  730.0 23.3 copy-start.82
  730.1 23.3 copy-start.102
  761.2 22.7 slice-start.4
  769.2 14.6 copy-start.17
  769.2 14.6 slice-start.5
  769.3 14.6 copy-start.24
  769.3 14.6 copy-start.25
  769.3 14.6 copy-start.26
  794.2 1591.6 %reduce-scatter.2.cloned.1.call-start = ((), (), s32[]{:S(2)}) async-start(), calls=%async_computation.3 | async-start | bytes 69206016 | tf_op jit(solution)/shard_map/reduce_scatter | solution.py:304
  825.1 17.4 slice-start
  829.4 13.1 copy-start.9
  829.4 13.1 slice-start.1
  854.9 21.3 copy-start.62
  983.1 1406.1 %copy-start.99 = (f32[8]{0:T(128)S(1)}, f32[8]{0:T(128)}, u32[]{:S(2)}) copy-start(f32[8]{0:T(128)} %get-tuple-element.22) | copy-start | bytes 100
  983.1 1446.2 %copy-start.108 = (f32[8]{0:T(128)S(1)}, f32[8]{0:T(128)}, u32[]{:S(2)}) copy-start(f32[8]{0:T(128)} %copy-done.107) | copy-start | bytes 100
  983.1 1446.8 %copy-start.32 = (f32[2,6144]{1,0:T(2,128)S(1)}, f32[2,6144]{1,0:T(2,128)}, u32[]{:S(2)}) copy-start(f32[2,6144]{1,0:T(2,128)} %param.16) | copy-start | bytes 147460
  983.1 1446.8 %copy-start.34 = (f32[2,6144]{1,0:T(2,128)S(1)}, f32[2,6144]{1,0:T(2,128)}, u32[]{:S(2)}) copy-start(f32[2,6144]{1,0:T(2,128)} %param.18) | copy-start | bytes 147460
  983.1 1446.8 %copy-start.35 = (f32[2,6144]{1,0:T(2,128)S(1)}, f32[2,6144]{1,0:T(2,128)}, u32[]{:S(2)}) copy-start(f32[2,6144]{1,0:T(2,128)} %param.17) | copy-start | bytes 147460
  983.1 1448.6 %copy-start.19 = (f32[8,64,1024]{2,1,0:T(8,128)S(1)}, f32[8,64,1024]{2,1,0:T(8,128)}, u32[]{:S(2)}) copy-start(f32[8,64,1024]{2,1,0:T(8,128)} %param.13) | copy-start | bytes 6291460
  (55 other events, 352.7 us)
Sparse Core Ops, SparseCore 0:
  10.8 127.5 all-gather.3
  140.0 201.4 all-gather.5
  794.3 122.9 all-reduce.3
  983.3 1402.4 reduce-scatter.1
where the time goes:
time: 2450 us
  waiting for transfers between devices  1680 us (69%)
  matrix products  327 us (13%)
  local copies, waits for them, and re-layouts  240 us (10%)
  other arithmetic  94.7 us (4%)
  blocking collectives  85.5 us (3%)
    reduce_scatter x1, waiting for transfers between devices, per_device(): lax.psum_scatter(arranged, ('section', 'batch'), scatter_dimension=0, til...  1400 us
    all_gather x1, waiting for transfers between devices, per_device(): all_slots = lax.all_gather(shard_rows, 'section', axis=0, tiled=True)  152 us
    all_gather x1, waiting for transfers between devices, per_device(): lax.all_gather(masters.astype(jnp.bfloat16), 'batch', axis=1, tiled=True)  128 us
    scatter x1, local copies, waits for them, and re-layouts, per_device(): arranged.at[target_slot.reshape(-1)]  107 us
    dot_general x1, matrix products, forward(): jnp.einsum('rld,gde->rlge', input_two, up_w, preferred_element_type=float...  49.3 us
  transfers between devices with their start and end apart: 4, of which 3 were waited for; matrix products, arithmetic and copies ran while one was open for 8% of the time, Pallas kernels for 0%

commit v1 on v0

--- a/solution.py
+++ b/solution.py
@@ -1,8 +1,11 @@
+import functools
 import math
 
 import jax
 import jax.numpy as jnp
 from jax import lax
+from jax.experimental import pallas as pl
+from jax.experimental.pallas import tpu as pltpu
 from jax.sharding import PartitionSpec as P
 
 D = 1024
@@ -13,7 +16,7 @@
 LEVELS = 8
 PHONES = 512
 SECTIONS = 8
-
+CORES = 2
 
 clip_limit = 0.002
 learn_rate = 0.02
@@ -26,13 +29,767 @@
 pos_scale = 0.1
 exact = lax.Precision.HIGHEST
 float_out = jnp.float32
+low = jnp.bfloat16
+MESH = pl.DeviceIdType.MESH
+MIB = 1 << 20
+
+
+class Place:
+    def __init__(self, mesh):
+        self.groups = mesh.shape["section"]
+        self.batch = mesh.shape["batch"]
+        self.ny = self.groups // CORES
+        self.nx = 1 << (int(math.log2(self.batch)) // 2)
+        self.nz = self.batch // self.nx
+        self.panel = D // self.groups
+        self.half = D // CORES
+
+    def here(self):
+        self.s = lax.axis_index("section")
+        self.j = lax.axis_index("batch")
+        self.y = self.s // CORES
+        self.c = self.s % CORES
+        self.z = self.j // self.nx
+        self.x = self.j % self.nx
+
+    def panel_of(self, s):
+        return (s % CORES) * self.ny + s // CORES
+
+    def section_peer(self, d):
+        return (self.s + d) % self.groups
+
+    def x_of(self, d):
+        return (self.x + d) % self.nx
+
+    def y_of(self, d):
+        return (self.y + d) % self.ny
+
+    def z_of(self, d):
+        return (self.z + d) % self.nz
+
+    def at_x(self, d):
+        return (self.s, self.z * self.nx + self.x_of(d))
+
+    def at_y(self, d):
+        return (self.y_of(d) * CORES + self.c, self.j)
+
+    def at_z(self, d):
+        return (self.s, self.z_of(d) * self.nx + self.x)
+
+    def at_core(self):
+        return (self.y * CORES + (1 - self.c), self.j)
+
+    def columns(self, index, width):
+        return pl.ds(pl.multiple_of(index * width, width), width)
+
+    def barrier(self):
+        sem = pltpu.get_barrier_semaphore()
+        peers = [(self.section_peer(d), self.j) for d in range(1, self.groups)]
+        peers += [self.at_x(d) for d in range(1, self.nx)]
+        peers += [self.at_z(d) for d in range(1, self.nz)]
+        for peer in peers:
+            pl.semaphore_signal(sem, inc=1, device_id=peer, device_id_type=MESH)
+        pl.semaphore_wait(sem, len(peers))
+
+    def small_slots(self):
+        return (self.groups - 1) + (self.nx - 1) + (self.nz - 1)
+
+    def small_sum(self, value, sent, landed, send_sem, recv_sem):
+        slot = 0
+        stages = (
+            (self.groups, lambda d: (self.section_peer(d), self.j)),
+            (self.nx, self.at_x),
+            (self.nz, self.at_z),
+        )
+        for stage, (count, target) in enumerate(stages):
+            sent[stage] = value
+            copies = []
+            for d in range(1, count):
+                copy = remote(
+                    sent.at[stage], landed.at[slot], send_sem.at[slot], recv_sem.at[slot], target(d)
+                )
+                copy.start()
+                copies.append((copy, slot))
+                slot += 1
+            for copy, _ in copies:
+                copy.wait()
+            for _, where in copies:
+                value = value + landed[where]
+        return value
+
+
+def remote(src, dst, send_sem, recv_sem, device):
+    return pltpu.make_async_remote_copy(
+        src_ref=src,
+        dst_ref=dst,
+        send_sem=send_sem,
+        recv_sem=recv_sem,
+        device_id=device,
+        device_id_type=MESH,
+    )
+
+
+def gather_kernel(
+    pc,
+    owners_ref,
+    masters_ref,
+    table_ref,
+    counts_ref,
+    w_ref,
+    table_out,
+    counts_out,
+    rounded,
+    slots,
+    pieces,
+    sent,
+    landed,
+    a_send,
+    a_recv,
+    t_send,
+    t_recv,
+    own_sem,
+    z_send,
+    z_recv,
+    e_send,
+    e_recv,
+    f_send,
+    f_recv,
+    c_send,
+    c_recv,
+    m_send,
+    m_recv,
+):
+    pc.here()
+    blocks = w_ref.shape[0]
+    per_group = masters_ref.shape[0]
+    own_sections = table_ref.shape[0]
+    mine = pc.columns(pc.panel_of(pc.s), pc.panel)
+    core_half = pc.columns(pc.c, pc.half)
+    pc.barrier()
+    rounded[...] = masters_ref[...].astype(low)
+    starts = []
+    for d in range(1, pc.groups):
+        peer = pc.section_peer(d)
+        columns = pc.columns(pc.panel_of(peer), pc.panel)
+        copy = remote(
+            rounded.at[:, :, columns],
+            slots.at[pl.ds(pc.s * per_group, per_group)],
+            a_send.at[d - 1],
+            a_recv.at[d - 1],
+            (peer, pc.j),
+        )
+        copy.start()
+        starts.append(copy)
+        copy = remote(
+            table_ref,
+            table_out.at[pl.ds(pc.s * own_sections, own_sections)],
+            t_send.at[d - 1],
+            t_recv.at[d - 1],
+            (peer, pc.j),
+        )
+        copy.start()
+        starts.append(copy)
+    table_out[pl.ds(pc.s * own_sections, own_sections)] = table_ref[...]
+    slots[pl.ds(pc.s * per_group, per_group)] = rounded[:, :, mine]
+    counts_out[...] = pc.small_sum(counts_ref[...], sent, landed, m_send, m_recv)
+    for copy in starts:
+        copy.wait()
+    for b in range(blocks):
+        pieces[b] = slots[owners_ref[b]]
+
+    def own(b):
+        return pltpu.make_async_copy(
+            pieces.at[b], w_ref.at[b, pc.z, pc.x, :, mine], own_sem.at[b]
+        )
+
+    def along_z(b):
+        return [
+            remote(
+                pieces.at[b],
+                w_ref.at[b, pc.z, pc.x, :, mine],
+                z_send.at[b, d - 1],
+                z_recv.at[b, d - 1],
+                pc.at_z(d),
+            )
+            for d in range(1, pc.nz)
+        ]
+
+    def first_x(b):
+        part = w_ref.at[b, :, pc.x, :, mine]
+        return [
+            remote(part, part, e_send.at[b, d - 1], e_recv.at[b, d - 1], pc.at_x(d))
+            for d in range(1, pc.nx)
+        ]
+
+    def first_y(b):
+        part = w_ref.at[b, :, pc.x, :, mine]
+        return [
+            remote(part, part, e_send.at[b, d - 1], e_recv.at[b, d - 1], pc.at_y(d))
+            for d in range(1, pc.ny)
+        ]
+
+    def then_y(b):
+        part = w_ref.at[b, :, :, :, mine]
+        return [
+            remote(part, part, f_send.at[b, d - 1], f_recv.at[b, d - 1], pc.at_y(d))
+            for d in range(1, pc.ny)
+        ]
+
+    def then_x(b):
+        part = w_ref.at[b, :, pc.x, :, core_half]
+        return [
+            remote(part, part, f_send.at[b, d - 1], f_recv.at[b, d - 1], pc.at_x(d))
+            for d in range(1, pc.nx)
+        ]
+
+    def to_core(b):
+        part = w_ref.at[b, :, :, :, core_half]
+        return [remote(part, part, c_send.at[b], c_recv.at[b], pc.at_core())]
+
+    def begin(copies):
+        for copy in copies:
+            copy.start()
+
+    def landed_all(copies):
+        for copy in copies:
+            copy.wait_recv()
+
+    def gone(copies):
+        for copy in copies:
+            copy.wait_send()
+
+    def by_parity(b, even, odd, act):
+        @pl.when(b % 2 == 0)
+        def _():
+            act(even(b))
+
+        @pl.when(b % 2 == 1)
+        def _():
+            act(odd(b))
+
+    ahead = 4
+
+    def launch(b, carry):
+        own(b).start()
+        begin(along_z(b))
+        return carry
+
+    lax.fori_loop(0, min(ahead, blocks), launch, 0)
+
+    def tick(t, carry):
+        @pl.when(t + ahead < blocks)
+        def _():
+            launch(t + ahead, 0)
+
+        @pl.when(t < blocks)
+        def _():
+            own(t).wait()
+            landed_all(along_z(t))
+            by_parity(t, first_x, first_y, begin)
+
+        b = t - 2
+
+        @pl.when((b >= 0) & (b < blocks))
+        def _():
+            by_parity(b, first_x, first_y, landed_all)
+            by_parity(b, then_y, then_x, begin)
+
+        e = t - 4
+
+        @pl.when((e >= 0) & (e < blocks))
+        def _():
+            by_parity(e, then_y, then_x, landed_all)
+            begin(to_core(e))
+
+        return carry
+
+    lax.fori_loop(0, blocks + 4, tick, 0)
+
+    def finish(b, carry):
+        landed_all(to_core(b))
+        gone(to_core(b))
+        gone(along_z(b))
+        by_parity(b, first_x, first_y, gone)
+        by_parity(b, then_y, then_x, gone)
+        return carry
+
+    lax.fori_loop(0, blocks, finish, 0)
+
+
+def gather_weights(pc, masters, table, counts, owners):
+    per_group, rows, _ = masters.shape
+    blocks = owners.shape[0]
+    own_sections = table.shape[0]
+    hops = max(pc.nx, pc.ny) - 1
+    dma = pltpu.SemaphoreType.DMA
+    vmem = pl.BlockSpec(memory_space=pltpu.VMEM)
+    w, table_all, counts_all = pl.pallas_call(
+        functools.partial(gather_kernel, pc),
+        out_shape=(
+            jax.ShapeDtypeStruct((blocks, pc.nz, pc.nx, rows, D), low),
+            jax.ShapeDtypeStruct((own_sections * pc.groups, 8, D), float_out),
+            jax.ShapeDtypeStruct((8, 128), float_out),
+        ),
+        in_specs=[pl.BlockSpec(memory_space=pltpu.SMEM), vmem, vmem, vmem],
+        out_specs=(pl.BlockSpec(memory_space=pl.ANY), vmem, vmem),
+        scratch_shapes=[
+            pltpu.VMEM((per_group, rows, D), low),
+            pltpu.VMEM((per_group * pc.groups, rows, pc.panel), low),
+            pltpu.VMEM((blocks, rows, pc.panel), low),
+            pltpu.VMEM((3, 8, 128), float_out),
+            pltpu.VMEM((pc.small_slots(), 8, 128), float_out),
+            dma((pc.groups - 1,)),
+            dma((pc.groups - 1,)),
+            dma((pc.groups - 1,)),
+            dma((pc.groups - 1,)),
+            dma((blocks,)),
+            dma((blocks, pc.nz - 1)),
+            dma((blocks, pc.nz - 1)),
+            dma((blocks, hops)),
+            dma((blocks, hops)),
+            dma((blocks, hops)),
+            dma((blocks, hops)),
+            dma((blocks,)),
+            dma((blocks,)),
+            dma((pc.small_slots(),)),
+            dma((pc.small_slots(),)),
+        ],
+        name="gather_weights",
+        compiler_params=pltpu.CompilerParams(
+            collective_id=0, has_side_effects=True, vmem_limit_bytes=24 * MIB
+        ),
+    )(owners, masters, table, counts)
+    return w.reshape(blocks, pc.nz * pc.nx * rows, D), table_all, counts_all
+
+
+def reduce_kernel(pc, sources, *refs):
+    count_in = len({s for s in sources for s in (s[0], s[2])})
+    block_of_ref = refs[0]
+    arrays = refs[1 : 1 + count_in]
+    table_ref, loss_ref = refs[1 + count_in : 3 + count_in]
+    out_ref, table_out, sums_out = refs[3 + count_in : 6 + count_in]
+    (
+        x_buf,
+        y_buf,
+        own_half,
+        send_half,
+        core_in,
+        first_a,
+        first_b,
+        then_a,
+        then_b,
+        z_in,
+        final,
+        by_slot,
+        square,
+        table_in,
+        table_mid,
+        sent,
+        landed,
+        in_sem,
+        c_send,
+        c_recv,
+        e_send,
+        e_recv,
+        f_send,
+        f_recv,
+        z_send,
+        z_recv,
+        a_send,
+        a_recv,
+        o_sem,
+        t_send,
+        t_recv,
+        m_send,
+        m_recv,
+    ) = refs[6 + count_in :]
+    pc.here()
+    blocks = len(sources)
+    per_group = out_ref.shape[0]
+    own_sections = table_out.shape[0]
+    rows = out_ref.shape[1]
+    width = x_buf.shape[2]
+    keep = pc.columns(pc.c, pc.half)
+    away = pc.columns(1 - pc.c, pc.half)
+    pc.barrier()
+
+    def fetch(t, act):
+        for b, (xs, xc, ys, yc) in enumerate(sources):
+
+            @pl.when(t == b)
+            def _(xs=xs, xc=xc, ys=ys, yc=yc, b=b):
+                slot = b % 2
+                x_src = arrays[xs].at[xc[0], :, pl.ds(xc[1], width)]
+                y_src = arrays[ys].at[yc]
+                act(pltpu.make_async_copy(x_src, x_buf.at[slot], in_sem.at[slot, 0]))
+                act(pltpu.make_async_copy(y_src, y_buf.at[slot], in_sem.at[slot, 1]))
+
+    def to_core(b):
+        return [
+            remote(
+                send_half.at[b % 4], core_in.at[b], c_send.at[b], c_recv.at[b], pc.at_core()
+            )
+        ]
+
+    def first_x(b):
+        return [
+            remote(
+                core_in.at[b, :, pc.x_of(d)],
+                first_a.at[b // 2, d - 1],
+                e_send.at[b, d - 1],
+                e_recv.at[b, d - 1],
+                pc.at_x(d),
+            )
+            for d in range(1, pc.nx)
+        ]
+
+    def first_y(b):
+        return [
+            remote(
+                core_in.at[b, :, :, :, pc.columns(pc.y_of(d), pc.panel)],
+                first_b.at[b // 2, d - 1],
+                e_send.at[b, d - 1],
+                e_recv.at[b, d - 1],
+                pc.at_y(d),
+            )
+            for d in range(1, pc.ny)
+        ]
+
+    def then_y(b):
+        return [
+            remote(
+                first_a.at[b // 2, 0, :, :, pc.columns(pc.y_of(d), pc.panel)],
+                then_a.at[b // 2, d - 1],
+                f_send.at[b, d - 1],
+                f_recv.at[b, d - 1],
+                pc.at_y(d),
+            )
+            for d in range(1, pc.ny)
+        ]
+
+    def then_x(b):
+        return [
+            remote(
+                first_b.at[b // 2, 0, :, pc.x_of(d)],
+                then_b.at[b // 2, d - 1],
+                f_send.at[b, d - 1],
+                f_recv.at[b, d - 1],
+                pc.at_x(d),
+            )
+            for d in range(1, pc.nx)
+        ]
+
+    def along_z(b, source):
+        return [
+            remote(
+                source.at[b // 2, 0, pc.z_of(d)],
+                z_in.at[b, d - 1],
+                z_send.at[b, d - 1],
+                z_recv.at[b, d - 1],
+                pc.at_z(d),
+            )
+            for d in range(1, pc.nz)
+        ]
+
+    def begin(copies):
+        for copy in copies:
+            copy.start()
+
+    def landed_all(copies):
+        for copy in copies:
+            copy.wait_recv()
+
+    def gone(copies):
+        for copy in copies:
+            copy.wait_send()
+
+    table_stage = []
+    for d in range(1, pc.groups):
+        peer = pc.section_peer(d)
+        table_stage.append(
+            remote(
+                table_ref.at[pl.ds(peer * own_sections, own_sections)],
+                table_in.at[d - 1],
+                t_send.at[d - 1],
+                t_recv.at[d - 1],
+                (peer, pc.j),
+            )
+        )
+    begin(table_stage)
+    square[...] = jnp.zeros_like(square)
+    final[blocks] = jnp.zeros(final.shape[1:], low)
+    fetch(0, lambda copy: copy.start())
+
+    def tick(t, carry):
+        @pl.when(t + 1 < blocks)
+        def _():
+            fetch(t + 1, lambda copy: copy.start())
+
+        @pl.when(t < blocks)
+        def _():
+            fetch(t, lambda copy: copy.wait())
+            slot = t % 2
+            own_half[slot] = lax.dot_general(
+                x_buf[slot],
+                y_buf[slot, :, keep],
+                (((0,), (0,)), ((), ())),
+                preferred_element_type=float_out,
+            )
+
+            @pl.when(t >= 4)
+            def _():
+                gone(to_core(t - 4))
+
+            send_half[t % 4] = (
+                lax.dot_general(
+                    x_buf[slot],
+                    y_buf[slot, :, away],
+                    (((0,), (0,)), ((), ())),
+                    preferred_element_type=float_out,
+                )
+                .astype(low)
+                .reshape(send_half.shape[1:])
+            )
+            begin(to_core(t))
+
+        b = t - 1
+
+        @pl.when((b >= 0) & (b < blocks))
+        def _():
+            landed_all(to_core(b))
+            core_in[b] = (
+                core_in[b].astype(float_out) + own_half[b % 2].reshape(core_in.shape[1:])
+            ).astype(low)
+
+            @pl.when(b % 2 == 0)
+            def _():
+                begin(first_x(b))
+
+            @pl.when(b % 2 == 1)
+            def _():
+                begin(first_y(b))
+
+        e = t - 3
+
+        @pl.when((e >= 0) & (e < blocks))
+        def _():
+            @pl.when(e % 2 == 0)
+            def _():
+                landed_all(first_x(e))
+                total = core_in[e, :, pc.x].astype(float_out)
+                for d in range(pc.nx - 1):
+                    total = total + first_a[e // 2, d].astype(float_out)
+                first_a[e // 2, 0] = total.astype(low)
+                begin(then_y(e))
+
+            @pl.when(e % 2 == 1)
+            def _():
+                landed_all(first_y(e))
+                total = core_in[e, :, :, :, pc.columns(pc.y, pc.panel)].astype(float_out)
+                for d in range(pc.ny - 1):
+                    total = total + first_b[e // 2, d].astype(float_out)
+                first_b[e // 2, 0] = total.astype(low)
+                begin(then_x(e))
+
+        f = t - 5
+
+        @pl.when((f >= 0) & (f < blocks))
+        def _():
+            @pl.when(f % 2 == 0)
+            def _():
+                landed_all(then_y(f))
+                total = first_a[f // 2, 0, :, :, pc.columns(pc.y, pc.panel)].astype(float_out)
+                for d in range(pc.ny - 1):
+                    total = total + then_a[f // 2, d].astype(float_out)
+                then_a[f // 2, 0] = total.astype(low)
+                begin(along_z(f, then_a))
+
+            @pl.when(f % 2 == 1)
+            def _():
+                landed_all(then_x(f))
+                total = first_b[f // 2, 0, :, pc.x].astype(float_out)
+                for d in range(pc.nx - 1):
+                    total = total + then_b[f // 2, d].astype(float_out)
+                then_b[f // 2, 0] = total.astype(low)
+                begin(along_z(f, then_b))
+
+        g = t - 7
+
+        @pl.when((g >= 0) & (g < blocks))
+        def _():
+            def close(source):
+                landed_all(along_z(g, source))
+                total = source[g // 2, 0, pc.z].astype(float_out)
+                for d in range(pc.nz - 1):
+                    total = total + z_in[g, d].astype(float_out)
+                rounded = total.astype(low)
+                final[g] = rounded
+                wide = rounded.astype(float_out)
+                square[...] += jnp.sum(wide * wide, axis=0, keepdims=True)
+
+            @pl.when(g % 2 == 0)
+            def _():
+                close(then_a)
+
+            @pl.when(g % 2 == 1)
+            def _():
+                close(then_b)
+
+        return carry
+
+    lax.fori_loop(0, blocks + 7, tick, 0)
+
+    for i in range(per_group * pc.groups):
+        by_slot[i] = final[block_of_ref[i]]
+    mine = pc.columns(pc.panel_of(pc.s), pc.panel)
+    ends = []
+    for d in range(1, pc.groups):
+        peer = pc.section_peer(d)
+        ends.append(
+            remote(
+                by_slot.at[pl.ds(peer * per_group, per_group)],
+                out_ref.at[:, :, mine],
+                a_send.at[d - 1],
+                a_recv.at[d - 1],
+                (peer, pc.j),
+            )
+        )
+    begin(ends)
+    own = pltpu.make_async_copy(
+        by_slot.at[pl.ds(pc.s * per_group, per_group)], out_ref.at[:, :, mine], o_sem
+    )
+    own.start()
+
+    for copy in table_stage:
+        copy.wait()
+    total = table_ref[pl.ds(pc.s * own_sections, own_sections)]
+    for d in range(pc.groups - 1):
+        total = total + table_in[d]
+    slot = pc.groups - 1
+    for stage, (count, target) in enumerate(((pc.nx, pc.at_x), (pc.nz, pc.at_z))):
+        table_mid[stage] = total
+        copies = []
+        for d in range(1, count):
+            copies.append(
+                (
+                    remote(
+                        table_mid.at[stage],
+                        table_in.at[slot],
+                        t_send.at[slot],
+                        t_recv.at[slot],
+                        target(d),
+                    ),
+                    slot,
+                )
+            )
+            slot += 1
+        begin([copy for copy, _ in copies])
+        for copy, _ in copies:
+            copy.wait()
+        for _, where in copies:
+            total = total + table_in[where]
+    table_out[...] = total
+
+    table_square = jnp.sum(total * total) / pc.batch
+    lane = lax.broadcasted_iota(jnp.int32, (8, 128), 1)
+    part = jnp.where(lane == 0, jnp.sum(square[...]) + table_square, loss_ref[...])
+    sums_out[...] = pc.small_sum(part, sent, landed, m_send, m_recv)
+    for copy in ends:
+        copy.wait()
+    own.wait()
+
+    def finish(b, carry):
+        gone(to_core(b))
+        return carry
+
+    lax.fori_loop(max(blocks - 4, 0), blocks, finish, 0)
+
+    def finish_rest(b, carry):
+        @pl.when(b % 2 == 0)
+        def _():
+            gone(first_x(b))
+            gone(then_y(b))
+            gone(along_z(b, then_a))
+
+        @pl.when(b % 2 == 1)
+        def _():
+            gone(first_y(b))
+            gone(then_x(b))
+            gone(along_z(b, then_b))
+
+        return carry
+
+    lax.fori_loop(0, blocks, finish_rest, 0)
+
+
+def reduce_grads(pc, arrays, sources, table, loss, block_of, per_group):
+    blocks = len(sources)
+    positions = arrays[0].shape[1]
+    width = D // 2
+    rows = width // pc.batch
+    own_sections = SECTIONS // pc.groups
+    hops = max(pc.nx, pc.ny) - 1
+    evens, odds = (blocks + 1) // 2, blocks // 2
+    steps = pc.small_slots()
+    dma = pltpu.SemaphoreType.DMA
+    vmem = pl.BlockSpec(memory_space=pltpu.VMEM)
+    anyspace = pl.BlockSpec(memory_space=pl.ANY)
+    nz, nx, ny, half, panel = pc.nz, pc.nx, pc.ny, pc.half, pc.panel
+    return pl.pallas_call(
+        functools.partial(reduce_kernel, pc, sources),
+        out_shape=(
+            jax.ShapeDtypeStruct((per_group, rows, D), low),
+            jax.ShapeDtypeStruct((own_sections, 8, D), float_out),
+            jax.ShapeDtypeStruct((8, 128), float_out),
+        ),
+        in_specs=[pl.BlockSpec(memory_space=pltpu.SMEM)] + [anyspace] * len(arrays) + [vmem, vmem],
+        out_specs=(vmem, vmem, vmem),
+        scratch_shapes=[
+            pltpu.VMEM((2, positions, width), low),
+            pltpu.VMEM((2, positions, D), low),
+            pltpu.VMEM((2, width, half), float_out),
+            pltpu.VMEM((4, nz, nx, rows, half), low),
+            pltpu.VMEM((blocks, nz, nx, rows, half), low),
+            pltpu.VMEM((evens, nx - 1, nz, rows, half), low),
+            pltpu.VMEM((odds, ny - 1, nz, nx, rows, panel), low),
+            pltpu.VMEM((evens, ny - 1, nz, rows, panel), low),
+            pltpu.VMEM((odds, nx - 1, nz, rows, panel), low),
+            pltpu.VMEM((blocks, nz - 1, rows, panel), low),
+            pltpu.VMEM((blocks + 1, rows, panel), low),
+            pltpu.VMEM((per_group * pc.groups, rows, panel), low),
+            pltpu.VMEM((1, panel), float_out),
+            pltpu.VMEM((steps, own_sections, 8, D), float_out),
+            pltpu.VMEM((2, own_sections, 8, D), float_out),
+            pltpu.VMEM((3, 8, 128), float_out),
+            pltpu.VMEM((steps, 8, 128), float_out),
+            dma((2, 2)),
+            dma((blocks,)),
+            dma((blocks,)),
+            dma((blocks, hops)),
+            dma((blocks, hops)),
+            dma((blocks, hops)),
+            dma((blocks, hops)),
+            dma((blocks, nz - 1)),
+            dma((blocks, nz - 1)),
+            dma((pc.groups - 1,)),
+            dma((pc.groups - 1,)),
+            dma,
+            dma((steps,)),
+            dma((steps,)),
+            dma((steps,)),
+            dma((steps,)),
+        ],
+        name="reduce_grads",
+        compiler_params=pltpu.CompilerParams(
+            collective_id=1, has_side_effects=True, vmem_limit_bytes=56 * MIB
+        ),
+    )(block_of, *arrays, table, loss)
 
 
 def positions(segs):
-    index = jnp.broadcast_to(jnp.arange(segs.shape[-1], dtype=jnp.int32), segs.shape)
-    first = jnp.ones(segs.shape[:-1] + (1,), dtype=bool)
-    change = jnp.concatenate([first, segs[..., 1:] != segs[..., :-1]], axis=-1)
-    starts = lax.cummax(jnp.where(change, index, jnp.zeros_like(index)), axis=segs.ndim - 1)
+    index = jnp.arange(segs.shape[-1], dtype=jnp.int32)
+    same = segs[..., :, None] == segs[..., None, :]
+    starts = jnp.min(jnp.where(same, index, segs.shape[-1]), axis=-1)
     return (index - starts).astype(jnp.float32)
 
 
@@ -68,12 +825,8 @@
     qkv_w = blocks[5:11].reshape(3, width, width)
     out_w = blocks[11:13].reshape(width, width)
     up_w = blocks[13:21].reshape(4, width, width)
-    down_w = blocks[21:29].reshape(4 * width, width)
+    down_w = blocks[21:29].reshape(4, width, width)
     return (code_w, phone_w, head_w, qkv_w, out_w, up_w, down_w)
-
-
-def pack(pieces, half, width):
-    return jnp.concatenate([piece.reshape(-1, half, width) for piece in pieces], axis=0)
 
 
 def attend_scores(queries, key_vecs, same):
@@ -83,7 +836,7 @@
     return jnp.where(same[:, None], scores, -1000000000.0)
 
 
-def forward(matrices, params, phones, codes, segments, section_ids, targets, section_hot):
+def forward(matrices, params, phones, codes, segments, section_ids, targets):
     code_w, phone_w, head_w, qkv_w, out_w, up_w, down_w = matrices
     rows, length = segments.shape
     levels = (jnp.arange(LEVELS)[None, :] <= section_ids[:, None]).astype(jnp.bfloat16)
@@ -116,16 +869,15 @@
     stream = stream + jnp.einsum("rld,de->rle", mixed, out_w, preferred_element_type=float_out)
     normed_two, scale_two = normalize(stream)
     input_two = (normed_two * (1.0 + params[:, 2]) + params[:, 3]).astype(jnp.bfloat16)
-    hidden = jnp.einsum("rld,gde->rlge", input_two, up_w, preferred_element_type=float_out)
-    active = jax.nn.gelu(hidden, approximate=False).astype(jnp.bfloat16).reshape(rows, length, FF)
-    stream = stream + jnp.einsum("rlf,fd->rld", active, down_w, preferred_element_type=float_out)
+    hidden = jnp.einsum("rld,gde->grle", input_two, up_w, preferred_element_type=float_out)
+    active = jax.nn.gelu(hidden, approximate=False).astype(jnp.bfloat16)
+    stream = stream + jnp.einsum("grle,ged->rld", active, down_w, preferred_element_type=float_out)
     normed_three, scale_three = normalize(stream)
     input_three = (normed_three * (1.0 + params[:, 4]) + params[:, 5]).astype(jnp.bfloat16)
     logits = jnp.einsum("rld,dc->rlc", input_three, head_w, preferred_element_type=float_out)
     log_norm = jax.nn.logsumexp(logits, axis=-1)
     target_hot = (targets[:, :, None] == vocab).astype(jnp.float32)
     losses = log_norm - jnp.sum(logits * target_hot, axis=-1)
-    section_loss = jnp.sum(section_hot * jnp.sum(losses, axis=1)[:, None], axis=0)
     kept = (
         multi,
         phone_hot,
@@ -148,7 +900,7 @@
         log_norm,
         target_hot,
     )
-    return (kept, section_loss)
+    return (kept, jnp.sum(losses, axis=1))
 
 
 def backward(matrices, params, kept, row_weight):
@@ -178,24 +930,18 @@
     rows, length = (same.shape[0], same.shape[1])
     predicted = jnp.exp(logits - log_norm[..., None])
     grad_logits = ((predicted - target_hot) * row_weight[:, None, None]).astype(jnp.bfloat16)
-    grad_head = jnp.einsum(
-        "rld,rlc->dc", input_three, grad_logits, preferred_element_type=float_out
-    )
     grad_three = jnp.einsum("rlc,dc->rld", grad_logits, head_w, preferred_element_type=float_out)
     grad_stream, gain_three, shift_three = norm_back(
         grad_three, normed_three, scale_three, params[:, 4]
     )
     grad_ffn = grad_stream.astype(jnp.bfloat16)
-    grad_down = jnp.einsum("rlf,rld->fd", active, grad_ffn, preferred_element_type=float_out)
-    grad_active = jnp.einsum("rld,fd->rlf", grad_ffn, down_w, preferred_element_type=float_out)
+    grad_active = jnp.einsum("rld,ged->grle", grad_ffn, down_w, preferred_element_type=float_out)
     _, gelu_pull = jax.vjp(lambda value: jax.nn.gelu(value, approximate=False), hidden)
-    grad_hidden = gelu_pull(grad_active.reshape(hidden.shape))[0].astype(jnp.bfloat16)
-    grad_up = jnp.einsum("rld,rlge->gde", input_two, grad_hidden, preferred_element_type=float_out)
-    grad_two = jnp.einsum("rlge,gde->rld", grad_hidden, up_w, preferred_element_type=float_out)
+    grad_hidden = gelu_pull(grad_active)[0].astype(jnp.bfloat16)
+    grad_two = jnp.einsum("grle,gde->rld", grad_hidden, up_w, preferred_element_type=float_out)
     grad_norm_two, gain_two, shift_two = norm_back(grad_two, normed_two, scale_two, params[:, 2])
     grad_stream = grad_stream + grad_norm_two
     grad_attn = grad_stream.astype(jnp.bfloat16)
-    grad_out = jnp.einsum("rld,rle->de", mixed, grad_attn, preferred_element_type=float_out)
     grad_mixed = jnp.einsum("rle,de->rld", grad_attn, out_w, preferred_element_type=float_out)
     grad_mixed = grad_mixed.astype(jnp.bfloat16).reshape(rows, length, HEADS, HD)
     scores = attend_scores(heads[0], heads[1], same)
@@ -221,20 +967,40 @@
         .reshape(3, rows, length, D)
         .astype(jnp.bfloat16)
     )
-    grad_proj = jnp.einsum("rld,krle->kde", input_one, grad_qkv, preferred_element_type=float_out)
     grad_one = jnp.einsum("krle,kde->rld", grad_qkv, qkv_w, preferred_element_type=float_out)
     grad_norm_one, gain_one, shift_one = norm_back(grad_one, normed_one, scale_one, params[:, 0])
     grad_embed = (grad_stream + grad_norm_one).astype(jnp.bfloat16)
-    grad_code = jnp.einsum("rlc,rld->cd", multi, grad_embed, preferred_element_type=float_out)
-    grad_phone = jnp.einsum("rlp,rld->pd", phone_hot, grad_embed, preferred_element_type=float_out)
-    half = phone_w.shape[0]
-    block_grads = pack(
-        (grad_code, grad_phone, grad_head, grad_proj, grad_out, grad_up, grad_down), half, D
-    )
     row_grads = jnp.stack(
         [gain_one, shift_one, gain_two, shift_two, gain_three, shift_three], axis=1
     )
-    return (block_grads, row_grads)
+    flat = (-1, rows * length)
+    arrays = [
+        multi.reshape(*flat, CODES),
+        phone_hot.reshape(*flat, PHONES),
+        input_three.reshape(*flat, D),
+        input_one.reshape(*flat, D),
+        mixed.reshape(*flat, D),
+        input_two.reshape(*flat, D),
+        active.reshape(*flat, D),
+        grad_embed.reshape(*flat, D),
+        grad_logits.reshape(*flat, CODES),
+        grad_qkv.reshape(*flat, D),
+        grad_attn.reshape(*flat, D),
+        grad_hidden.reshape(*flat, D),
+        grad_ffn.reshape(*flat, D),
+    ]
+    return arrays, row_grads
+
+
+def block_sources():
+    half = D // 2
+    made = [(0, (0, 0), 7, 0), (0, (0, half), 7, 0), (1, (0, 0), 7, 0)]
+    made += [(2, (0, i * half), 8, 0) for i in range(2)]
+    made += [(3, (0, i * half), 9, k) for k in range(3) for i in range(2)]
+    made += [(4, (0, i * half), 10, 0) for i in range(2)]
+    made += [(5, (0, i * half), 11, g) for g in range(4) for i in range(2)]
+    made += [(6, (g, i * half), 12, 0) for g in range(4) for i in range(2)]
+    return tuple(made)
 
 
 def adam(weight, first, second, grad, rate, step):
@@ -247,6 +1013,7 @@
 
 
 def per_device(
+    pc,
     masters,
     first_moment,
     second_moment,
@@ -261,49 +1028,40 @@
     sections,
     targets,
 ):
-    section_width = lax.axis_size("section")
-    batch_width = lax.axis_size("batch")
     section_ids = sections[:, 0]
     row_count = section_ids.shape[0]
+    own_sections = section_table.shape[0]
     section_hot = (section_ids[:, None] == jnp.arange(SECTIONS)[None, :]).astype(jnp.float32)
     local_counts = jnp.sum(section_hot, axis=0) * segments.shape[1]
-    shard_rows = lax.all_gather(masters.astype(jnp.bfloat16), "batch", axis=1, tiled=True)
-    all_slots = lax.all_gather(shard_rows, "section", axis=0, tiled=True)
-    blocks = jnp.take(all_slots, owners, axis=0)
-    table = lax.all_gather(section_table, "section", axis=0, tiled=True)
+    padded = jnp.pad(section_table.reshape(own_sections, 6, D), ((0, 0), (0, 2), (0, 0)))
+    blocks, table, counts = gather_weights(
+        pc, masters, padded, jnp.broadcast_to(local_counts[:, None], (SECTIONS, 128)), owners
+    )
+    counts = counts[:, 0]
     matrices = unpack(blocks)
-    params = jnp.einsum("rs,sk->rk", section_hot, table, precision=exact).reshape(
-        row_count, 6, 1, D
-    )
-    kept, section_loss = forward(
-        matrices, params, phones, codes, segments, section_ids, targets, section_hot
-    )
-    counts, loss_sums = lax.psum((local_counts, section_loss), ("section", "batch"))
+    params = jnp.einsum(
+        "rs,sk->rk", section_hot, table[:, :6].reshape(SECTIONS, 6 * D), precision=exact
+    ).reshape(row_count, 6, 1, D)
+    kept, row_losses = forward(
+        matrices, params, phones, codes, segments, section_ids, targets
+    )
     row_weight = jnp.sum(section_hot / (SECTIONS * counts)[None, :], axis=1)
-    block_grads, row_grads = backward(matrices, params, kept, row_weight)
+    arrays, row_grads = backward(matrices, params, kept, row_weight)
     table_local = jnp.einsum(
         "rs,rk->sk", section_hot, row_grads.reshape(row_count, 6 * D), precision=exact
     )
-    table_sum = lax.psum(table_local, ("section", "batch"))
-    own_count = section_table.shape[0]
-    table_grad = lax.dynamic_slice_in_dim(
-        table_sum, lax.axis_index("section") * own_count, own_count, 0
-    )
-    per_group = masters.shape[0]
-    piece_rows = masters.shape[1]
-    split_grads = block_grads.reshape(block_grads.shape[0], batch_width, piece_rows, D)
-    group_of = owners // per_group
-    within = owners % per_group
-    target_slot = (
-        (group_of * batch_width)[:, None] * per_group
-        + jnp.arange(batch_width)[None, :] * per_group
-        + within[:, None]
-    )
-    arranged = jnp.zeros((section_width * batch_width * per_group, piece_rows, D), jnp.float32)
-    arranged = arranged.at[target_slot.reshape(-1)].set(split_grads.reshape(-1, piece_rows, D))
-    own_grad = lax.psum_scatter(arranged, ("section", "batch"), scatter_dimension=0, tiled=True)
-    square_sum = jnp.sum(own_grad * own_grad) + jnp.sum(table_grad * table_grad) / batch_width
-    grad_norm = jnp.sqrt(lax.psum(square_sum, ("section", "batch")))
+    table_local = jnp.pad(table_local.reshape(SECTIONS, 6, D), ((0, 0), (0, 2), (0, 0)))
+    loss_part = jnp.broadcast_to(jnp.sum(row_weight * row_losses), (8, 128))
+    slot_ids = jnp.arange(masters.shape[0] * pc.groups)
+    held = owners[None, :] == slot_ids[:, None]
+    block_of = jnp.min(jnp.where(held, jnp.arange(owners.shape[0]), owners.shape[0]), axis=1)
+    own_grad, table_grad, sums = reduce_grads(
+        pc, arrays, block_sources(), table_local, loss_part, block_of, masters.shape[0]
+    )
+    own_grad = own_grad.astype(jnp.float32)
+    table_grad = table_grad[:, :6].reshape(own_sections, 6 * D)
+    grad_norm = jnp.sqrt(sums[0, 0])
+    loss = sums[0, 1]
     clip_factor = jnp.minimum(1.0, clip_limit / grad_norm)
     step = step_count[0].astype(jnp.float32)
     new_masters, new_first, new_second = adam(
@@ -312,7 +1070,6 @@
     new_table, new_table_first, new_table_second = adam(
         section_table, table_first, table_second, table_grad * clip_factor, table_rate, step
     )
-    loss = jnp.sum(loss_sums / (SECTIONS * counts))
     return (
         new_masters,
         new_first,
@@ -327,7 +1084,7 @@
 
 def solution(mesh):
     return jax.shard_map(
-        per_device,
+        functools.partial(per_device, Place(mesh)),
         mesh=mesh,
         in_specs=(
             P("section", "batch", None),

time: 2450 us -> 789 us (0.32)
  waiting for transfers between devices: 1680 us -> 0 us
  Pallas kernels: 0 us -> 335 us
  local copies, waits for them, and re-layouts: 240 us -> 98.9 us
  blocking collectives: 85.5 us -> 0 us
  matrix products: 327 us -> 253 us
    reduce_scatter x1 -> x0, waiting for transfers between devices: 1400 us -> none  [per_device(): lax.psum_scatter(arranged, ('section', 'batch'), scatter_dimension=0, til...]
    pallas_call x0 -> x2, Pallas kernels: none -> 335 us  [the longest x1 168 us: reduce_grads(): pl.pallas_call(functools.partial(reduce_kernel, pc, sources), out_shape=(...]
    all_gather x2 -> x0, waiting for transfers between devices: 280 us -> none  [the longest x1 152 us: per_device(): all_slots = lax.all_gather(shard_rows, 'section', axis=0, tiled=True)]
    scatter x1 -> x0, local copies, waits for them, and re-layouts: 107 us -> none  [per_device(): arranged.at[target_slot.reshape(-1)]]
    psum x2 -> x0, blocking collectives: 78.1 us -> none  [the longest x1 39.4 us: per_device(): grad_norm = jnp.sqrt(lax.psum(square_sum, ('section', 'batch')))]
    dot_general x12 -> x5, matrix products: 172 us -> 101 us  [the longest x1 46.4 us: forward(): jnp.einsum('rld,gde->grle', input_two, up_w, preferred_element_type=float...]
    another operation x3 -> x9, local copies, waits for them, and re-layouts: 10.4 us -> 44.8 us  [backward(): jnp.stack([grad_queries, grad_key_vecs, grad_values])]
    unnamed x247 -> x220, local copies, waits for them, and re-layouts: 37.5 us -> 11.9 us
  transfers between devices with their start and end apart: 4 -> 0, of which waited for: 3 -> 0; matrix products, arithmetic and copies ran while one was open for 8% -> 0% of each run, Pallas kernels for 0% -> 0%
where the time goes in v1:
time: 789 us; the launch traced here: 778 us
  Pallas kernels  335 us (42%)
  matrix products  253 us (32%)
  local copies, waits for them, and re-layouts  98.9 us (13%)
  other arithmetic  86.1 us (11%)
    pallas_call x1, Pallas kernels, reduce_grads(): pl.pallas_call(functools.partial(reduce_kernel, pc, sources), out_shape=(...  168 us
    pallas_call x1, Pallas kernels, gather_weights(): pl.pallas_call(functools.partial(gather_kernel, pc), out_shape=(jax.Shape...  167 us
    dot_general x1, matrix products, forward(): jnp.einsum('rld,gde->grle', input_two, up_w, preferred_element_type=float...  46.4 us
    another operation x9, local copies, waits for them, and re-layouts, backward(): jnp.stack([grad_queries, grad_key_vecs, grad_values])  44.8 us
    convert_element_type x1, other arithmetic, backward(): grad_scores = (probs * (grad_probs - jnp.sum(probs * grad_probs, axis=-1,...  28.1 us
    dot_general x1, matrix products, backward(): jnp.einsum('rlhe,rmhe->rhlm', grad_mixed, heads[2], preferred_element_typ...  25.7 us
    dot_general x1, matrix products, backward(): jnp.einsum('rld,ged->grle', grad_ffn, down_w, preferred_element_type=floa...  22.9 us
    dot_general x1, matrix products, backward(): jnp.einsum('grle,gde->rld', grad_hidden, up_w, preferred_element_type=flo...  16.8 us

profile of v1, /device:TPU:0, one launch (start us, length us, event | category | flops | bytes accessed | tf_op | source)
XLA Modules:
  0.0 778.0 jit_solution(9958748610916925617)
XLA Ops:
  0.6 1.1 fusion.140
  2.6 0.8 convert_reduce_fusion
  3.5 0.8 reshape.792
  4.4 1.6 copy-done
  6.6 167.2 %gather_weights.1 = (bf16[29,4,2,64,1024]{4,3,2,1,0:T(8,128)(2,1)}, f32[8,8,1024]{2,1,0:T(8,128)S(1)}, f32[8,128]{1,0:T(8,128)S(1)}) custom-call(s32[29]{0:T(128)S(1)} %copy-done.2, f32[8,64,1024]{2,1,0:T(8,128)S(1)} %copy-done, f32[2,8,1024]{2,1,0:T(8,128)S(1)} %pad.8.table_ref, f32[8,128]{1,0:T(8,128)S(1)} %broadcast_in_dim.44.counts_ref), custom_call_target="tpu_custom_call" | custom-call | tf_op jit(solution)/shard_map/gather_weights/pallas_call | solution.py:326
  173.8 6.1 fusion.137
  180.0 5.6 fusion.55
  185.6 1.3 slice.146
  187.4 16.3 %fusion.142 = (f32[2,512]{1,0:T(2,128)S(1)}, f32[2,512,1024]{2,1,0:T(8,128)S(1)}) fusion(f32[1024]{0:T(1024)S(1)} %fusion.116, f32[2,512]{1,0:T(2,128)S(1)} %subtract_convert_fusion, pred[1024]{0:T(1024)(128)(4,1)S(1)} %fusion.110, f32[2,512,1024]{2,1,0:T(8,128)S(1)} %fusion.55, bf16[512,1024,1]{1,0,2:T(8,128)(2,1)S(1)} %bitcast.367, ...), kind=kOutput, calls=%fused_computation.277 | convolution fusion | flops 1080556544 | bytes 9454592 | tf_op jit(solution)/shard_map/rlp,pd->rld/dot_general | solution.py:853
  203.7 0.9 multiply_reduce_fusion.7
  205.7 0.7 add_convert_fusion.3
  206.4 4.3 slice.147
  210.7 2.5 copy-done.30
  213.3 7.2 convert_bitcast_fusion
  221.3 13.8 %fusion = (f32[2,16,512]{2,1,0:T(8,128)S(1)}, f32[2,16,512,512]{2,3,1,0:T(8,128)}) fusion(pred[2,512,512]{1,2,0:T(8,128)(4,1)S(1)} %broadcast_compare_fusion, bf16[2,512,16,64]{1,3,2,0:T(8,128)(2,1)S(1)} %bitcast.337, bf16[2,512,16,64]{1,3,2,0:T(8,128)(2,1)S(1)} %bitcast.333), kind=kOutput, calls=%fused_computation.5 | convolution fusion | flops 1098891264 | bytes 38338560 | tf_op jit(solution)/shard_map/rlhe,rmhe->rhlm/dot_general | solution.py:833
  235.1 14.1 %exponential_reduce_fusion = f32[2,16,512]{2,1,0:T(8,128)S(1)} fusion(f32[2,16,512,512]{2,3,1,0:T(8,128)} %get-tuple-element.81, f32[2,16,512]{2,1,0:T(8,128)S(1)} %is-finite_select_fusion, pred[2,512,512]{1,2,0:T(8,128)(4,1)S(1)} %broadcast_compare_fusion), kind=kLoop, calls=%fused_computation.3 | loop fusion | flops 33538048 | bytes 34209792 | tf_op jit(solution)/shard_map/reduce_sum | solution.py:865
  249.3 15.7 %convolution_convert_fusion.2 = bf16[2,16,64,512]{3,2,1,0:T(8,128)(2,1)} fusion(bf16[2,512,16,64]{1,3,2,0:T(8,128)(2,1)S(1)} %bitcast.341, f32[2,16,512,512]{2,3,1,0:T(8,128)} %get-tuple-element.81, f32[2,16,512]{2,1,0:T(8,128)S(1)} %log_add_fusion, pred[2,512,512]{1,2,0:T(8,128)(4,1)S(1)} %broadcast_compare_fusion), kind=kOutput, calls=%fused_computation.156 | convolution fusion | flops 1108344832 | bytes 38338560 | tf_op jit(solution)/shard_map/rhlm,rmhe->rlhe/dot_general | solution.py:867
  265.0 5.9 fusion.143
  271.5 0.8 add_convert_fusion.2
  272.4 10.5 %fusion.138 = (bf16[8,4,2,64,1024]{4,3,2,1,0:T(8,128)(2,1)}, bf16[8,4,2,64,1024]{4,3,2,1,0:T(8,128)(2,1)S(1)}) fusion(bf16[29,4,2,64,1024]{4,3,2,1,0:T(8,128)(2,1)} %get-tuple-element.14), kind=kLoop, calls=%fused_computation.273 | loop fusion | bytes 33554432 | tf_op jit(solution)/shard_map/slice | solution.py:828
  282.8 46.4 %fusion.11 = (bf16[4,2,512,1024]{3,2,1,0:T(8,128)(2,1)S(1)}, f32[4,2,512,1024]{3,2,1,0:T(8,128)}, f32[4,1024,2,512]{1,3,2,0:T(8,128)}) fusion(bf16[4,1024,1024,1]{2,1,3,0:T(8,128)(2,1)S(1)} %bitcast.354, bf16[2,512,1024]{2,1,0:T(8,128)(2,1)S(1)} %add_convert_fusion.2), kind=kOutput, calls=%fused_computation.24 | convolution fusion | flops 8862564352 | bytes 52428800 | tf_op jit(solution)/shard_map/rld,gde->grle/dot_general | solution.py:872
  329.3 14.3 %fusion.144 = (f32[2,512]{1,0:T(2,128)S(1)}, f32[2,512,1024]{2,1,0:T(8,128)S(1)}) fusion(f32[2,512,1024]{2,1,0:T(8,128)S(1)} %get-tuple-element.83, bf16[4,2,512,1024]{3,2,1,0:T(8,128)(2,1)S(1)} %get-tuple-element.44, bf16[4,1024,1024,1]{2,1,3,0:T(8,128)(2,1)} %bitcast.356), kind=kOutput, calls=%fused_computation.279 | convolution fusion | flops 8592030720 | bytes 25169920 | tf_op jit(solution)/shard_map/grle,ged->rld/dot_general | solution.py:874
  344.4 0.7 add_convert_fusion.1
  345.2 2.2 copy-done.34
  347.4 2.4 fusion.145
  349.8 1.6 select_reduce_fusion
  352.9 1.3 multiply_convert_fusion.3
  354.2 3.5 multiply_reduce_fusion.1
  357.8 1.3 fusion.100
  359.7 22.9 %fusion.8 = bf16[4,2,512,1024]{3,2,1,0:T(8,128)(2,1)} fusion(f32[4,2,512,1024]{3,2,1,0:T(8,128)} %get-tuple-element.45, bf16[4,1024,1024,1]{2,1,3,0:T(8,128)(2,1)} %bitcast.357, f32[4,1024,2,512]{1,3,2,0:T(8,128)} %get-tuple-element.84, bf16[2,512,1024]{2,1,0:T(8,128)(2,1)S(1)} %fusion.100), kind=kOutput, calls=%fused_computation.16 | convolution fusion | flops 8648654848 | bytes 52428800 | tf_op jit(solution)/shard_map/rld,ged->grle/dot_general | solution.py:938
  382.7 16.8 %fusion.34 = (f32[2,1024]{1,0:T(2,128)S(1)}, f32[2,512]{1,0:T(2,128)S(1)}, f32[2,512]{1,0:T(2,128)S(1)}, f32[2,1024]{1,0:T(2,128)S(1)}, f32[2,512,1024,1]{2,1,0,3:T(8,128)}) fusion(f32[2,512,1024]{2,1,0:T(8,128)} %copy-done.6, f32[2,512]{1,0:T(2,128)S(1)} %copy-done.51, f32[2,512]{1,0:T(2,128)S(1)} %copy-done.45, f32[2,1024]{1,0:T(2,128)S(1)} %copy-done.40, ...), kind=kOutput, calls=%fused_computation.58 | convolution fusion | flops 8599365632 | bytes 25206784 | tf_op jit(solution)/shard_map/grle,gde->rld/dot_general | solution.py:941
  399.5 6.1 fusion.135
  405.6 1.3 copy-done.20
  407.0 3.7 convolution_convert_fusion.1
  410.7 2.9 copy.69
  413.6 25.7 %multiply_reduce_fusion = (f32[2,16,512]{2,1,0:T(8,128)S(1)}, f32[2,16,512,512]{2,3,1,0:T(8,128)}) fusion(f32[2,16,512,512]{2,3,1,0:T(8,128)} %get-tuple-element.81, f32[2,16,512]{2,1,0:T(8,128)S(1)} %copy-done.36, pred[2,512,512]{1,2,0:T(8,128)(4,1)S(1)} %copy-done.12, bf16[2,512,16,64]{1,3,2,0:T(8,128)(2,1)S(1)} %bitcast.339, ...), kind=kOutput, calls=%fused_computation.1 | convolution fusion | flops 1115668480 | bytes 71958528 | tf_op jit(solution)/shard_map/rlhe,rmhe->rhlm/dot_general | solution.py:953
  439.3 28.1 %multiply_convert_fusion = bf16[2,16,512,512]{2,3,1,0:T(8,128)(2,1)} fusion(f32[2,16,512,512]{2,3,1,0:T(8,128)} %get-tuple-element.92, f32[2,16,512,512]{2,3,1,0:T(8,128)} %get-tuple-element.81, f32[2,16,512]{2,1,0:T(8,128)S(1)} %get-tuple-element.91, f32[2,16,512]{2,1,0:T(8,128)S(1)} %copy-done.36, pred[2,512,512]{1,2,0:T(8,128)(4,1)S(1)} %copy-done.12), kind=kLoop, calls=%fused_computation | loop fusion | flops 50331648 | bytes 84541440 | tf_op jit(solution)/shard_map/convert_element_type | solution.py:958
  467.4 9.2 %multiply_convert_fusion.2 = bf16[2,16,64,512]{3,2,1,0:T(8,128)(2,1)S(1)} fusion(bf16[2,512,16,64]{1,3,2,0:T(8,128)(2,1)} %bitcast.334, bf16[2,16,512,512]{2,3,1,0:T(8,128)(2,1)} %multiply_convert_fusion), kind=kOutput, calls=%fused_computation.65 | convolution fusion | flops 1075838976 | bytes 20971520 | tf_op jit(solution)/shard_map/rhlm,rmhe->rlhe/dot_general | solution.py:959
  476.6 2.5 copy.73
  479.1 12.8 %multiply_convert_fusion.1 = bf16[2,16,64,512]{3,2,1,0:T(8,128)(2,1)} fusion(bf16[2,512,16,64]{1,3,2,0:T(8,128)(2,1)} %bitcast.338, bf16[2,16,512,512]{2,3,1,0:T(8,128)(2,1)} %multiply_convert_fusion), kind=kOutput, calls=%fused_computation.64 | convolution fusion | flops 1075838976 | bytes 20971520 | tf_op jit(solution)/shard_map/rhlm,rlhe->rmhe/dot_general | solution.py:962
  492.0 3.9 copy.74
  495.9 16.1 %convolution_convert_fusion = bf16[2,16,64,512]{3,2,1,0:T(8,128)(2,1)} fusion(bf16[2,512,16,64]{1,3,2,0:T(8,128)(2,1)} %bitcast.340, f32[2,16,512,512]{2,3,1,0:T(8,128)} %get-tuple-element.81, f32[2,16,512]{2,1,0:T(8,128)S(1)} %copy-done.36, pred[2,512,512]{1,2,0:T(8,128)(4,1)S(1)} %copy-done.12), kind=kOutput, calls=%fused_computation.154 | convolution fusion | flops 1108344832 | bytes 38338560 | tf_op jit(solution)/shard_map/rhlm,rlhe->rmhe/dot_general | solution.py:950
  512.1 3.9 copy.75
  516.1 13.8 %fusion.33 = (f32[2,1024]{1,0:T(2,128)S(1)}, f32[2,512]{1,0:T(2,128)S(1)}, f32[2,512]{1,0:T(2,128)S(1)}, f32[2,1024]{1,0:T(2,128)S(1)}, f32[2,512,1024,1]{2,1,3,0:T(8,128)}) fusion(f32[2,512,1024]{2,1,0:T(8,128)} %copy-done.8, f32[2,512]{1,0:T(2,128)S(1)} %copy-done.69, f32[2,512]{1,0:T(2,128)S(1)} %copy-done.47, f32[2,1024]{1,0:T(2,128)S(1)} %copy-done.42, ...), kind=kOutput, calls=%fused_computation.54 | convolution fusion | flops 6458173440 | bytes 21012480 | tf_op jit(solution)/shard_map/krle,kde->rld/dot_general | solution.py:970
  530.3 0.7 pad.9.refs_14_
  531.0 4.7 copy.100
  535.8 6.7 reshape.830
  542.4 4.7 copy.101
  547.2 6.7 reshape.831
  553.8 4.7 copy.102
  558.6 6.8 reshape.832
  565.4 6.9 pad_maximum_fusion.refs_10_
  572.4 1.2 copy-done.31
  573.6 2.3 add_convert_fusion
  576.6 1.2 broadcast_in_dim.52.refs_15_
  577.8 4.8 copy.99
  582.8 6.5 reshape.829.refs_5_
  589.8 5.8 fusion.70.refs_1_
  595.6 1.2 fusion.89.refs_2_
  597.4 168.0 %reduce_grads.1 = (bf16[8,64,1024]{2,1,0:T(8,128)(2,1)}, f32[2,8,1024]{2,1,0:T(8,128)}, f32[8,128]{1,0:T(8,128)}) custom-call(s32[32]{0:T(128)} %select_reduce_fusion.2.refs_0_, bf16[1,1024,1024]{2,1,0:T(8,128)(2,1)} %fusion.70.refs_1_, bf16[1,1024,512]{2,1,0:T(8,128)(2,1)} %fusion.89.refs_2_, bf16[1,1024,1024]{2,1,0:T(8,128)(2,1)} %bitcast.346, ...), custom_call_target="tpu_custom_call" | custom-call | tf_op jit(solution)/shard_map/reduce_grads/pallas_call | solution.py:738
  765.5 1.3 fusion.141
  767.5 0.8 multiply_bitcast_fusion
  769.2 0.8 multiply_subtract_fusion.1
  770.0 6.4 multiply_subtract_fusion
  (253 shorter events, 9.5 us)
Async XLA Ops:
  2.5 177.4 %copy-start.79 = (bf16[2]{0:T(256)(128)(2,1)}, bf16[2]{0:T(256)(128)(2,1)S(1)}, u32[]{:S(2)}) copy-start(bf16[2]{0:T(256)(128)(2,1)S(1)} %get-tuple-element.71) | copy-start | bytes 16
  2.5 177.4 %copy-start.81 = (bf16[2]{0:T(256)(128)(2,1)}, bf16[2]{0:T(256)(128)(2,1)S(1)}, u32[]{:S(2)}) copy-start(bf16[2]{0:T(256)(128)(2,1)S(1)} %get-tuple-element.72) | copy-start | bytes 16
  2.6 177.4 %copy-start.83 = (bf16[2]{0:T(256)(128)(2,1)}, bf16[2]{0:T(256)(128)(2,1)S(1)}, u32[]{:S(2)}) copy-start(bf16[2]{0:T(256)(128)(2,1)S(1)} %get-tuple-element.73) | copy-start | bytes 16
  2.6 177.4 %copy-start.85 = (bf16[2]{0:T(256)(128)(2,1)}, bf16[2]{0:T(256)(128)(2,1)S(1)}, u32[]{:S(2)}) copy-start(bf16[2]{0:T(256)(128)(2,1)S(1)} %get-tuple-element.74) | copy-start | bytes 16
  2.6 177.4 %copy-start.87 = (bf16[2]{0:T(256)(128)(2,1)}, bf16[2]{0:T(256)(128)(2,1)S(1)}, u32[]{:S(2)}) copy-start(bf16[2]{0:T(256)(128)(2,1)S(1)} %get-tuple-element.75) | copy-start | bytes 16
  2.6 177.4 %copy-start.89 = (bf16[2]{0:T(256)(128)(2,1)}, bf16[2]{0:T(256)(128)(2,1)S(1)}, u32[]{:S(2)}) copy-start(bf16[2]{0:T(256)(128)(2,1)S(1)} %get-tuple-element.76) | copy-start | bytes 16
  2.6 177.4 %copy-start.91 = (bf16[2]{0:T(256)(128)(2,1)}, bf16[2]{0:T(256)(128)(2,1)S(1)}, u32[]{:S(2)}) copy-start(bf16[2]{0:T(256)(128)(2,1)S(1)} %get-tuple-element.70) | copy-start | bytes 16
  2.6 177.4 %copy-start.93 = (bf16[2]{0:T(256)(128)(2,1)}, bf16[2]{0:T(256)(128)(2,1)S(1)}, u32[]{:S(2)}) copy-start(bf16[2]{0:T(256)(128)(2,1)S(1)} %get-tuple-element.77) | copy-start | bytes 16
  180.0 6.9 copy-start.43
  180.0 7.3 copy-start.77
  204.6 6.1 copy-start.68
  205.7 5.0 copy-start.41
  205.7 65.8 %copy-start.39 = (f32[2,1024]{1,0:T(2,128)}, f32[2,1024]{1,0:T(2,128)S(1)}, u32[]{:S(2)}) copy-start(f32[2,1024]{1,0:T(2,128)S(1)} %get-tuple-element.57) | copy-start | bytes 24580
  220.9 14.2 %copy-start.10 = (bf16[1,2,512,1024]{2,3,1,0:T(8,128)(2,1)}, bf16[1,2,512,1024]{2,3,1,0:T(8,128)(2,1)S(1)}, u32[]{:S(2)}) copy-start(bf16[1,2,512,1024]{2,3,1,0:T(8,128)(2,1)S(1)} %get-tuple-element.51) | copy-start | bytes 6291460
  220.9 14.2 %copy-start.14 = (bf16[1,2,512,1024]{2,3,1,0:T(8,128)(2,1)}, bf16[1,2,512,1024]{2,3,1,0:T(8,128)(2,1)S(1)}, u32[]{:S(2)}) copy-start(bf16[1,2,512,1024]{2,3,1,0:T(8,128)(2,1)S(1)} %get-tuple-element.52) | copy-start | bytes 6291460
  220.9 28.4 %copy-start.16 = (bf16[1,2,512,1024]{2,3,1,0:T(8,128)(2,1)}, bf16[1,2,512,1024]{2,3,1,0:T(8,128)(2,1)S(1)}, u32[]{:S(2)}) copy-start(bf16[1,2,512,1024]{2,3,1,0:T(8,128)(2,1)S(1)} %get-tuple-element.53) | copy-start | bytes 6291460
  221.3 28.0 %copy-start.11 = (pred[2,512,512]{1,2,0:T(8,128)(4,1)}, pred[2,512,512]{1,2,0:T(8,128)(4,1)S(1)}, u32[]{:S(2)}) copy-start(pred[2,512,512]{1,2,0:T(8,128)(4,1)S(1)} %broadcast_compare_fusion) | copy-start | bytes 1572868
  249.3 15.7 %copy-start.35 = (f32[2,16,512]{2,1,0:T(8,128)}, f32[2,16,512]{2,1,0:T(8,128)S(1)}, u32[]{:S(2)}) copy-start(f32[2,16,512]{2,1,0:T(8,128)S(1)} %log_add_fusion) | copy-start | bytes 196612
  270.9 58.4 %copy-start.6 = (f32[2,512,1024]{2,1,0:T(8,128)}, f32[2,512,1024]{2,1,0:T(8,128)S(1)}, u32[]{:S(2)}) copy-start(f32[2,512,1024]{2,1,0:T(8,128)S(1)} %get-tuple-element.83) | copy-start | bytes 12582916
  271.5 11.3 %copy-start.50 = (f32[2,512]{1,0:T(2,128)}, f32[2,512]{1,0:T(2,128)S(1)}, u32[]{:S(2)}) copy-start(f32[2,512]{1,0:T(2,128)S(1)} %add_rsqrt_fusion.1) | copy-start | bytes 12292
  272.4 10.5 %copy-start.22 = (bf16[2,512,1024]{2,1,0:T(8,128)(2,1)}, bf16[2,512,1024]{2,1,0:T(8,128)(2,1)S(1)}, u32[]{:S(2)}) copy-start(bf16[2,512,1024]{2,1,0:T(8,128)(2,1)S(1)} %add_convert_fusion.2) | copy-start | bytes 6291460
  282.8 46.4 %copy-start.29 = (bf16[8,4,2,64,1024]{4,3,2,1,0:T(8,128)(2,1)}, bf16[8,4,2,64,1024]{4,3,2,1,0:T(8,128)(2,1)S(1)}, u32[]{:S(2)}) copy-start(bf16[8,4,2,64,1024]{4,3,2,1,0:T(8,128)(2,1)S(1)} %get-tuple-element.50) | copy-start | bytes 25165828
  329.3 14.4 %copy-start.28 = (bf16[4,2,512,1024]{3,2,1,0:T(8,128)(2,1)}, bf16[4,2,512,1024]{3,2,1,0:T(8,128)(2,1)S(1)}, u32[]{:S(2)}) copy-start(bf16[4,2,512,1024]{3,2,1,0:T(8,128)(2,1)S(1)} %get-tuple-element.44) | copy-start | bytes 25165828
  343.7 14.1 %copy-start.4 = (f32[2,512,1024]{2,1,0:T(8,128)}, f32[2,512,1024]{2,1,0:T(8,128)S(1)}, u32[]{:S(2)}) copy-start(f32[2,512,1024]{2,1,0:T(8,128)S(1)} %get-tuple-element.86) | copy-start | bytes 12582916
  359.7 22.9 %copy-start.26 = (bf16[2,512,1024]{2,1,0:T(8,128)(2,1)}, bf16[2,512,1024]{2,1,0:T(8,128)(2,1)S(1)}, u32[]{:S(2)}) copy-start(bf16[2,512,1024]{2,1,0:T(8,128)(2,1)S(1)} %fusion.100) | copy-start | bytes 6291460
  359.7 22.9 %copy-start.40 = (f32[2,1024]{1,0:T(2,128)S(1)}, f32[2,1024]{1,0:T(2,128)}, u32[]{:S(2)}) copy-start(f32[2,1024]{1,0:T(2,128)} %copy-done.39) | copy-start | bytes 24580
  359.7 23.0 %copy-start.45 = (f32[2,512]{1,0:T(2,128)S(1)}, f32[2,512]{1,0:T(2,128)}, u32[]{:S(2)}) copy-start(f32[2,512]{1,0:T(2,128)} %copy-done.44) | copy-start | bytes 12292
  359.7 23.0 %copy-start.51 = (f32[2,512]{1,0:T(2,128)S(1)}, f32[2,512]{1,0:T(2,128)}, u32[]{:S(2)}) copy-start(f32[2,512]{1,0:T(2,128)} %copy-done.50) | copy-start | bytes 12292
  382.7 16.8 %copy-start.5 = (f32[2,512,1024]{2,1,0:T(8,128)S(1)}, f32[2,512,1024]{2,1,0:T(8,128)}, u32[]{:S(2)}) copy-start(f32[2,512,1024]{2,1,0:T(8,128)} %copy-done.4) | copy-start | bytes 12582916
  382.7 16.8 %copy-start.7 = (f32[2,512,1024]{2,1,0:T(8,128)S(1)}, f32[2,512,1024]{2,1,0:T(8,128)}, u32[]{:S(2)}) copy-start(f32[2,512,1024]{2,1,0:T(8,128)} %copy-done.6) | copy-start | bytes 12582916
  382.7 16.8 %copy-start.18 = (f32[2,512,1024]{2,1,0:T(8,128)S(1)}, f32[2,512,1024]{2,1,0:T(8,128)}, u32[]{:S(2)}) copy-start(f32[2,512,1024]{2,1,0:T(8,128)} %copy-done.17) | copy-start | bytes 12582916
  399.5 7.5 copy-start.33
  413.6 25.7 %copy-start.15 = (bf16[2,512,1024]{1,2,0:T(8,128)(2,1)}, bf16[2,512,1024]{1,2,0:T(8,128)(2,1)S(1)}, u32[]{:S(2)}) copy-start(bf16[2,512,1024]{1,2,0:T(8,128)(2,1)S(1)} %copy.69) | copy-start | bytes 6291460
  516.0 13.9 %copy-start.73 = (f32[2,1024]{1,0:T(2,128)S(1)}, f32[2,1024]{1,0:T(2,128)}, u32[]{:S(2)}) copy-start(f32[2,1024]{1,0:T(2,128)} %get-tuple-element.20) | copy-start | bytes 24580
  516.0 13.9 %copy-start.72 = (f32[2,1024]{1,0:T(2,128)S(1)}, f32[2,1024]{1,0:T(2,128)}, u32[]{:S(2)}) copy-start(f32[2,1024]{1,0:T(2,128)} %get-tuple-element.31) | copy-start | bytes 24580
  516.1 13.9 %copy-start.76 = (s32[2,1]{0,1:T(1,128)S(1)}, s32[2,1]{0,1:T(1,128)}, u32[]{:S(2)}) copy-start(s32[2,1]{0,1:T(1,128)} %param.24) | copy-start | bytes 28
  535.8 6.7 copy-start.13
  547.2 6.7 copy-start.25
  558.6 6.9 copy-start.27
  565.4 7.0 copy-start.9
  565.4 7.0 copy-start.19
  565.4 8.2 %copy-start.31 = (f32[2,512,1024,1]{2,1,3,0:T(8,128)S(1)}, f32[2,512,1024,1]{2,1,3,0:T(8,128)}, u32[]{:S(2)}) copy-start(f32[2,512,1024,1]{2,1,3,0:T(8,128)} %get-tuple-element.93) | copy-start | bytes 12582916
  582.6 6.7 copy-start.92
  582.6 6.7 copy-start.94
  582.6 6.7 copy-start.88
  582.6 6.8 copy-start.90
  582.7 6.8 copy-start.84
  582.7 6.8 copy-start.86
  582.7 6.9 copy-start.80
  582.7 6.9 copy-start.82
  582.7 7.0 copy-start.53
  582.7 7.0 copy-start.55
  582.7 7.0 copy-start.57
  582.7 7.0 copy-start.59
  582.7 7.0 copy-start.61
  582.7 7.0 copy-start.63
  582.8 7.0 copy-start.65
  582.8 7.0 copy-start.67
  582.8 12.8 %copy-start.78 = (s32[2,512]{1,0:T(2,128)S(1)}, s32[2,512]{1,0:T(2,128)}, u32[]{:S(2)}) copy-start(s32[2,512]{1,0:T(2,128)} %param.21) | copy-start | bytes 12292
  582.8 14.0 %copy-start.3 = (s32[29]{0:T(128)S(1)}, s32[29]{0:T(128)}, u32[]{:S(2)}) copy-start(s32[29]{0:T(128)} %owners_ref.1) | copy-start | bytes 352
  597.4 171.8 %copy-start.37 = (f32[2,6144]{1,0:T(2,128)S(1)}, f32[2,6144]{1,0:T(2,128)}, u32[]{:S(2)}) copy-start(f32[2,6144]{1,0:T(2,128)} %param.16) | copy-start | bytes 147460
  597.4 171.8 %copy-start.48 = (f32[2,6144]{1,0:T(2,128)S(1)}, f32[2,6144]{1,0:T(2,128)}, u32[]{:S(2)}) copy-start(f32[2,6144]{1,0:T(2,128)} %param.18) | copy-start | bytes 147460
  597.4 171.8 %copy-start.49 = (f32[2,6144]{1,0:T(2,128)S(1)}, f32[2,6144]{1,0:T(2,128)}, u32[]{:S(2)}) copy-start(f32[2,6144]{1,0:T(2,128)} %param.17) | copy-start | bytes 147460
  597.4 172.6 %copy-start.1 = (f32[8,64,1024]{2,1,0:T(8,128)S(1)}, f32[8,64,1024]{2,1,0:T(8,128)}, u32[]{:S(2)}) copy-start(f32[8,64,1024]{2,1,0:T(8,128)} %masters_ref.1) | copy-start | bytes 6291460
  (34 other events, 77.8 us)

commit v2 on v0

v2 whole, which is shorter than its diff:
```python
import functools
import math

import jax
import jax.numpy as jnp
import numpy as np
from jax import lax
from jax.experimental import pallas as pl
from jax.experimental.pallas import tpu as pltpu
from jax.sharding import PartitionSpec as P

D = 1024
HEADS = 16
HD = 64
CODES = 1024
LEVELS = 8
PHONES = 512
SECTIONS = 8
CORES = 2

clip_limit = 0.002
learn_rate = 0.02
table_rate = 0.1
beta_one = 0.9
beta_two = 0.95
adam_eps = 1e-08
decay_rate = 0.1
norm_eps = 1e-05
pos_scale = 0.1
float_out = jnp.float32
low = jnp.bfloat16
MESH = pl.DeviceIdType.MESH
MIB = 1 << 20


class Place:
    def __init__(self, mesh):
        self.groups = mesh.shape["section"]
        self.batch = mesh.shape["batch"]
        self.ny = self.groups // CORES
        self.nx = 1 << (int(math.log2(self.batch)) // 2)
        self.nz = self.batch // self.nx
        self.panel = D // self.groups
        self.half = D // CORES

    def here(self):
        self.s = lax.axis_index("section")
        self.j = lax.axis_index("batch")
        self.y = lax.div(self.s, CORES)
        self.c = lax.rem(self.s, CORES)
        self.z = lax.div(self.j, self.nx)
        self.x = lax.rem(self.j, self.nx)
        self.sections = [lax.rem(self.s + d, self.groups) for d in range(self.groups)]
        self.xs = [lax.rem(self.x + d, self.nx) for d in range(self.nx)]
        self.ys = [lax.rem(self.y + d, self.ny) for d in range(self.ny)]
        self.zs = [lax.rem(self.z + d, self.nz) for d in range(self.nz)]
        self.x_peers = [(self.s, self.z * self.nx + x) for x in self.xs]
        self.y_peers = [(y * CORES + self.c, self.j) for y in self.ys]
        self.z_peers = [(self.s, z * self.nx + self.x) for z in self.zs]
        self.core_peer = (self.y * CORES + (1 - self.c), self.j)

    def panel_of(self, s):
        return lax.rem(s, CORES) * self.ny + lax.div(s, CORES)

    def section_peer(self, d):
        return self.sections[d]

    def x_of(self, d):
        return self.xs[d]

    def y_of(self, d):
        return self.ys[d]

    def z_of(self, d):
        return self.zs[d]

    def at_x(self, d):
        return self.x_peers[d]

    def at_y(self, d):
        return self.y_peers[d]

    def at_z(self, d):
        return self.z_peers[d]

    def at_core(self):
        return self.core_peer

    def columns(self, index, width):
        return pl.ds(pl.multiple_of(index * width, width), width)

    def near_peers(self):
        return [
            (self.sections[d], self.z * self.nx + self.xs[e])
            for d in range(self.groups)
            for e in range(self.nx)
            if d or e
        ]

    def barrier(self):
        sem = pltpu.get_barrier_semaphore()
        peers = self.near_peers() + [self.at_z(d) for d in range(1, self.nz)]
        for peer in peers:
            pl.semaphore_signal(sem, inc=1, device_id=peer, device_id_type=MESH)
        pl.semaphore_wait(sem, len(peers))

    def small_slots(self):
        return (self.groups * self.nx - 1) + (self.nz - 1)

    def table_slots(self):
        return (self.groups - 1) + (self.nx - 1) + (self.nz - 1)

    def small_stages(self, held, sent, landed, send_sem, recv_sem):
        near = self.near_peers()
        far = [self.at_z(d) for d in range(1, self.nz)]

        def stage(number, peers, first):
            copies = [
                remote(
                    sent.at[number],
                    landed.at[first + n],
                    send_sem.at[first + n],
                    recv_sem.at[first + n],
                    peer,
                )
                for n, peer in enumerate(peers)
            ]

            def start():
                sent[number] = held[...]
                for copy in copies:
                    copy.start()

            def end():
                for copy in copies:
                    copy.wait()
                total = held[...]
                for n in range(len(peers)):
                    total = total + landed[first + n]
                held[...] = total

            return start, end

        return [stage(0, near, 0), stage(1, far, len(near))]


def remote(src, dst, send_sem, recv_sem, device):
    return pltpu.make_async_remote_copy(
        src_ref=src,
        dst_ref=dst,
        send_sem=send_sem,
        recv_sem=recv_sem,
        device_id=device,
        device_id_type=MESH,
    )


ROWS_AT_ONCE = 256
BLOCKS = 29
CODE, PHONE, QKV, OUT, UP, DOWN, HEAD = 0, 2, 3, 9, 11, 19, 27
FRONT = 9
OUTWARD = (0, 1, 2, 5, 6, 7, 8, 9, 10, 11, 12, *range(13, 29), 3, 4)
HOMEWARD = (3, 4, *range(21, 29), *range(13, 21), 11, 12, 5, 6, 7, 8, 9, 10, 0, 1, 2)


def begin(copies):
    for copy in copies:
        copy.start()


def landed_all(copies):
    for copy in copies:
        copy.wait_recv()


def gone(copies):
    for copy in copies:
        copy.wait_send()


LONG_EVERY = 7
LONG_OUT, LONG_HOME = 3, 1
LONGS = len(range(LONG_HOME, BLOCKS, LONG_EVERY))
NEARS = BLOCKS - LONGS


def place_among(b):
    return b - lax.div(b + (LONG_EVERY - 1 - LONG_HOME), LONG_EVERY)


def by_kind(b, at, near=None, far=None):
    long = lax.rem(b, LONG_EVERY) == at
    if near is not None:
        pl.when(jnp.logical_not(long))(near)
    if far is not None:
        pl.when(long)(far)


def rank_cuts(per_group):
    return sorted({0, min(2, per_group), min(4, per_group), per_group})


def rank_keys(owners_ref, order, per_group, groups):
    seen = [jnp.int32(0)] * groups
    keys = []
    for b in order:
        section = jnp.clip(lax.div(owners_ref[b], per_group), 0, groups - 1)
        rank = jnp.int32(0)
        for g in range(groups):
            rank = jnp.where(section == g, seen[g], rank)
            seen[g] = seen[g] + jnp.where(section == g, 1, 0)
        keys.append(section * per_group + jnp.minimum(rank, per_group - 1))
    return keys


def within(value, count):
    return (value >= 0) & (value < count)


def times(a, b):
    return lax.dot_general(a, b, (((1,), (0,)), ((), ())), preferred_element_type=float_out)


def times_t(a, b):
    return lax.dot_general(a, b, (((1,), (1,)), ((), ())), preferred_element_type=float_out)


def turned_times(a, b):
    return lax.dot_general(a, b, (((0,), (0,)), ((), ())), preferred_element_type=float_out)


def normalize(stream):
    centred = stream - jnp.mean(stream, axis=-1, keepdims=True)
    scale = lax.rsqrt(jnp.mean(centred * centred, axis=-1, keepdims=True) + norm_eps)
    return (centred * scale, scale)


def norm_back(grad, normed, scale, gain):
    inner = grad * (1.0 + gain)
    result = scale * (
        inner
        - jnp.mean(inner, axis=-1, keepdims=True)
        - normed * jnp.mean(inner * normed, axis=-1, keepdims=True)
    )
    return (
        result,
        jnp.sum(grad * normed, axis=0, keepdims=True),
        jnp.sum(grad, axis=0, keepdims=True),
    )


def rates():
    column = np.arange(D)
    return column, np.exp(-(2 * (column // 2)) * (math.log(10000.0) / D))


def index_waves(length):
    column, rate = rates()
    angle = np.arange(length)[:, None] * rate
    sine, cosine = np.sin(angle), np.cos(angle)
    even = column % 2 == 0
    same = pos_scale * np.where(even, sine, cosine)
    other = pos_scale * np.where(even, cosine, sine)
    return jnp.asarray(same, jnp.float32), jnp.asarray(other, jnp.float32)


def column_of(row):
    wide = jnp.broadcast_to(row.astype(float_out), (128, row.shape[1]))
    return wide.T[:, :1].astype(jnp.int32)


def masks():
    lane = lax.broadcasted_iota(jnp.int32, (1, 2 * HD), 1)
    return [(lane // HD == h).astype(low) for h in range(2)]


def in_turn(items, first, middle, last):
    ahead, behind = first(*items[0]), None
    for n, item in enumerate(items):
        now = ahead
        if n + 1 < len(items):
            ahead = first(*items[n + 1])
        made = middle(*item, *now)
        if behind is not None:
            last(*behind)
        behind = (*item, *made)
    last(*behind)


def attend_pairs(same, heads):
    turned = [v.astype(float_out).T.astype(low) for _, _, v in heads]
    outs = [[] for _ in heads]
    stats = [[] for _ in heads]
    scaled = [mask * HD ** (-0.5) for mask in masks()]

    def first(n, h):
        q, k, _ = heads[n]
        return (times_t(k, q * scaled[h]),)

    def middle(n, h, scores):
        scores = jnp.where(same, scores, -1000000000.0)
        top = jnp.max(scores, axis=0, keepdims=True)
        powers = jnp.exp(scores - top)
        total = jnp.sum(powers, axis=0, keepdims=True)
        stats[n].append(top + jnp.log(total))
        return ((powers * (1.0 / total)).astype(low),)

    def last(n, h, probs):
        outs[n].append(times(turned[n][h * HD : (h + 1) * HD], probs))

    in_turn([(n, h) for n in range(len(heads)) for h in range(2)], first, middle, last)
    return [jnp.concatenate(out, axis=0).T.astype(low) for out in outs], stats


def attend_pair_back(same, q, k, v, do, stats):
    k_turned = (k.astype(float_out) * HD ** (-0.5)).T.astype(low)
    width = q.shape[0] // 2
    q_of = [q * (mask * HD ** (-0.5)) for mask in masks()]
    do_of = [do * mask for mask in masks()]
    dq = [[], []]
    sums = [0.0, 0.0]

    def part(c):
        return slice(c * width, (c + 1) * width)

    def first(c, h):
        return times_t(k, q_of[h][part(c)]), times_t(v, do_of[h][part(c)])

    def middle(c, h, scores, grad):
        scores = jnp.where(same[:, part(c)], scores, -1000000000.0)
        probs = jnp.exp(scores - stats[h][:, part(c)])
        level = jnp.sum(probs * grad, axis=0, keepdims=True)
        return probs.astype(low), (probs * (grad - level)).astype(low)

    def last(c, h, probs, back):
        sums[0] = sums[0] + times(back, q_of[h][part(c)])
        sums[1] = sums[1] + times(probs, do_of[h][part(c)])
        dq[h].append(times(k_turned[h * HD : (h + 1) * HD], back))

    in_turn([(c, h) for c in range(2) for h in range(2)], first, middle, last)
    turned = jnp.concatenate([jnp.concatenate(parts, axis=1) for parts in dq], axis=0)
    return turned.T.astype(low), sums[0].astype(low), sums[1].astype(low)


def front_kernel(
    pc,
    owners_ref,
    ids_ref,
    masters_ref,
    raw_table,
    codes_ref,
    phones_ref,
    segs_ref,
    rate_ref,
    same_ref,
    other_ref,
    w_ref,
    params_ref,
    multi_out,
    hot_out,
    x_out,
    h_out,
    qkv_out,
    mixed_out,
    lse_ref,
    x1_out,
    h2_out,
    act_out,
    slope_out,
    x2_out,
    table_ref,
    seg_col,
    phone_col,
    code_cols,
    starts_ref,
    waves,
    rounded,
    ordered,
    counts_ref,
    *rest,
):
    parts = len(rank_cuts(ordered.shape[0])) - 1
    slots = rest[:parts]
    (
        pieces,
        table_all,
        wf,
        multi,
        hot,
        x0,
        h1,
        pool,
        wo,
        h2,
        act,
        slope,
        sent,
        landed,
        key_ref,
        in_sem,
        a_send,
        a_recv,
        t_send,
        t_recv,
        own_sem,
        z_send,
        z_recv,
        e_send,
        e_recv,
        f_send,
        f_recv,
        c_send,
        c_recv,
        m_send,
        m_recv,
        w_sem,
        out_sem,
        qkv_sem,
        mix_sem,
        o_sem,
        u_sem,
        d_sem,
        x1_sem,
        act_sem,
        x2_sem,
    ) = rest[parts:]
    pc.here()
    blocks = BLOCKS
    per_group, piece = rounded.shape[:2]
    own_sections = table_ref.shape[0]
    rows, length = segs_ref.shape
    steps = length // ROWS_AT_ONCE
    pairs = HEADS // 2
    mine = pc.columns(pc.panel_of(pc.s), pc.panel)
    core_half = pc.columns(pc.c, pc.half)
    loads = [
        pltpu.make_async_copy(
            masters_ref, x0.at[pl.ds(0, per_group * piece)], in_sem.at[0]
        ),
        pltpu.make_async_copy(same_ref, waves.at[0], in_sem.at[1]),
        pltpu.make_async_copy(other_ref, waves.at[1], in_sem.at[2]),
    ]
    begin(loads)
    keys = rank_keys(owners_ref, OUTWARD, per_group, pc.groups)
    for p in range(blocks):
        key_ref[p] = keys[p]
    base = pc.s * per_group
    slot_of = []
    for k in range(per_group):
        slot = jnp.int32(0)
        for p in range(blocks):
            slot = jnp.where(keys[p] == base + k, owners_ref[OUTWARD[p]] - base, slot)
        slot_of.append(slot)
    table_ref[...] = jnp.zeros_like(table_ref)
    for k in range(6):
        for n in range(own_sections):
            table_ref[n, k : k + 1] = raw_table[n : n + 1, k * D : (k + 1) * D]
    pc.barrier()
    loads[0].wait()
    rounded[...] = x0[: per_group * piece].astype(low).reshape(rounded.shape)
    for k in range(per_group):
        ordered[k] = rounded[jnp.clip(slot_of[k], 0, per_group - 1)]
    cuts = rank_cuts(per_group)
    for m, place in enumerate(slots):
        for k in range(cuts[m], cuts[m + 1]):
            place[pc.s, k - cuts[m]] = ordered[k, :, mine]

    def exchange(m):
        first, count = cuts[m], cuts[m + 1] - cuts[m]
        return [
            remote(
                ordered.at[
                    pl.ds(first, count),
                    :,
                    pc.columns(pc.panel_of(pc.section_peer(d)), pc.panel),
                ],
                slots[m].at[pc.s],
                a_send.at[m, d - 1],
                a_recv.at[m, d - 1],
                (pc.section_peer(d), pc.j),
            )
            for d in range(1, pc.groups)
        ]

    def table_exchange():
        return [
            remote(
                table_ref,
                table_all.at[pl.ds(pc.s * own_sections, own_sections)],
                t_send.at[d - 1],
                t_recv.at[d - 1],
                (pc.section_peer(d), pc.j),
            )
            for d in range(1, pc.groups)
        ]

    for m in range(len(cuts) - 1):
        begin(exchange(m))
    begin(table_exchange())
    table_all[pl.ds(pc.s * own_sections, own_sections)] = table_ref[...]
    section = lax.broadcasted_iota(jnp.int32, (SECTIONS, 128), 0)
    counts = jnp.zeros((SECTIONS, 128), jnp.float32)
    for r in range(rows):
        counts = counts + jnp.where(section == ids_ref[0, r], float(length), 0.0)
    counts_ref[...] = counts
    small = pc.small_stages(counts_ref, sent, landed, m_send, m_recv)

    def take_pieces(m):
        for copy in exchange(m):
            copy.wait()
        until = cuts[m + 1] if m + 2 < len(cuts) else blocks
        for p in range(cuts[m], until):
            key = jnp.clip(key_ref[p], 0, per_group * pc.groups - 1)
            section, rank = lax.div(key, per_group), lax.rem(key, per_group)
            found = slots[0][section, jnp.minimum(rank, cuts[1] - 1)]
            for n in range(1, m + 1):
                last = cuts[n + 1] - cuts[n] - 1
                here = slots[n][section, jnp.clip(rank - cuts[n], 0, last)]
                found = jnp.where(rank >= cuts[n], here, found)
            pieces[p] = found

    def set_params():
        for copy in table_exchange():
            copy.wait()
        line = lax.broadcasted_iota(jnp.int32, (8, D), 0)
        for r in range(rows):
            held = jnp.sum(
                jnp.where(section == ids_ref[0, r], counts_ref[...], 0.0), axis=0, keepdims=True
            )
            weight = 1.0 / (SECTIONS * jnp.concatenate([held] * (D // 128), axis=1))
            params_ref[r] = jnp.where(line == 6, weight, table_all[ids_ref[0, r]])

    def own(p):
        return pltpu.make_async_copy(
            pieces.at[p], w_ref.at[p, pc.z, pc.x, :, mine], own_sem.at[p]
        )

    def along_z(p):
        return [
            remote(
                pieces.at[p],
                w_ref.at[p, pc.z, pc.x, :, mine],
                z_send.at[p, d - 1],
                z_recv.at[p, d - 1],
                pc.at_z(d),
            )
            for d in range(1, pc.nz)
        ]

    def spread(p, part, send_sem, recv_sem, count, target, source=None, first=0):
        source = part if source is None else source
        return [
            remote(
                source,
                part,
                send_sem.at[p, first + d - 1],
                recv_sem.at[p, first + d - 1],
                target(d),
            )
            for d in range(1, count)
        ]

    middle_z = pc.nz // 2
    lower, upper = pl.ds(0, middle_z), pl.ds(middle_z, pc.nz - middle_z)

    def first_x(p):
        part = w_ref.at[p, lower, pc.x, :, mine]
        return spread(p, part, e_send, e_recv, pc.nx, pc.at_x)

    def first_y(p):
        part = w_ref.at[p, upper, pc.x, :, mine]
        return spread(p, part, e_send, e_recv, pc.ny, pc.at_y, first=pc.nx - 1)

    def then_y(p):
        part = w_ref.at[p, lower, :, :, mine]
        return spread(p, part, f_send, f_recv, pc.ny, pc.at_y)

    def then_x(p):
        part = w_ref.at[p, upper, pc.x, :, core_half]
        return spread(p, part, f_send, f_recv, pc.nx, pc.at_x, first=pc.ny - 1)

    def far_x(p):
        part = w_ref.at[p, pc.z, pc.x, :, mine]
        return spread(p, part, e_send, e_recv, pc.nx, pc.at_x, pieces.at[p])

    def far_y(p):
        part = w_ref.at[p, pc.z, :, :, mine]
        return spread(p, part, f_send, f_recv, pc.ny, pc.at_y)

    def ring(p, k):
        part = w_ref.at[p, pc.z_of((pc.nz - k + 1) % pc.nz), :, :, core_half]
        return [remote(part, part, z_send.at[p, k - 1], z_recv.at[p, k - 1], pc.at_z(1))]

    def to_core(p):
        part = w_ref.at[p, :, :, :, core_half]
        return [remote(part, part, c_send.at[p], c_recv.at[p], pc.at_core())]

    def into_vmem(p):
        return pltpu.make_async_copy(w_ref.at[p], wf.at[p], w_sem.at[p])

    for r in range(rows):
        at = pl.ds(r * length, length)
        tall = jnp.concatenate(
            [codes_ref[r].astype(float_out), jnp.zeros((128 - LEVELS, length), float_out)], axis=0
        )
        code_cols[at] = tall.T.astype(jnp.int32)
        seg_col[pl.ds(r * length, length)] = column_of(segs_ref[r : r + 1])
        phone_col[pl.ds(r * length, length)] = column_of(phones_ref[r : r + 1])
        starts = [
            jnp.sum(jnp.where(segs_ref[r : r + 1] < k, 1.0, 0.0), axis=1, keepdims=True)
            for k in (0, 1, 2)
        ]
        angle = jnp.concatenate(starts, axis=0) * rate_ref[...]
        odd = lax.broadcasted_iota(jnp.int32, angle.shape, 1) % 2
        starts_ref[r, 0:3] = jnp.cos(angle)
        starts_ref[r, 3:6] = jnp.where(odd == 1, 1.0, -1.0) * jnp.sin(angle)

    def chunk(i):
        return pl.ds(i * ROWS_AT_ONCE, ROWS_AT_ONCE)

    def embed_out(i):
        made = ((multi, multi_out), (hot, hot_out), (x0, x_out), (h1, h_out))
        return [
            pltpu.make_async_copy(a.at[chunk(i)], b.at[chunk(i)], out_sem.at[i, n])
            for n, (a, b) in enumerate(made)
        ]

    def qkv_copy(n):
        return pltpu.make_async_copy(pool.at[n], qkv_out.at[n], qkv_sem.at[n])

    def weight(first, count=2):
        return wf[first : first + count].reshape(count * D // 2, D)

    def prepare_step(i):
        at = chunk(i)
        r, local = i // steps, pl.ds((i % steps) * ROWS_AT_ONCE, ROWS_AT_ONCE)
        vocab = lax.broadcasted_iota(jnp.int32, (ROWS_AT_ONCE, CODES), 1)
        count = jnp.zeros((ROWS_AT_ONCE, CODES), jnp.float32)
        for level in range(LEVELS):
            code = code_cols[at, level : level + 1]
            code = jnp.where(ids_ref[0, r] >= level, code, -1)
            count = count + jnp.where(code == vocab, 1.0, 0.0)
        multi[at] = count.astype(low)
        names = lax.broadcasted_iota(jnp.int32, (ROWS_AT_ONCE, PHONES), 1)
        hot[at] = jnp.where(phone_col[at] == names, 1.0, 0.0).astype(low)
        segs = seg_col[at]
        cosine, sine = (
            jnp.where(
                segs == 0,
                starts_ref[r, k : k + 1],
                jnp.where(segs == 1, starts_ref[r, k + 1 : k + 2], starts_ref[r, k + 2 : k + 3]),
            )
            for k in (0, 3)
        )
        x0[at] = waves[0, local] * cosine + waves[1, local] * sine

    def embed_step(i):
        at, r = chunk(i), i // steps
        stream = times(multi[at], weight(CODE)) + times(hot[at], weight(PHONE, 1)) + x0[at]
        x0[at] = stream
        normed, _ = normalize(stream)
        h1[at] = (normed * (1.0 + params_ref[r, 0:1]) + params_ref[r, 1:2]).astype(low)
        begin(embed_out(i))

    def project_step(k):
        for r in range(rows):
            made = times(h1[r * length : (r + 1) * length], wf[pl.ds(QKV + 2 * k, 2)].reshape(D, D))
            pool[rows * k + r] = made.astype(low).reshape(pool.shape[1:])
            qkv_copy(rows * k + r).start()

    def row(r):
        return pl.ds(r * length, length)

    def mixed_copy(r):
        return pltpu.make_async_copy(pool.at[3 * rows + r], mixed_out.at[r], mix_sem.at[r])

    def attend_step(n):
        r, h = lax.div(2 * n, pairs), lax.rem(2 * n, pairs)
        same = seg_col[row(r)] == segs_ref[pl.ds(r, 1)]
        at = [pc.columns(h + e, 2 * HD) for e in range(2)]
        outs, stats = attend_pairs(
            same,
            [
                [
                    pool[rows * k + r, :, :, :, columns].reshape(length, 2 * HD)
                    for k in range(3)
                ]
                for columns in at
            ],
        )
        for e in range(2):
            pool[3 * rows + r, :, :, :, at[e]] = outs[e].reshape(*pool.shape[1:4], 2 * HD)
            for k, lse in enumerate(stats[e]):
                lse_ref[r, h + e, k : k + 1] = lse

        @pl.when(h + 2 == pairs)
        def _():
            mixed_copy(r).start()

    def out_weight():
        return pltpu.make_async_copy(w_ref.at[pl.ds(OUT, 2)], wo, o_sem)

    def up_weight():
        return pltpu.make_async_copy(w_ref.at[pl.ds(UP, 8)], wf.at[pl.ds(0, 8)], u_sem)

    def down_weight(p):
        return pltpu.make_async_copy(w_ref.at[p], pool.at[p - DOWN], d_sem.at[p - DOWN])

    def stream_copies(i):
        return [
            pltpu.make_async_copy(x0.at[chunk(i)], x1_out.at[chunk(i)], x1_sem.at[i, 0]),
            pltpu.make_async_copy(h2.at[chunk(i)], h2_out.at[chunk(i)], x1_sem.at[i, 1]),
        ]

    def act_copy(i):
        return pltpu.make_async_copy(
            act.at[:, chunk(i)], act_out.at[:, chunk(i)], act_sem.at[i, 0]
        )

    def slope_copy(i):
        return pltpu.make_async_copy(
            slope.at[i % 2], slope_out.at[:, chunk(i)], act_sem.at[i, 1]
        )

    def out_step(i):
        at, r = chunk(i), i // steps
        for copy in embed_out(i):
            copy.wait()
        depth = pc.nz // steps
        mixed = pool[3 * rows + r, pl.ds(i % steps * depth, depth)].reshape(ROWS_AT_ONCE, D)
        stream = x0[at] + times(mixed, wo[...].reshape(D, D))
        x0[at] = stream
        normed, _ = normalize(stream)
        h2[at] = (normed * (1.0 + params_ref[r, 2:3]) + params_ref[r, 3:4]).astype(low)
        begin(stream_copies(i))

    def up_step(i):
        at = chunk(i)

        @pl.when(i >= 2)
        def _():
            slope_copy(i - 2).wait()

        for g in range(4):
            u = times(h2[at], weight(2 * g))
            cdf = 0.5 + 0.5 * lax.erf(u * math.sqrt(0.5))
            density = jnp.exp(-0.5 * (u * u)) * (1.0 / math.sqrt(2.0 * math.pi))
            act[g, at] = (u * cdf).astype(low)
            slope[i % 2, g] = (cdf + u * density).astype(low)
        begin([act_copy(i), slope_copy(i)])

    def x2_copy(r):
        return pltpu.make_async_copy(x0.at[row(r)], x2_out.at[row(r)], x2_sem.at[r])

    def down_step(g):
        down_weight(DOWN + 2 * g).wait()
        down_weight(DOWN + 2 * g + 1).wait()
        for r in range(rows):
            at = row(r)
            x0[at] = x0[at] + times(act[g, at], pool[2 * g : 2 * g + 2].reshape(D, D))
            if g == 3:
                x2_copy(r).start()

    ahead = 4
    hops = pc.nz - 1
    embed_steps = rows * steps
    lands = [
        p + (2 * hops + 1 if p % LONG_EVERY == LONG_OUT else 6) for p in range(blocks)
    ]
    embed_from = max(lands[:QKV]) + 1
    project_from = max(
        embed_from + embed_steps,
        *(max(lands[QKV + 2 * k : QKV + 2 * k + 2]) + 1 - k for k in range(3)),
    )
    attend_from = project_from + 3
    out_from = max(attend_from + rows * pairs // 2, max(lands[OUT:UP]) + 2)
    out_ticks = embed_steps // 2
    up_fetch = max(max(lands[UP:DOWN]) + 1, attend_from)
    up_from = max(out_from + out_ticks, up_fetch + 1)
    late = max(1, out_from + out_ticks - min(lands[DOWN:HEAD]))
    down_at = []
    for g in range(4):
        landed_by = max(lands[DOWN + 2 * g : DOWN + 2 * g + 2]) + late + 1
        after = down_at[-1] + 1 if down_at else up_from + embed_steps
        down_at.append(max(landed_by, after))

    def step(p, body):
        pl.when(within(p, blocks))(lambda: body(p))

    def launch(p):
        own(p).start()
        by_kind(p, LONG_OUT, lambda: begin(along_z(p)), lambda: begin(far_x(p)))

    def far_second(p):
        def far():
            own(p).wait()
            landed_all(far_x(p))
            begin(far_y(p))

        by_kind(p, LONG_OUT, far=far)

    def first(p):
        def near():
            own(p).wait()
            landed_all(along_z(p))
            begin(first_x(p) + first_y(p))

        def far():
            landed_all(far_y(p))
            begin(ring(p, 1))

        by_kind(p, LONG_OUT, near, far)

    def ring_on(k):
        def body(p):
            def far():
                landed_all(ring(p, k - 1))
                begin(ring(p, k))

            by_kind(p, LONG_OUT, far=far)

        return body

    def then(p):
        def near():
            landed_all(first_x(p))
            begin(then_y(p))
            landed_all(first_y(p))
            begin(then_x(p))

        by_kind(p, LONG_OUT, near)

    def core_near(p):
        def near():
            landed_all(then_y(p) + then_x(p))
            begin(to_core(p))

        by_kind(p, LONG_OUT, near)

    def core_far(p):
        def far():
            landed_all(ring(p, hops))
            begin(to_core(p))

        by_kind(p, LONG_OUT, far=far)

    def held(p):
        @pl.when((p >= DOWN) & (p < HEAD))
        def _():
            down_weight(p).start()

    def arrived(p):
        landed_all(to_core(p))

        @pl.when(p < FRONT)
        def _():
            into_vmem(p).start()

    sent_after = 2 * hops + 4

    def sent_off(p):
        gone(to_core(p))

        def near():
            gone(along_z(p) + first_x(p) + first_y(p) + then_y(p) + then_x(p))

        def far():
            gone(far_x(p) + far_y(p))
            for k in range(1, pc.nz):
                gone(ring(p, k))

        by_kind(p, LONG_OUT, near, far)

    def tick(turn, carry):
        t = turn - ahead
        for m in range(len(cuts) - 1):
            pl.when(turn == cuts[m])(functools.partial(take_pieces, m))
        step(turn, launch)
        step(t + 2, far_second)
        step(t, first)
        step(t - 2, then)
        for k in range(2, pc.nz):
            step(t - 2 * (k - 1), ring_on(k))
        step(t - 5, core_near)
        step(t - 2 * hops, core_far)
        step(t - 6, lambda p: by_kind(p, LONG_OUT, lambda: arrived(p)))
        step(t - 2 * hops - 1, lambda p: by_kind(p, LONG_OUT, far=lambda: arrived(p)))
        step(t - 6 - late, lambda p: by_kind(p, LONG_OUT, lambda: held(p)))
        step(t - 2 * hops - 1 - late, lambda p: by_kind(p, LONG_OUT, far=lambda: held(p)))

        for stage, (start, end) in enumerate(small):
            pl.when(turn == ahead + 1 + 2 * stage)(start)
            pl.when(turn == ahead + 2 + 2 * stage)(end)
        pl.when(turn == ahead + 7)(set_params)

        @pl.when(t == 0)
        def _():
            loads[1].wait()
            loads[2].wait()

        @pl.when(within(t, embed_steps))
        def _():
            prepare_step(t)

        @pl.when(t == embed_from)
        def _():
            for p in range(QKV):
                into_vmem(p).wait()

        @pl.when(within(t - embed_from, embed_steps))
        def _():
            embed_step(t - embed_from)

        @pl.when(within(t - project_from, 3))
        def _():
            k = t - project_from
            into_vmem(QKV + 2 * k).wait()
            into_vmem(QKV + 2 * k + 1).wait()
            project_step(k)

        @pl.when(within(t - attend_from, rows * pairs // 2))
        def _():
            attend_step(t - attend_from)

        @pl.when(t == out_from - 1)
        def _():
            out_weight().start()

        @pl.when(t == up_fetch)
        def _():
            up_weight().start()

        @pl.when(t == out_from)
        def _():
            out_weight().wait()
            for n in range(3 * rows):
                qkv_copy(n).wait()

        @pl.when(within(t - out_from, out_ticks))
        def _():
            out_step(2 * (t - out_from))
            out_step(2 * (t - out_from) + 1)

        @pl.when(t == out_from + out_ticks - 1)
        def _():
            for r in range(rows):
                mixed_copy(r).wait()

        @pl.when(t == up_from)
        def _():
            up_weight().wait()

        @pl.when(within(t - up_from, embed_steps))
        def _():
            up_step(t - up_from)

        for g in range(4):

            @pl.when(t == down_at[g])
            def _(g=g):
                if g == 0:
                    for i in range(embed_steps):
                        for copy in stream_copies(i):
                            copy.wait()
                down_step(g)

        step(t - sent_after, sent_off)
        return carry

    last = max(blocks + 6, blocks + 2 * hops, down_at[-1] + 1)
    lax.fori_loop(0, last + ahead, tick, 0)

    def finish(p, carry):
        sent_off(p)
        return carry

    lax.fori_loop(last - sent_after, blocks, finish, 0)
    for i in range(embed_steps):
        act_copy(i).wait()
    for i in range(embed_steps - 2, embed_steps):
        slope_copy(i).wait()
    for r in range(rows):
        x2_copy(r).wait()


def like(shape, dtype=low):
    return jax.ShapeDtypeStruct(shape, dtype)


def front(pc, owners, ids, masters, table, codes, phones, segments):
    per_group, piece, _ = masters.shape
    rows, length = segments.shape
    total = rows * length
    rate = jnp.asarray(rates()[1][None], jnp.float32)
    own_sections = table.shape[0]
    hops = pc.nx - 1 + pc.ny - 1
    same, other = index_waves(length)
    small = pc.small_slots()
    embed_steps = total // ROWS_AT_ONCE
    cuts = rank_cuts(per_group)
    dma = pltpu.SemaphoreType.DMA
    vmem = pl.BlockSpec(memory_space=pltpu.VMEM)
    smem = pl.BlockSpec(memory_space=pltpu.SMEM)
    far = pl.BlockSpec(memory_space=pl.ANY)
    return pl.pallas_call(
        functools.partial(front_kernel, pc),
        out_shape=(
            like((BLOCKS, pc.nz, pc.nx, piece, D)),
            like((rows, 8, D), float_out),
            like((total, CODES)),
            like((total, PHONES)),
            like((total, D), float_out),
            like((total, D)),
            like((3 * rows, pc.nz, pc.nx, piece, D)),
            like((rows, pc.nz, pc.nx, piece, D)),
            like((rows, HEADS // 2, 2, length), float_out),
            like((total, D), float_out),
            like((total, D)),
            like((4, total, D)),
            like((4, total, D)),
            like((total, D), float_out),
        ),
        in_specs=[smem, smem, far] + [vmem] * 5 + [far, far],
        out_specs=(far, vmem, far, far, far, far, far, far, vmem, far, far, far, far, far),
        scratch_shapes=[
            pltpu.VMEM((own_sections, 8, D), float_out),
            pltpu.VMEM((total, 1), jnp.int32),
            pltpu.VMEM((total, 1), jnp.int32),
            pltpu.VMEM((total, 128), jnp.int32),
            pltpu.VMEM((rows, 8, D), float_out),
            pltpu.VMEM((2, length, D), float_out),
            pltpu.VMEM((per_group, piece, D), low),
            pltpu.VMEM((per_group, piece, D), low),
            pltpu.VMEM((SECTIONS, 128), float_out),
            *(
                pltpu.VMEM((pc.groups, b - a, piece, pc.panel), low)
                for a, b in zip(cuts[:-1], cuts[1:], strict=True)
            ),
            pltpu.VMEM((BLOCKS, piece, pc.panel), low),
            pltpu.VMEM((own_sections * pc.groups, 8, D), float_out),
            pltpu.VMEM((FRONT, pc.nz, pc.nx, piece, D), low),
            pltpu.VMEM((total, CODES), low),
            pltpu.VMEM((total, PHONES), low),
            pltpu.VMEM((total, D), float_out),
            pltpu.VMEM((total, D), low),
            pltpu.VMEM((max(4 * rows, 8), pc.nz, pc.nx, piece, D), low),
            pltpu.VMEM((2, pc.nz, pc.nx, piece, D), low),
            pltpu.VMEM((total, D), low),
            pltpu.VMEM((4, total, D), low),
            pltpu.VMEM((2, 4, ROWS_AT_ONCE, D), low),
            pltpu.VMEM((2, 8, 128), float_out),
            pltpu.VMEM((small, 8, 128), float_out),
            pltpu.SMEM((BLOCKS,), jnp.int32),
            dma((3,)),
            dma((3, pc.groups - 1)),
            dma((3, pc.groups - 1)),
            dma((pc.groups - 1,)),
            dma((pc.groups - 1,)),
            dma((BLOCKS,)),
            dma((BLOCKS, pc.nz - 1)),
            dma((BLOCKS, pc.nz - 1)),
            dma((BLOCKS, hops)),
            dma((BLOCKS, hops)),
            dma((BLOCKS, hops)),
            dma((BLOCKS, hops)),
            dma((BLOCKS,)),
            dma((BLOCKS,)),
            dma((small,)),
            dma((small,)),
            dma((FRONT,)),
            dma((embed_steps, 4)),
            dma((3 * rows,)),
            dma((rows,)),
            dma,
            dma,
            dma((8,)),
            dma((embed_steps, 2)),
            dma((embed_steps, 2)),
            dma((rows,)),
        ],
        name="front",
        compiler_params=pltpu.CompilerParams(
            collective_id=0, has_side_effects=True, vmem_limit_bytes=62 * MIB
        ),
    )(owners, ids, masters.reshape(-1, D), table, codes, phones, segments, rate, same, other)


FAR = ("h3", "act", "h2", "mixed", "h1", "multi", "hot", "dlogits", "dffn", "du", "dattn")


HOME = (
    (0, 2, "h3", "dlogits"),
    (2, 8, "act", "dffn"),
    (10, 8, "h2", "du"),
    (18, 2, "mixed", "dattn"),
    (20, 6, "h1", "dqkv"),
    (26, 2, "multi", "demb"),
    (28, 1, "hot", "demb"),
)


def back_kernel(pc, *refs):
    held = dict(zip(FAR, refs[2 : 2 + len(FAR)], strict=True))
    owners_ref, ids_ref = refs[:2]
    (
        qkv_ref,
        do_ref,
        x0_ref,
        dx_ref,
        w_ref,
        lse_ref,
        segs_ref,
        params_ref,
        rows_ref,
        loss_ref,
        out_ref,
        table_out,
        sums_out,
        seg_col,
        block_of_ref,
        key_ref,
        rank_ref,
        arrived,
        sums_ref,
        x_buf,
        y_buf,
        own_half,
        send_half,
        core_in,
        first_a,
        first_b,
        then_in,
        z_in,
        far_z,
        far_yx,
        far_in,
        final,
        by_slot,
        square,
        heads,
        dqkv,
        demb,
        qkv_w,
        chunks,
        row_sums,
        table_mine,
        table_in,
        table_mid,
        sent,
        landed,
        in_sem,
        head_sem,
        chunk_sem,
        w_sem,
        free_sem,
        c_send,
        c_recv,
        e_send,
        e_recv,
        f_send,
        f_recv,
        z_send,
        z_recv,
        a_send,
        a_recv,
        t_send,
        t_recv,
        m_send,
        m_recv,
    ) = refs[2 + len(FAR) :]
    held["dqkv"], held["demb"] = dqkv, demb
    pc.here()
    blocks = BLOCKS
    per_group = out_ref.shape[0]
    own_sections = table_out.shape[0]
    rows, length = segs_ref.shape
    pairs = HEADS // 2
    steps = length // ROWS_AT_ONCE
    attend_steps, embed_steps = rows * pairs, rows * steps
    width = x_buf.shape[2]
    keep = pc.columns(pc.c, pc.half)
    away = pc.columns(1 - pc.c, pc.half)
    core_slots = core_in.shape[0]
    hops = pc.nz - 1
    release = 2 * pc.nz - 1

    def fetch(t):
        for from_, count, xs, ys in HOME:
            u = t - from_

            @pl.when(within(u, count))
            def _(xs=xs, ys=ys, u=u):
                slot = lax.rem(t, 2)
                x_ref, y_ref = held[xs], held[ys]
                columns = pc.columns(lax.rem(u, 2), width)
                x_src = x_ref.at[lax.div(u, 2), :, columns] if len(x_ref.shape) == 3 else x_ref.at[:, columns]
                y_src = y_ref.at[lax.div(u, 2)] if len(y_ref.shape) == 3 else y_ref
                pltpu.make_async_copy(x_src, x_buf.at[slot], in_sem.at[slot, 0]).start()
                pltpu.make_async_copy(y_src, y_buf.at[slot], in_sem.at[slot, 1]).start()

    def fetched(slot):
        for n, buf in enumerate((x_buf, y_buf)):
            pltpu.make_async_copy(buf.at[slot], buf.at[slot], in_sem.at[slot, n]).wait()

    def head_copies(n):
        r, h, slot = n // pairs, n % pairs, n % 2
        at, columns = pl.ds(r * length, length), pc.columns(h, 2 * HD)
        copies = [
            pltpu.make_async_copy(
                qkv_ref.at[k, at, columns], heads.at[slot, k], head_sem.at[slot, k]
            )
            for k in range(3)
        ]
        copies.append(
            pltpu.make_async_copy(do_ref.at[at, columns], heads.at[slot, 3], head_sem.at[slot, 3])
        )
        return copies

    def chunk(i):
        return pl.ds(i * ROWS_AT_ONCE, ROWS_AT_ONCE)

    def chunk_copies(i):
        slot = i % 2
        return [
            pltpu.make_async_copy(x0_ref.at[chunk(i)], chunks.at[slot, 0], chunk_sem.at[slot, 0]),
            pltpu.make_async_copy(dx_ref.at[chunk(i)], chunks.at[slot, 1], chunk_sem.at[slot, 1]),
        ]

    weight_copy = pltpu.make_async_copy(w_ref.at[pl.ds(QKV, 6)], qkv_w, w_sem)

    def attend_back_step(n):
        r, h, slot = n // pairs, n % pairs, n % 2
        at, columns = pl.ds(r * length, length), pc.columns(h, 2 * HD)
        same = seg_col[at] == segs_ref[pl.ds(r, 1)]
        stats = [lse_ref[r, h, k : k + 1] for k in range(2)]
        made = attend_pair_back(same, *(heads[slot, k] for k in range(4)), stats)
        for k in range(3):
            dqkv[k, at, columns] = made[k]

    def embed_back_step(i):
        for copy in chunk_copies(i):
            copy.wait()
        r, slot = i // steps, i % 2
        dh = 0.0
        for k in range(3):
            dh = dh + times_t(
                dqkv[k, chunk(i)], qkv_w[2 * k : 2 * k + 2].reshape(D, D)
            )
        normed, scale = normalize(chunks[slot, 0])
        dx, gain, shift = norm_back(dh, normed, scale, params_ref[r, 0:1])
        demb[chunk(i)] = (chunks[slot, 1] + dx).astype(low)
        row_sums[r, 0:2] += jnp.concatenate([gain, shift], axis=0)

    def to_core(b):
        return [
            remote(
                send_half.at[lax.rem(b, 4)],
                core_in.at[lax.rem(b, core_slots)],
                c_send.at[b],
                c_recv.at[b],
                pc.at_core(),
            )
        ]

    middle_z = pc.nz // 2
    lower, upper = slice(0, middle_z), slice(middle_z, pc.nz)
    lower_at, upper_at = pl.ds(0, middle_z), pl.ds(middle_z, pc.nz - middle_z)

    def first_x(b):
        return [
            remote(
                core_in.at[lax.rem(b, core_slots), lower_at, pc.x_of(d)],
                first_a.at[place_among(b), d - 1],
                e_send.at[b, d - 1],
                e_recv.at[b, d - 1],
                pc.at_x(d),
            )
            for d in range(1, pc.nx)
        ]

    def first_y(b):
        return [
            remote(
                core_in.at[
                    lax.rem(b, core_slots), upper_at, :, :, pc.columns(pc.y_of(d), pc.panel)
                ],
                first_b.at[place_among(b), d - 1],
                e_send.at[b, pc.nx - 1 + d - 1],
                e_recv.at[b, pc.nx - 1 + d - 1],
                pc.at_y(d),
            )
            for d in range(1, pc.ny)
        ]

    def then_y(b):
        return [
            remote(
                first_a.at[place_among(b), 0, :, :, pc.columns(pc.y_of(d), pc.panel)],
                then_in.at[place_among(b), d - 1, lower_at],
                f_send.at[b, d - 1],
                f_recv.at[b, d - 1],
                pc.at_y(d),
            )
            for d in range(1, pc.ny)
        ]

    def then_x(b):
        return [
            remote(
                first_b.at[place_among(b), 0, :, pc.x_of(d)],
                then_in.at[place_among(b), d - 1, upper_at],
                f_send.at[b, pc.ny - 1 + d - 1],
                f_recv.at[b, pc.ny - 1 + d - 1],
                pc.at_x(d),
            )
            for d in range(1, pc.nx)
        ]

    def along_z(b):
        return [
            remote(
                then_in.at[place_among(b), 0, pc.z_of(d)],
                z_in.at[place_among(b), d - 1],
                z_send.at[b, d - 1],
                z_recv.at[b, d - 1],
                pc.at_z(d),
            )
            for d in range(1, pc.nz)
        ]

    def ring(b, k):
        n = lax.div(b, LONG_EVERY)
        source = (
            core_in.at[lax.rem(b, core_slots), pc.z_of(hops)] if k == 1 else far_z.at[n, k - 2]
        )
        return [
            remote(source, far_z.at[n, k - 1], z_send.at[b, k - 1], z_recv.at[b, k - 1], pc.at_z(1))
        ]

    def far_y(b):
        n = lax.div(b, LONG_EVERY)
        return [
            remote(
                far_z.at[n, hops - 1, :, :, pc.columns(pc.y_of(d), pc.panel)],
                far_yx.at[n, d - 1],
                f_send.at[b, d - 1],
                f_recv.at[b, d - 1],
                pc.at_y(d),
            )
            for d in range(1, pc.ny)
        ]

    def far_x(b):
        n = lax.div(b, LONG_EVERY)
        return [
            remote(
                far_yx.at[n, 0, pc.x_of(d)],
                far_in.at[n, d - 1],
                e_send.at[b, d - 1],
                e_recv.at[b, d - 1],
                pc.at_x(d),
            )
            for d in range(1, pc.nx)
        ]

    def summed(own, landed_ref, index, count):
        total = own.astype(float_out)
        for d in range(count - 1):
            total = total + landed_ref[index, d].astype(float_out)
        return total

    def table_stage():
        return [
            remote(
                table_mine.at[pl.ds(pc.section_peer(d) * own_sections, own_sections)],
                table_in.at[d - 1],
                t_send.at[d - 1],
                t_recv.at[d - 1],
                (pc.section_peer(d), pc.j),
            )
            for d in range(1, pc.groups)
        ]

    def table_hop(stage):
        count, target = ((pc.nx, pc.at_x), (pc.nz, pc.at_z))[stage]
        first = pc.groups - 1 + stage * (pc.nx - 1)
        return [
            remote(
                table_mid.at[stage],
                table_in.at[first + d - 1],
                t_send.at[first + d - 1],
                t_recv.at[first + d - 1],
                target(d),
            )
            for d in range(1, count)
        ]

    def table_landed(copies, own, first):
        for copy in copies:
            copy.wait()
        total = own
        for n in range(len(copies)):
            total = total + table_in[first + n]
        return total

    def table_after_section():
        own = table_mine[pl.ds(pc.s * own_sections, own_sections)]
        table_mid[0] = table_landed(table_stage(), own, 0)
        begin(table_hop(0))

    def table_after_x():
        table_mid[1] = table_landed(table_hop(0), table_mid[0], pc.groups - 1)
        begin(table_hop(1))

    def table_after_z():
        first = pc.groups - 1 + pc.nx - 1
        table_out[...] = table_landed(table_hop(1), table_mid[1], first)

    fetch(0)
    begin(head_copies(0))
    weight_copy.start()
    pc.barrier()
    square[...] = jnp.zeros_like(square)
    final[blocks] = jnp.zeros(final.shape[1:], low)
    row_sums[...] = rows_ref[...]
    for r in range(rows):
        seg_col[pl.ds(r * length, length)] = column_of(segs_ref[r : r + 1])

    base = pc.s * per_group

    def rank_blocks():
        keys = rank_keys(owners_ref, HOMEWARD[::-1], per_group, pc.groups)[::-1]
        for b in range(blocks):
            key_ref[b] = keys[b]
        for i in range(per_group):
            rank = jnp.int32(per_group)
            for b in range(blocks):
                rank = jnp.where(owners_ref[HOMEWARD[b]] == base + i, keys[b] - base, rank)
            rank_ref[i] = rank

        def find(i, carry):
            where = jnp.int32(blocks)
            for b in range(blocks):
                where = jnp.where(key_ref[b] == i, b, where)
            block_of_ref[i] = where
            return carry

        lax.fori_loop(0, per_group * pc.groups, find, 0)

    arrived[:, per_group] = jnp.zeros((pc.groups, *arrived.shape[2:]), low)
    early = per_group // 2
    panel = pc.panel_of(pc.s)

    def exchange(m):
        ranks = pl.ds(early, per_group - early) if m == 0 else pl.ds(0, early)
        return [
            remote(
                by_slot.at[pc.section_peer(d), ranks],
                arrived.at[panel, ranks],
                a_send.at[m, d - 1],
                a_recv.at[m, d - 1],
                (pc.section_peer(d), pc.j),
            )
            for d in range(1, pc.groups)
        ]

    def send_ranks(m):
        for k in range(early, per_group) if m == 0 else range(early):
            for g in range(pc.groups):
                where = jnp.clip(block_of_ref[g * per_group + k], 0, blocks)
                by_slot[g, k] = final[where]
            arrived[panel, k] = by_slot[pc.s, k]
        begin(exchange(m))

    def step(b, body):
        pl.when(within(b, blocks))(lambda: body(b))

    def first(b):
        landed_all(to_core(b))
        at = lax.rem(b, core_slots)
        core_in[at] = (
            core_in[at].astype(float_out) + own_half[lax.rem(b, 2)].reshape(core_in.shape[1:])
        ).astype(low)
        by_kind(
            b,
            LONG_HOME,
            lambda: begin(first_x(b) + first_y(b)),
            lambda: begin(ring(b, 1)),
        )

    def then(b):
        at, n = lax.rem(b, core_slots), place_among(b)

        def near():
            landed_all(first_x(b))
            first_a[n, 0] = summed(core_in[at, lower, pc.x], first_a, n, pc.nx).astype(low)
            begin(then_y(b))
            landed_all(first_y(b))
            mine = pc.columns(pc.y, pc.panel)
            first_b[n, 0] = summed(
                core_in[at, upper, :, :, mine], first_b, n, pc.ny
            ).astype(low)
            begin(then_x(b))

        by_kind(b, LONG_HOME, near)

    def ring_on(k):
        def body(b):
            def far():
                landed_all(ring(b, k))
                n, held_for = lax.div(b, LONG_EVERY), pc.z_of((2 * pc.nz - 1 - k) % pc.nz)
                far_z[n, k - 1] = (
                    far_z[n, k - 1].astype(float_out)
                    + core_in[lax.rem(b, core_slots), held_for].astype(float_out)
                ).astype(low)
                begin(ring(b, k + 1) if k < hops else far_y(b))

            by_kind(b, LONG_HOME, far=far)

        return body

    def third(b):
        n = place_among(b)

        def near():
            landed_all(then_y(b))
            total = first_a[n, 0, :, :, pc.columns(pc.y, pc.panel)].astype(float_out)
            for d in range(pc.ny - 1):
                total = total + then_in[n, d, lower].astype(float_out)
            then_in[n, 0, lower] = total.astype(low)
            landed_all(then_x(b))
            total = first_b[n, 0, :, pc.x].astype(float_out)
            for d in range(pc.nx - 1):
                total = total + then_in[n, d, upper].astype(float_out)
            then_in[n, 0, upper] = total.astype(low)
            begin(along_z(b))

        by_kind(b, LONG_HOME, near)

    def far_third(b):
        def far():
            landed_all(far_y(b))
            n, mine = lax.div(b, LONG_EVERY), pc.columns(pc.y, pc.panel)
            far_yx[n, 0] = summed(far_z[n, hops - 1, :, :, mine], far_yx, n, pc.ny).astype(low)
            begin(far_x(b))

        by_kind(b, LONG_HOME, far=far)

    def let_go(b):
        by_kind(
            b,
            LONG_HOME,
            lambda: gone(first_x(b) + first_y(b)),
            lambda: gone(ring(b, 1)),
        )

        @pl.when(b < blocks - core_slots)
        def _():
            pl.semaphore_signal(free_sem, inc=1, device_id=pc.at_core(), device_id_type=MESH)

    def settle(b, total):
        rounded = total.astype(low)
        final[b] = rounded
        wide = rounded.astype(float_out)
        square[...] += jnp.sum(wide * wide, axis=0, keepdims=True)

    def close(b):
        n = place_among(b)

        def near():
            landed_all(along_z(b))
            settle(b, summed(then_in[n, 0, pc.z], z_in, n, pc.nz))

        by_kind(b, LONG_HOME, near)

    def far_close(b):
        def far():
            landed_all(far_x(b))
            n = lax.div(b, LONG_EVERY)
            settle(b, summed(far_yx[n, 0, pc.x], far_in, n, pc.nx))

        by_kind(b, LONG_HOME, far=far)

    def sent_off(b):
        def far():
            for k in range(2, pc.nz):
                gone(ring(b, k))
            gone(far_y(b) + far_x(b))

        by_kind(
            b,
            LONG_HOME,
            lambda: gone(then_y(b) + then_x(b) + along_z(b)),
            far,
        )

    early_at = 1 + max(
        b + (release + 4 if b % LONG_EVERY == LONG_HOME else 7) for b in range(blocks - early)
    )

    def weigh(t):
        slot = lax.rem(t, 2)
        send_half[lax.rem(t, 4)] = (
            turned_times(x_buf[slot], y_buf[slot, :, away])
            .astype(low)
            .reshape(send_half.shape[1:])
        )
        own_half[slot] = turned_times(x_buf[slot], y_buf[slot, :, keep])

    def make_ready(t):
        fetched(lax.rem(t, 2))

        @pl.when(t >= 4)
        def _():
            gone(to_core(t - 4))

    def leave(t):
        @pl.when(t >= core_slots)
        def _():
            pl.semaphore_wait(free_sem, 1)

        begin(to_core(t))

    def serve(t):
        step(t - 1, first)
        step(t - 3, then)
        for k in range(1, pc.nz):
            step(t - 2 * k - 1, ring_on(k))
        step(t - 5, third)
        step(t - release, let_go)
        step(t - release - 2, far_third)
        step(t - 7, close)
        step(t - release - 4, far_close)

    def attending(t, carry):
        fetch(t + 1)

        @pl.when(t + 1 < attend_steps)
        def _():
            begin(head_copies(t + 1))

        for copy in head_copies(t):
            copy.wait()
        make_ready(t)
        weigh(t)
        attend_back_step(t)
        leave(t)
        serve(t)
        return carry

    def later(t, carry):
        pl.when(t + 1 < blocks)(lambda: fetch(t + 1))
        i = lax.div(t - attend_steps, 2)
        odd = lax.rem(t - attend_steps, 2)

        @pl.when((t < attend_steps + 2 * embed_steps) & (odd == 0))
        def _():
            begin(chunk_copies(i))

        @pl.when(t < blocks)
        def _():
            make_ready(t)
            weigh(t)
            leave(t)

        serve(t)
        pl.when(t == blocks - 2)(rank_blocks)
        pl.when(t == early_at)(lambda: send_ranks(0))

        @pl.when((t < attend_steps + 2 * embed_steps) & (odd == 1))
        def _():
            @pl.when(t == attend_steps + 1)
            def _():
                weight_copy.wait()

            embed_back_step(i)

        table_at = attend_steps + 2 * embed_steps

        @pl.when(t == table_at)
        def _():
            for section in range(own_sections * pc.groups):
                total = jnp.zeros(row_sums.shape[1:], float_out)
                for r in range(rows):
                    total = total + jnp.where(ids_ref[0, r] == section, row_sums[r], 0.0)
                table_mine[section] = total
            begin(table_stage())

        pl.when(t == table_at + 4)(table_after_section)
        pl.when(t == table_at + 8)(table_after_x)
        for k in range(2):
            b = 2 * (t - table_at) + k
            pl.when((t >= table_at) & (b < sent_in_loop))(functools.partial(sent_off, b))

        return carry

    last_long = LONG_HOME + (LONGS - 1) * LONG_EVERY
    last_tick = attend_steps + 2 * embed_steps + 8
    ticks = max(
        last_tick + 1, blocks + 7, blocks + release, last_long + release + 5, early_at + 1
    )
    sent_in_loop = min(blocks - 7, 2 * (ticks - attend_steps - 2 * embed_steps))
    lax.fori_loop(0, attend_steps, attending, 0)
    lax.fori_loop(attend_steps, ticks, later, 0)

    send_ranks(1)

    table_after_z()
    total = table_out[...]
    table_square = jnp.sum(total * total) / pc.batch
    lane = lax.broadcasted_iota(jnp.int32, (8, 128), 1)
    part = jnp.where(lane == 0, jnp.sum(square[...]) + table_square, loss_ref[...])
    sums_ref[...] = part
    for start, end in pc.small_stages(sums_ref, sent, landed, m_send, m_recv):
        start()
        end()
    sums_out[...] = sums_ref[...]
    for copy in exchange(0) + exchange(1):
        copy.wait()
    for i in range(per_group):
        for q in range(pc.groups):
            rank = jnp.clip(rank_ref[i], 0, per_group)
            out_ref[i, :, q * pc.panel : (q + 1) * pc.panel] = arrived[q, rank]

    for b in range(blocks - 4, blocks):
        gone(to_core(b))

    def finish(b, carry):
        sent_off(b)
        return carry

    lax.fori_loop(sent_in_loop, blocks, finish, 0)


def back(pc, owners, ids, arrays, near, per_group):
    total = arrays[0].shape[0]
    rows, length = near[6].shape
    width = D // 2
    piece = width // pc.batch
    own_sections = SECTIONS // pc.groups
    hops = pc.nx - 1 + pc.ny - 1
    blocks = BLOCKS
    steps, small = pc.table_slots(), pc.small_slots()
    dma = pltpu.SemaphoreType.DMA
    vmem = pl.BlockSpec(memory_space=pltpu.VMEM)
    smem = pl.BlockSpec(memory_space=pltpu.SMEM)
    far = pl.BlockSpec(memory_space=pl.ANY)
    nz, nx, ny, half, panel = pc.nz, pc.nx, pc.ny, pc.half, pc.panel
    return pl.pallas_call(
        functools.partial(back_kernel, pc),
        out_shape=(
            like((per_group, piece, D)),
            like((own_sections, 8, D), float_out),
            like((8, 128), float_out),
        ),
        in_specs=[smem, smem] + [far] * len(arrays) + [far] * 5 + [vmem] * 5,
        out_specs=(vmem, vmem, vmem),
        scratch_shapes=[
            pltpu.VMEM((total, 1), jnp.int32),
            pltpu.SMEM((per_group * pc.groups,), jnp.int32),
            pltpu.SMEM((BLOCKS,), jnp.int32),
            pltpu.SMEM((per_group,), jnp.int32),
            pltpu.VMEM((pc.groups, per_group + 1, piece, panel), low),
            pltpu.VMEM((8, 128), float_out),
            pltpu.VMEM((2, total, width), low),
            pltpu.VMEM((2, total, D), low),
            pltpu.VMEM((2, width, half), float_out),
            pltpu.VMEM((4, nz, nx, piece, half), low),
            pltpu.VMEM((2 * nz + 4, nz, nx, piece, half), low),
            pltpu.VMEM((NEARS, nx - 1, nz // 2, piece, half), low),
            pltpu.VMEM((NEARS, ny - 1, nz - nz // 2, nx, piece, panel), low),
            pltpu.VMEM((NEARS, max(nx, ny) - 1, nz, piece, panel), low),
            pltpu.VMEM((NEARS, nz - 1, piece, panel), low),
            pltpu.VMEM((LONGS, nz - 1, nx, piece, half), low),
            pltpu.VMEM((LONGS, ny - 1, nx, piece, panel), low),
            pltpu.VMEM((LONGS, nx - 1, piece, panel), low),
            pltpu.VMEM((blocks + 1, piece, panel), low),
            pltpu.VMEM((pc.groups, per_group, piece, panel), low),
            pltpu.VMEM((1, panel), float_out),
            pltpu.VMEM((2, 4, length, 2 * HD), low),
            pltpu.VMEM((3, total, D), low),
            pltpu.VMEM((total, D), low),
            pltpu.VMEM((6, nz, nx, piece, D), low),
            pltpu.VMEM((2, 2, ROWS_AT_ONCE, D), float_out),
            pltpu.VMEM((rows, 8, D), float_out),
            pltpu.VMEM((own_sections * pc.groups, 8, D), float_out),
            pltpu.VMEM((steps, own_sections, 8, D), float_out),
            pltpu.VMEM((2, own_sections, 8, D), float_out),
            pltpu.VMEM((2, 8, 128), float_out),
            pltpu.VMEM((small, 8, 128), float_out),
            dma((2, 2)),
            dma((2, 4)),
            dma((2, 2)),
            dma,
            pltpu.SemaphoreType.REGULAR,
            dma((blocks,)),
            dma((blocks,)),
            dma((blocks, hops)),
            dma((blocks, hops)),
            dma((blocks, hops)),
            dma((blocks, hops)),
            dma((blocks, nz - 1)),
            dma((blocks, nz - 1)),
            dma((2, pc.groups - 1)),
            dma((2, pc.groups - 1)),
            dma((steps,)),
            dma((steps,)),
            dma((small,)),
            dma((small,)),
        ],
        name="back",
        compiler_params=pltpu.CompilerParams(
            collective_id=1, has_side_effects=True, vmem_limit_bytes=62 * MIB
        ),
    )(owners, ids, *arrays, *near)


def matrix(ref, first, count=2):
    return ref[first : first + count].reshape(count * ref.shape[1], ref.shape[2])


def row_block(width, count=ROWS_AT_ONCE):
    return pl.BlockSpec((count, width), lambda i: (i, 0))


def plane_block(planes, width=D, count=ROWS_AT_ONCE):
    return pl.BlockSpec((planes, count, width), lambda i: (0, i, 0))


def per_row(steps, height=8):
    return pl.BlockSpec((1, height, D), lambda i: (i // steps, 0, 0))


def compiler(mib):
    return pltpu.CompilerParams(vmem_limit_bytes=mib * MIB)


def cost(flops, reach, deep=0):
    return pl.CostEstimate(flops=flops, bytes_accessed=reach, transcendentals=deep)


def middle_kernel(
    steps,
    slope_ref,
    x1_ref,
    x2_ref,
    params_ref,
    targets_ref,
    w_ref,
    h3_ref,
    dlogits_ref,
    dffn_ref,
    du_ref,
    dattn_ref,
    do_ref,
    dx_ref,
    rows_ref,
    loss_ref,
    out_w,
    up_w,
    down_w,
    head_w,
    sems,
):
    step = pl.program_id(0)
    loads = [
        pltpu.make_async_copy(w_ref.at[pl.ds(first, dst.shape[0])], dst, sems.at[n])
        for n, (first, dst) in enumerate(
            ((HEAD, head_w), (DOWN, down_w), (UP, up_w), (OUT, out_w))
        )
    ]

    def ready(n):
        pl.when(step == 0)(loads[n].wait)

    pl.when(step == 0)(lambda: begin(loads))
    par = [params_ref[0, k : k + 1] for k in range(7)]
    n3, scale3 = normalize(x2_ref[...])
    h3 = (n3 * (1.0 + par[4]) + par[5]).astype(low)
    h3_ref[...] = h3
    ready(0)
    logits = times(h3, matrix(head_w, 0))
    top = jnp.max(logits, axis=-1, keepdims=True)
    lse = top + jnp.log(jnp.sum(jnp.exp(logits - top), axis=-1, keepdims=True))
    vocab = lax.broadcasted_iota(jnp.int32, logits.shape, 1)
    wanted = targets_ref[
        pl.ds(step // steps, 1),
        pl.ds(pl.multiple_of(step % steps * ROWS_AT_ONCE, ROWS_AT_ONCE), ROWS_AT_ONCE),
    ]
    picked = column_of(wanted) == vocab
    losses = lse - jnp.sum(jnp.where(picked, logits, 0.0), axis=-1, keepdims=True)
    weight = par[6]
    dlogits = ((jnp.exp(logits - lse) - jnp.where(picked, 1.0, 0.0)) * weight).astype(low)
    dlogits_ref[...] = dlogits
    dh3 = times_t(dlogits, matrix(head_w, 0))
    dx2, gain3, shift3 = norm_back(dh3, n3, scale3, par[4])
    dffn = dx2.astype(low)
    dffn_ref[...] = dffn
    dh2 = 0.0
    ready(1)
    ready(2)
    for g in range(4):
        du = (times_t(dffn, matrix(down_w, 2 * g)) * slope_ref[g].astype(float_out)).astype(low)
        du_ref[g] = du
        dh2 = dh2 + times_t(du, matrix(up_w, 2 * g))
    n2, scale2 = normalize(x1_ref[...])
    dx1, gain2, shift2 = norm_back(dh2, n2, scale2, par[2])
    dx1 = dx1 + dx2
    dx_ref[...] = dx1
    dattn = dx1.astype(low)
    dattn_ref[...] = dattn
    ready(3)
    do_ref[...] = times_t(dattn, matrix(out_w, 0)).astype(low)
    grads = jnp.concatenate([gain2, shift2, gain3, shift3], axis=0)

    @pl.when(step == 0)
    def _():
        loss_ref[...] = jnp.zeros_like(loss_ref)

    @pl.when(step % steps == 0)
    def _():
        rows_ref[...] = jnp.zeros_like(rows_ref)

    rows_ref[0, 2:6] += grads
    loss_ref[...] += jnp.sum(losses) * weight[:, :128]


def middle(w, slope, x1, x2, params, targets, length):
    total = x1.shape[0]
    steps = length // ROWS_AT_ONCE
    rows = total // length
    return pl.pallas_call(
        functools.partial(middle_kernel, steps),
        grid=(total // ROWS_AT_ONCE,),
        out_shape=(
            like((total, D)),
            like((total, CODES)),
            like((total, D)),
            like((4, total, D)),
            like((total, D)),
            like((total, D)),
            like((total, D), float_out),
            like((rows, 8, D), float_out),
            like((8, 128), float_out),
        ),
        in_specs=[
            plane_block(4),
            row_block(D),
            row_block(D),
            per_row(steps),
            pl.BlockSpec(targets.shape, lambda i: (0, 0)),
            pl.BlockSpec(memory_space=pl.ANY),
        ],
        out_specs=(
            row_block(D),
            row_block(CODES),
            row_block(D),
            plane_block(4),
            row_block(D),
            row_block(D),
            row_block(D),
            per_row(steps),
            pl.BlockSpec((8, 128), lambda i: (0, 0)),
        ),
        scratch_shapes=[
            *(pltpu.VMEM((count, D // 2, D), low) for count in (2, 8, 8, 2)),
            pltpu.SemaphoreType.DMA((4,)),
        ],
        name="middle",
        compiler_params=compiler(62),
        cost_estimate=cost(22 * total * D * D, 60 * MIB, 2 * total * D),
    )(slope, x1, x2, params, targets, w)


def adam(weight, first, second, grad, rate, fixes):
    new_first = beta_one * first + (1.0 - beta_one) * grad
    new_second = beta_two * second + (1.0 - beta_two) * grad * grad
    update = new_first * fixes[0] / (jnp.sqrt(new_second * fixes[1]) + adam_eps)
    return (weight - rate * (update + decay_rate * weight), new_first, new_second)


def update_kernel(
    step_ref,
    sums_ref,
    table_grad_ref,
    table_ref,
    table_first_ref,
    table_second_ref,
    grad_ref,
    masters_ref,
    first_ref,
    second_ref,
    new_masters,
    new_first,
    new_second,
    new_table,
    new_table_first,
    new_table_second,
    norm_ref,
    loss_ref,
    grad,
    state,
    made,
    in_sem,
    out_sem,
):
    slots = masters_ref.shape[0]

    def loads(i):
        copies = [pltpu.make_async_copy(grad_ref.at[i], grad.at[i], in_sem.at[i, 3])]
        for n, ref in enumerate((masters_ref, first_ref, second_ref)):
            copies.append(pltpu.make_async_copy(ref.at[i], state.at[n, i], in_sem.at[i, n]))
        return copies

    def stores(i):
        return [
            pltpu.make_async_copy(made.at[n, i], ref.at[i], out_sem.at[i, n])
            for n, ref in enumerate((new_masters, new_first, new_second))
        ]

    for i in range(slots):
        begin(loads(i))
    step = jnp.full((1, 128), step_ref[0]).astype(float_out)
    fixes = [
        1.0 / (1.0 - jnp.exp(step * math.log(beta)))[:, :1] for beta in (beta_one, beta_two)
    ]
    norm = jnp.sqrt(sums_ref[0:1, 0:1])
    clip = jnp.minimum(1.0, clip_limit / norm)
    norm_ref[...] = norm
    loss_ref[...] = sums_ref[0:1, 1:2]
    for n in range(table_ref.shape[0]):
        for k in range(6):
            at = (slice(n, n + 1), slice(k * D, (k + 1) * D))
            new_table[at], new_table_first[at], new_table_second[at] = adam(
                table_ref[at],
                table_first_ref[at],
                table_second_ref[at],
                table_grad_ref[n, k : k + 1] * clip,
                table_rate,
                fixes,
            )

    def one(i, carry):
        for copy in loads(i):
            copy.wait()
        results = adam(
            state[0, i],
            state[1, i],
            state[2, i],
            grad[i].astype(float_out) * clip,
            learn_rate,
            fixes,
        )
        for n, value in enumerate(results):
            made[n, i] = value
        begin(stores(i))
        return carry

    lax.fori_loop(0, slots, one, 0)
    for i in range(slots):
        for copy in stores(i):
            copy.wait()


def update(step, sums, grad, masters, first, second, table_grad, table, table_first, table_second):
    slots = masters.shape[0]
    vmem = pl.BlockSpec(memory_space=pltpu.VMEM)
    far = pl.BlockSpec(memory_space=pl.ANY)
    dma = pltpu.SemaphoreType.DMA
    return pl.pallas_call(
        update_kernel,
        out_shape=(
            *(like(masters.shape, float_out) for _ in range(3)),
            *(like(table.shape, float_out) for _ in range(3)),
            like((1, 1), float_out),
            like((1, 1), float_out),
        ),
        in_specs=[pl.BlockSpec(memory_space=pltpu.SMEM)] + [vmem] * 5 + [far] * 4,
        out_specs=(far, far, far, vmem, vmem, vmem, vmem, vmem),
        scratch_shapes=[
            pltpu.VMEM(grad.shape, low),
            pltpu.VMEM((3, *masters.shape), float_out),
            pltpu.VMEM((3, *masters.shape), float_out),
            dma((slots, 4)),
            dma((slots, 3)),
        ],
        name="update",
        compiler_params=compiler(62),
        cost_estimate=cost(20 * masters.size, 28 * masters.size),
    )(step, sums, table_grad, table, table_first, table_second, grad, masters, first, second)


def per_device(
    pc,
    masters,
    first_moment,
    second_moment,
    section_table,
    table_first,
    table_second,
    owners,
    step_count,
    phones,
    codes,
    segments,
    sections,
    targets,
):
    row_count, length = segments.shape
    ids = sections.reshape(1, row_count)
    blocks, params, multi, phone_hot, x0, h1, qkv, mixed, lse, x1, h2, act, slope, x2 = front(
        pc, owners, ids, masters, section_table, codes.swapaxes(1, 2), phones, segments
    )
    w = blocks.reshape(BLOCKS, D // 2, D)
    qkv = qkv.reshape(3, row_count * length, D)
    mixed = mixed.reshape(row_count * length, D)
    h3, dlogits, dffn, du, dattn, do, dx1, row_sums, loss_part = middle(
        w, slope, x1, x2, params, targets, length
    )
    own_grad, table_grad, sums = back(
        pc,
        owners,
        ids,
        (h3, act, h2, mixed, h1, multi, phone_hot, dlogits, dffn, du, dattn),
        (qkv, do, x0, dx1, blocks, lse, segments, params, row_sums, loss_part),
        masters.shape[0],
    )
    *state, grad_norm, loss = update(
        step_count,
        sums,
        own_grad,
        masters,
        first_moment,
        second_moment,
        table_grad,
        section_table,
        table_first,
        table_second,
    )
    return (*state, grad_norm.reshape(()), loss.reshape(()))


def solution(mesh):
    return jax.shard_map(
        functools.partial(per_device, Place(mesh)),
        mesh=mesh,
        in_specs=(
            P("section", "batch", None),
            P("section", "batch", None),
            P("section", "batch", None),
            P("section", None),
            P("section", None),
            P("section", None),
            P(),
            P(),
            P(("section", "batch"), None),
            P(("section", "batch"), None, None),
            P(("section", "batch"), None),
            P(("section", "batch"), None),
            P(("section", "batch"), None),
        ),
        out_specs=(
            P("section", "batch", None),
            P("section", "batch", None),
            P("section", "batch", None),
            P("section", None),
            P("section", None),
            P("section", None),
            P(),
            P(),
        ),
        check_vma=False,
    )
```

time: 2450 us -> 367 us (0.15)
  waiting for transfers between devices: 1680 us -> 0 us
  Pallas kernels: 0 us -> 365 us
  matrix products: 327 us -> 0 us
  local copies, waits for them, and re-layouts: 240 us -> 0 us
  other arithmetic: 94.7 us -> 0 us
  blocking collectives: 85.5 us -> 0 us
    reduce_scatter x1 -> x0, waiting for transfers between devices: 1400 us -> none  [per_device(): lax.psum_scatter(arranged, ('section', 'batch'), scatter_dimension=0, til...]
    pallas_call x0 -> x4, Pallas kernels: none -> 365 us  [the longest x1 162 us: back(): pl.pallas_call(functools.partial(back_kernel, pc), out_shape=(like((per_g...]
    dot_general x27 -> x0, matrix products: 327 us -> none  [the longest x1 49.3 us: forward(): jnp.einsum('rld,gde->rlge', input_two, up_w, preferred_element_type=float...]
    all_gather x2 -> x0, waiting for transfers between devices: 280 us -> none  [the longest x1 152 us: per_device(): all_slots = lax.all_gather(shard_rows, 'section', axis=0, tiled=True)]
    scatter x1 -> x0, local copies, waits for them, and re-layouts: 107 us -> none  [per_device(): arranged.at[target_slot.reshape(-1)]]
    psum x2 -> x0, blocking collectives: 78.1 us -> none  [the longest x1 39.4 us: per_device(): grad_norm = jnp.sqrt(lax.psum(square_sum, ('section', 'batch')))]
    unnamed x247 -> x0, local copies, waits for them, and re-layouts: 37.5 us -> none
    convert_element_type x5 -> x0, other arithmetic: 37 us -> none  [the longest x1 28.6 us: backward(): grad_scores = (probs * (grad_probs - jnp.sum(probs * grad_probs, axis=-1,...]
  transfers between devices with their start and end apart: 4 -> 0, of which waited for: 3 -> 0; matrix products, arithmetic and copies ran while one was open for 8% -> 0% of each run, Pallas kernels for 0% -> 0%
where the time goes in v2:
time: 367 us
  Pallas kernels  365 us (99%)
    pallas_call x1, Pallas kernels, back(): pl.pallas_call(functools.partial(back_kernel, pc), out_shape=(like((per_g...  162 us
    pallas_call x1, Pallas kernels, front(): pl.pallas_call(functools.partial(front_kernel, pc), out_shape=(like((BLOC...  152 us
    pallas_call x1, Pallas kernels, middle(): pl.pallas_call(functools.partial(middle_kernel, steps), grid=(total // RO...  43.1 us
    pallas_call x1, Pallas kernels, update(): pl.pallas_call(update_kernel, out_shape=(*(like(masters.shape, float_out)...  7.98 us

profile of v2, /device:TPU:0, one launch (start us, length us, event | category | flops | bytes accessed | tf_op | source)
XLA Modules:
  0.0 366.6 jit_solution(5737218536103390672)
XLA Ops:
  0.6 152.3 %front.1 = (bf16[29,4,2,64,1024]{4,3,2,1,0:T(8,128)(2,1)}, f32[2,8,1024]{2,1,0:T(8,128)}, bf16[1024,1024]{1,0:T(8,128)(2,1)}, bf16[1024,512]{1,0:T(8,128)(2,1)},...) custom-call(s32[29]{0:T(128)} %refs_0_.1, ...), custom_call_target="tpu_custom_call" | custom-call | tf_op jit(solution)/shard_map/front/pallas_call | solution.py:1005
  152.9 43.1 %middle.1 = (bf16[1024,1024]{1,0:T(8,128)(2,1)}, bf16[1024,1024]{1,0:T(8,128)(2,1)}, bf16[1024,1024]{1,0:T(8,128)(2,1)}, bf16[4,1024,1024]{2,1,0:T(8,128)(2,1)},...) custom-call(bf16[4,1024,1024]{2,1,0:T(8,128)(2,1)} %get-tuple-elemen, ...), custom_call_target="tpu_custom_call" | custom-call | flops 23622320128 | bytes 62914560 | tf_op jit(solution)/shard_map/middle/pallas_call | solution.py:1932
  196.0 161.6 %back.1 = (bf16[8,64,1024]{2,1,0:T(8,128)(2,1)}, f32[2,8,1024]{2,1,0:T(8,128)}, f32[8,128]{1,0:T(8,128)}) custom-call(s32[29]{0:T(128)} %refs_0_.1, s32[1,2]{1,0:T(1,128)} %bitcast.14, bf16[1024,1024]{1,0:T(8,128)(2,1)} %get-tuple-element.47.refs_2_, bf16[4,1024,1024]{2,1,0:T(8,128)(2,1)} %get-tuple-element.48.refs_3_, ...), custom_call_target="tpu_custom_call" | custom-call | tf_op jit(solution)/shard_map/back/pallas_call | solution.py:1749
  358.3 8.0 %update.1 = (f32[8,64,1024]{2,1,0:T(8,128)}, f32[8,64,1024]{2,1,0:T(8,128)}, f32[8,64,1024]{2,1,0:T(8,128)}, f32[2,6144]{1,0:T(2,128)}, f32[2,6144]{1,0:T(2,128)...) custom-call(s32[1]{0:T(128)S(6)} %copy.24.step_ref, f32[8,128]{1,0:T(8,128)} %get-tuple-element.65.sums_ref, ...), custom_call_target="tpu_custom_call" | custom-call | flops 10485760 | bytes 14680064 | tf_op jit(solution)/shard_map/update/pallas_call | solution.py:2070

commit v3 on v2

--- a/solution.py
+++ b/solution.py
@@ -777,10 +777,12 @@
     out_ticks = embed_steps // 2
     up_fetch = max(max(lands[UP:DOWN]) + 1, attend_from)
     up_from = max(out_from + out_ticks, up_fetch + 1)
-    late = max(1, out_from + out_ticks - min(lands[DOWN:HEAD]))
+    free_at = out_from + out_ticks
+    direct = max([p + 1 for p in range(DOWN, HEAD) if lands[p] < free_at], default=DOWN)
+    copied = {p: max(lands[p], free_at if p < direct else 0) for p in range(DOWN, HEAD)}
     down_at = []
     for g in range(4):
-        landed_by = max(lands[DOWN + 2 * g : DOWN + 2 * g + 2]) + late + 1
+        landed_by = max(copied[DOWN + 2 * g], copied[DOWN + 2 * g + 1]) + 1
         after = down_at[-1] + 1 if down_at else up_from + embed_steps
         down_at.append(max(landed_by, after))
 
@@ -844,17 +846,16 @@
 
         by_kind(p, LONG_OUT, far=far)
 
-    def held(p):
-        @pl.when((p >= DOWN) & (p < HEAD))
-        def _():
-            down_weight(p).start()
-
     def arrived(p):
         landed_all(to_core(p))
 
         @pl.when(p < FRONT)
         def _():
             into_vmem(p).start()
+
+        @pl.when((p >= direct) & (p < HEAD))
+        def _():
+            down_weight(p).start()
 
     sent_after = 2 * hops + 4
 
@@ -885,8 +886,8 @@
         step(t - 2 * hops, core_far)
         step(t - 6, lambda p: by_kind(p, LONG_OUT, lambda: arrived(p)))
         step(t - 2 * hops - 1, lambda p: by_kind(p, LONG_OUT, far=lambda: arrived(p)))
-        step(t - 6 - late, lambda p: by_kind(p, LONG_OUT, lambda: held(p)))
-        step(t - 2 * hops - 1 - late, lambda p: by_kind(p, LONG_OUT, far=lambda: held(p)))
+        for p in range(DOWN, direct):
+            pl.when(t == copied[p])(down_weight(p).start)
 
         for stage, (start, end) in enumerate(small):
             pl.when(turn == ahead + 1 + 2 * stage)(start)
@@ -1863,15 +1864,20 @@
     sems,
 ):
     step = pl.program_id(0)
+    parts = [(HEAD, head_w, 0)]
+    for g in range(4):
+        parts += [(DOWN + 2 * g, down_w, 2 * g), (UP + 2 * g, up_w, 2 * g)]
+    parts.append((OUT, out_w, 0))
     loads = [
-        pltpu.make_async_copy(w_ref.at[pl.ds(first, dst.shape[0])], dst, sems.at[n])
-        for n, (first, dst) in enumerate(
-            ((HEAD, head_w), (DOWN, down_w), (UP, up_w), (OUT, out_w))
-        )
+        pltpu.make_async_copy(w_ref.at[pl.ds(first, 2)], dst.at[pl.ds(at, 2)], sems.at[n])
+        for n, (first, dst, at) in enumerate(parts)
     ]
 
-    def ready(n):
-        pl.when(step == 0)(loads[n].wait)
+    def ready(*numbers):
+        @pl.when(step == 0)
+        def _():
+            for n in numbers:
+                loads[n].wait()
 
     pl.when(step == 0)(lambda: begin(loads))
     par = [params_ref[0, k : k + 1] for k in range(7)]
@@ -1897,9 +1903,8 @@
     dffn = dx2.astype(low)
     dffn_ref[...] = dffn
     dh2 = 0.0
-    ready(1)
-    ready(2)
     for g in range(4):
+        ready(1 + 2 * g, 2 + 2 * g)
         du = (times_t(dffn, matrix(down_w, 2 * g)) * slope_ref[g].astype(float_out)).astype(low)
         du_ref[g] = du
         dh2 = dh2 + times_t(du, matrix(up_w, 2 * g))
@@ -1909,7 +1914,7 @@
     dx_ref[...] = dx1
     dattn = dx1.astype(low)
     dattn_ref[...] = dattn
-    ready(3)
+    ready(9)
     do_ref[...] = times_t(dattn, matrix(out_w, 0)).astype(low)
     grads = jnp.concatenate([gain2, shift2, gain3, shift3], axis=0)
 
@@ -1964,7 +1969,7 @@
         ),
         scratch_shapes=[
             *(pltpu.VMEM((count, D // 2, D), low) for count in (2, 8, 8, 2)),
-            pltpu.SemaphoreType.DMA((4,)),
+            pltpu.SemaphoreType.DMA((10,)),
         ],
         name="middle",
         compiler_params=compiler(62),
@@ -1977,6 +1982,9 @@
     new_second = beta_two * second + (1.0 - beta_two) * grad * grad
     update = new_first * fixes[0] / (jnp.sqrt(new_second * fixes[1]) + adam_eps)
     return (weight - rate * (update + decay_rate * weight), new_first, new_second)
+
+
+SLOTS_AT_ONCE = 2
 
 
 def update_kernel(
@@ -2004,21 +2012,26 @@
     in_sem,
     out_sem,
 ):
-    slots = masters_ref.shape[0]
+    turns = masters_ref.shape[0] // SLOTS_AT_ONCE
+
+    def part(i):
+        return pl.ds(i * SLOTS_AT_ONCE, SLOTS_AT_ONCE)
 
     def loads(i):
-        copies = [pltpu.make_async_copy(grad_ref.at[i], grad.at[i], in_sem.at[i, 3])]
+        copies = [pltpu.make_async_copy(grad_ref.at[part(i)], grad.at[part(i)], in_sem.at[i, 3])]
         for n, ref in enumerate((masters_ref, first_ref, second_ref)):
-            copies.append(pltpu.make_async_copy(ref.at[i], state.at[n, i], in_sem.at[i, n]))
+            copies.append(
+                pltpu.make_async_copy(ref.at[part(i)], state.at[n, part(i)], in_sem.at[i, n])
+            )
         return copies
 
     def stores(i):
         return [
-            pltpu.make_async_copy(made.at[n, i], ref.at[i], out_sem.at[i, n])
+            pltpu.make_async_copy(made.at[n, part(i)], ref.at[part(i)], out_sem.at[i, n])
             for n, ref in enumerate((new_masters, new_first, new_second))
         ]
 
-    for i in range(slots):
+    for i in range(turns):
         begin(loads(i))
     step = jnp.full((1, 128), step_ref[0]).astype(float_out)
     fixes = [
@@ -2044,26 +2057,26 @@
         for copy in loads(i):
             copy.wait()
         results = adam(
-            state[0, i],
-            state[1, i],
-            state[2, i],
-            grad[i].astype(float_out) * clip,
+            state[0, part(i)],
+            state[1, part(i)],
+            state[2, part(i)],
+            grad[part(i)].astype(float_out) * clip,
             learn_rate,
             fixes,
         )
         for n, value in enumerate(results):
-            made[n, i] = value
+            made[n, part(i)] = value
         begin(stores(i))
         return carry
 
-    lax.fori_loop(0, slots, one, 0)
-    for i in range(slots):
+    lax.fori_loop(0, turns, one, 0)
+    for i in range(turns):
         for copy in stores(i):
             copy.wait()
 
 
 def update(step, sums, grad, masters, first, second, table_grad, table, table_first, table_second):
-    slots = masters.shape[0]
+    turns = masters.shape[0] // SLOTS_AT_ONCE
     vmem = pl.BlockSpec(memory_space=pltpu.VMEM)
     far = pl.BlockSpec(memory_space=pl.ANY)
     dma = pltpu.SemaphoreType.DMA
@@ -2081,8 +2094,8 @@
             pltpu.VMEM(grad.shape, low),
             pltpu.VMEM((3, *masters.shape), float_out),
             pltpu.VMEM((3, *masters.shape), float_out),
-            dma((slots, 4)),
-            dma((slots, 3)),
+            dma((turns, 4)),
+            dma((turns, 3)),
         ],
         name="update",
         compiler_params=compiler(62),

time: 367 us -> 364 us (level)
  no operation moved by 1% of the time
where the time goes in v3:
time: 364 us
  Pallas kernels  362 us (99%)
    pallas_call x1, Pallas kernels, back(): pl.pallas_call(functools.partial(back_kernel, pc), out_shape=(like((per_g...  162 us
    pallas_call x1, Pallas kernels, front(): pl.pallas_call(functools.partial(front_kernel, pc), out_shape=(like((BLOC...  150 us
    pallas_call x1, Pallas kernels, middle(): pl.pallas_call(functools.partial(middle_kernel, steps), grid=(total // RO...  42.7 us
    pallas_call x1, Pallas kernels, update(): pl.pallas_call(update_kernel, out_shape=(*(like(masters.shape, float_out)...  7.35 us

profile of v3, /device:TPU:0, one launch (start us, length us, event | category | flops | bytes accessed | tf_op | source)
XLA Modules:
  0.0 363.6 jit_solution(14988290954095661655)
XLA Ops:
  0.6 150.4 %front.1 = (bf16[29,4,2,64,1024]{4,3,2,1,0:T(8,128)(2,1)}, f32[2,8,1024]{2,1,0:T(8,128)}, bf16[1024,1024]{1,0:T(8,128)(2,1)}, bf16[1024,512]{1,0:T(8,128)(2,1)},...) custom-call(s32[29]{0:T(128)} %refs_0_.1, ...), custom_call_target="tpu_custom_call" | custom-call | tf_op jit(solution)/shard_map/front/pallas_call | solution.py:1006
  151.0 42.7 %middle.1 = (bf16[1024,1024]{1,0:T(8,128)(2,1)}, bf16[1024,1024]{1,0:T(8,128)(2,1)}, bf16[1024,1024]{1,0:T(8,128)(2,1)}, bf16[4,1024,1024]{2,1,0:T(8,128)(2,1)},...) custom-call(bf16[4,1024,1024]{2,1,0:T(8,128)(2,1)} %get-tuple-elemen, ...), custom_call_target="tpu_custom_call" | custom-call | flops 23622320128 | bytes 62914560 | tf_op jit(solution)/shard_map/middle/pallas_call | solution.py:1937
  193.8 161.5 %back.1 = (bf16[8,64,1024]{2,1,0:T(8,128)(2,1)}, f32[2,8,1024]{2,1,0:T(8,128)}, f32[8,128]{1,0:T(8,128)}) custom-call(s32[29]{0:T(128)} %refs_0_.1, s32[1,2]{1,0:T(1,128)} %bitcast.14, bf16[1024,1024]{1,0:T(8,128)(2,1)} %get-tuple-element.47.refs_2_, bf16[4,1024,1024]{2,1,0:T(8,128)(2,1)} %get-tuple-element.48.refs_3_, ...), custom_call_target="tpu_custom_call" | custom-call | tf_op jit(solution)/shard_map/back/pallas_call | solution.py:1750
  355.9 7.4 %update.1 = (f32[8,64,1024]{2,1,0:T(8,128)}, f32[8,64,1024]{2,1,0:T(8,128)}, f32[8,64,1024]{2,1,0:T(8,128)}, f32[2,6144]{1,0:T(2,128)}, f32[2,6144]{1,0:T(2,128)...) custom-call(s32[1]{0:T(128)S(6)} %copy.24.step_ref, f32[8,128]{1,0:T(8,128)} %get-tuple-element.65.sums_ref, ...), custom_call_target="tpu_custom_call" | custom-call | flops 10485760 | bytes 14680064 | tf_op jit(solution)/shard_map/update/pallas_call | solution.py:2083

commit v4 on v3

--- a/solution.py
+++ b/solution.py
@@ -1449,7 +1449,7 @@
         lax.fori_loop(0, per_group * pc.groups, find, 0)
 
     arrived[:, per_group] = jnp.zeros((pc.groups, *arrived.shape[2:]), low)
-    early = per_group // 2
+    early = per_group // 4
     panel = pc.panel_of(pc.s)
 
     def exchange(m):

time: 364 us -> 362 us (level)
  no operation moved by 1% of the time
where the time goes in v4:
time: 362 us
  Pallas kernels  360 us (99%)
    pallas_call x1, Pallas kernels, back(): pl.pallas_call(functools.partial(back_kernel, pc), out_shape=(like((per_g...  160 us
    pallas_call x1, Pallas kernels, front(): pl.pallas_call(functools.partial(front_kernel, pc), out_shape=(like((BLOC...  150 us
    pallas_call x1, Pallas kernels, middle(): pl.pallas_call(functools.partial(middle_kernel, steps), grid=(total // RO...  42.7 us
    pallas_call x1, Pallas kernels, update(): pl.pallas_call(update_kernel, out_shape=(*(like(masters.shape, float_out)...  7.35 us

profile of v4, /device:TPU:0, one launch (start us, length us, event | category | flops | bytes accessed | tf_op | source)
XLA Modules:
  0.0 362.1 jit_solution(3196185775587596617)
XLA Ops:
  0.6 150.4 %front.1 = (bf16[29,4,2,64,1024]{4,3,2,1,0:T(8,128)(2,1)}, f32[2,8,1024]{2,1,0:T(8,128)}, bf16[1024,1024]{1,0:T(8,128)(2,1)}, bf16[1024,512]{1,0:T(8,128)(2,1)},...) custom-call(s32[29]{0:T(128)} %refs_0_.1, ...), custom_call_target="tpu_custom_call" | custom-call | tf_op jit(solution)/shard_map/front/pallas_call | solution.py:1006
  151.0 42.7 %middle.1 = (bf16[1024,1024]{1,0:T(8,128)(2,1)}, bf16[1024,1024]{1,0:T(8,128)(2,1)}, bf16[1024,1024]{1,0:T(8,128)(2,1)}, bf16[4,1024,1024]{2,1,0:T(8,128)(2,1)},...) custom-call(bf16[4,1024,1024]{2,1,0:T(8,128)(2,1)} %get-tuple-elemen, ...), custom_call_target="tpu_custom_call" | custom-call | flops 23622320128 | bytes 62914560 | tf_op jit(solution)/shard_map/middle/pallas_call | solution.py:1937
  193.8 160.0 %back.1 = (bf16[8,64,1024]{2,1,0:T(8,128)(2,1)}, f32[2,8,1024]{2,1,0:T(8,128)}, f32[8,128]{1,0:T(8,128)}) custom-call(s32[29]{0:T(128)} %refs_0_.1, s32[1,2]{1,0:T(1,128)} %bitcast.14, bf16[1024,1024]{1,0:T(8,128)(2,1)} %get-tuple-element.47.refs_2_, bf16[4,1024,1024]{2,1,0:T(8,128)(2,1)} %get-tuple-element.48.refs_3_, ...), custom_call_target="tpu_custom_call" | custom-call | tf_op jit(solution)/shard_map/back/pallas_call | solution.py:1750
  354.4 7.4 %update.1 = (f32[8,64,1024]{2,1,0:T(8,128)}, f32[8,64,1024]{2,1,0:T(8,128)}, f32[8,64,1024]{2,1,0:T(8,128)}, f32[2,6144]{1,0:T(2,128)}, f32[2,6144]{1,0:T(2,128)...) custom-call(s32[1]{0:T(128)S(6)} %copy.24.step_ref, f32[8,128]{1,0:T(8,128)} %get-tuple-element.65.sums_ref, ...), custom_call_target="tpu_custom_call" | custom-call | flops 10485760 | bytes 14680064 | tf_op jit(solution)/shard_map/update/pallas_call | solution.py:2083
